TPU v7x, 128 devices: a whole 4x4x4 slice. The times are simulated.
128 devices in a mesh: blk: 32 (over z, y, core), pen: 4 (over x).
Axes of the slice: x: 4, y: 4, z: 4, core: 2. Of those that a mesh axis runs over, the one named last changes fastest.
Arguments:
- snapshots: bfloat16 [4, 512, 2048, 128], P(None, ('blk', 'pen')), may hold values from -110 to 110
- start_time: float32 [128, 64], replicated, may hold values from -6 to 6
- start_plane: float32 [512, 32], replicated, may hold values from -6 to 6
Outputs:
- time_basis: float32 [128, 64], replicated
- plane_basis: float32 [512, 32], replicated
- core_tensor: bfloat16 [4, 32, 131072], P(None, None, ('blk', 'pen'))
All inputs are finite; a program needn't handle non-finite values.
Results may differ from a plain program's by a relative error of at most 0.005.
Values may be sent and summed in bfloat16 or wider, within the bound.
No kernel may reach another device: no remote copies, remote signals or barrier semaphores. Data moves between devices by JAX's collectives and lax.ppermute only.
A program may use at most 64 MiB of HBM per device.

v0:
```python
import jax
import jax.numpy as jnp
from jax import lax
from jax.sharding import PartitionSpec as P

ITT = 3
ITX = 3


HIGHEST = lax.Precision.HIGHEST


def orthonormal(matrix):
    for repeat in range(2):
        square_gram = jnp.dot(matrix.T, matrix, precision=HIGHEST)
        lower_factor = jnp.linalg.cholesky(square_gram)
        matrix = jax.scipy.linalg.solve_triangular(lower_factor, matrix.T, lower=True).T
    return matrix


def subspace(operator_gram, initial, sweeps):
    current = initial
    for repeat in range(sweeps):
        current = orthonormal(jnp.dot(operator_gram, current, precision=HIGHEST))
    return current


def on_device(snapshots, start_time, start_plane):
    variables, planes, cell_count, window = snapshots.shape
    devices_all = lax.axis_size("blk") * lax.axis_size("pen")
    row_matrix = snapshots.reshape(variables * planes * cell_count, window)
    partial_time = jnp.dot(row_matrix.T, row_matrix, preferred_element_type=jnp.float32)
    gram_time = lax.psum(partial_time, ("blk", "pen")) / float(
        variables * planes * cell_count * devices_all
    )
    time_basis = subspace(gram_time, start_time, ITT)
    time_narrow = time_basis.astype(jnp.bfloat16)
    zero_block = jnp.zeros_like(time_narrow)
    pair_basis = jnp.stack(
        [
            jnp.concatenate([time_narrow, zero_block], axis=1),
            jnp.concatenate([zero_block, time_narrow], axis=1),
        ]
    )
    pair_count = cell_count // 2
    paired = snapshots.reshape(variables, planes, pair_count, 2, window)
    core_time = jnp.einsum(
        "vxpqt,qtl->vxpl", paired, pair_basis, preferred_element_type=jnp.float32
    ).astype(jnp.bfloat16)
    pencils = lax.all_to_all(core_time, ("blk", "pen"), split_axis=2, concat_axis=1, tiled=True)
    column_total = float(variables * pencils.shape[2] * pencils.shape[3] * devices_all)
    partial_plane = jnp.einsum(
        "vxpl,vypl->xy", pencils, pencils, preferred_element_type=jnp.float32
    )
    gram_plane = lax.psum(partial_plane, ("blk", "pen")) / column_total
    plane_basis = subspace(gram_plane, start_plane, ITX)
    plane_narrow = plane_basis.astype(jnp.bfloat16)
    core_blocks = jnp.einsum(
        "xk,vxpl->vkpl", plane_narrow, pencils, preferred_element_type=jnp.float32
    ).astype(jnp.bfloat16)
    core_tensor = core_blocks.reshape(variables, core_blocks.shape[1], -1)
    return (time_basis, plane_basis, core_tensor)


def solution(mesh):
    return jax.shard_map(
        on_device,
        mesh=mesh,
        in_specs=(P(None, ("blk", "pen"), None, None), P(), P()),
        out_specs=(P(), P(), P(None, None, ("blk", "pen"))),
        check_vma=False,
    )
```

profile of v0, /device:TPU:1, one launch (start us, length us, event | category | flops | bytes accessed | tf_op | source)
XLA Modules:
  0.0 526.8 jit_solution(338363436475321392)
XLA Ops:
  7.2 8.8 %convolution_bitcast_fusion.2 = f32[128,128]{1,0:T(8,128)} fusion(bf16[4,4,2048,128]{3,2,1,0:T(8,128)(2,1)} %param.9), kind=kOutput, calls=%fused_computation.11 | convolution fusion | flops 1073741824 | bytes 8454144 | tf_op jit(solution)/shard_map/dot_general | solution.py:32
  16.3 142.9 %all-reduce.5.cloned.1.call-done = f32[128,128]{1,0:T(8,128)} async-done(((f32[128,128]{1,0:T(8,128)}), f32[128,128]{1,0:T(8,128)}) %all-reduce.5.cloned.1.call-update) | async-done | bytes 65552 | tf_op jit(solution)/shard_map/psum | solution.py:33
  160.5 5.8 %cholesky.206 = f32[64,64]{1,0:T(8,128)S(1)} custom-call(f32[64,64]{1,0:T(8,128)S(1)} %fusion.62), custom_call_target="Cholesky" | custom-call | tf_op jit(solution)/shard_map/jit(cholesky)/cholesky | solution.py:16
  167.7 4.9 custom-call.20
  173.2 5.8 %cholesky.217 = f32[64,64]{1,0:T(8,128)S(1)} custom-call(f32[64,64]{1,0:T(8,128)S(1)} %fusion.58), custom_call_target="Cholesky" | custom-call | tf_op jit(solution)/shard_map/jit(cholesky)/cholesky | solution.py:16
  180.4 4.9 custom-call.21
  186.9 5.8 %cholesky.228 = f32[64,64]{1,0:T(8,128)S(1)} custom-call(f32[64,64]{1,0:T(8,128)S(1)} %fusion.55), custom_call_target="Cholesky" | custom-call | tf_op jit(solution)/shard_map/jit(cholesky)/cholesky | solution.py:16
  194.1 4.9 custom-call.22
  199.5 5.8 %cholesky.239 = f32[64,64]{1,0:T(8,128)S(1)} custom-call(f32[64,64]{1,0:T(8,128)S(1)} %fusion.51), custom_call_target="Cholesky" | custom-call | tf_op jit(solution)/shard_map/jit(cholesky)/cholesky | solution.py:16
  206.7 4.9 custom-call.23
  213.2 5.8 %cholesky.250 = f32[64,64]{1,0:T(8,128)S(1)} custom-call(f32[64,64]{1,0:T(8,128)S(1)} %fusion.48), custom_call_target="Cholesky" | custom-call | tf_op jit(solution)/shard_map/jit(cholesky)/cholesky | solution.py:16
  220.4 4.9 custom-call.24
  225.8 5.8 %cholesky.261 = f32[64,64]{1,0:T(8,128)S(1)} custom-call(f32[64,64]{1,0:T(8,128)S(1)} %fusion.44), custom_call_target="Cholesky" | custom-call | tf_op jit(solution)/shard_map/jit(cholesky)/cholesky | solution.py:16
  233.0 5.1 custom-call.25
  239.0 8.2 %fusion.2 = bf16[4,4,1024,128]{2,3,1,0:T(8,128)(2,1)} fusion(bf16[4,4,1024,2,128]{4,3,2,1,0:T(2,128)(2,1)} %bitcast.214, bf16[1,128,128]{1,2,0:T(8,128)(2,1)S(1)} %get-tuple-element.8, bf16[1,128,128]{1,2,0:T(8,128)(2,1)S(1)} %get-tuple-element.6), kind=kOutput, calls=%fused_computation.3 | convolution fusion | flops 1075970048 | bytes 12648448 | tf_op jit(solution)/shard_map/vxpqt,qtl->vxpl/dot_general | solution.py:47
  247.2 7.8 %copy.48 = bf16[4,4,1024,128]{3,1,0,2:T(4,128)(2,1)} copy(bf16[4,4,1024,128]{2,3,1,0:T(8,128)(2,1)} %fusion.2) | data formatting | bytes 8388608 | tf_op jit(solution)/shard_map/convert_element_type | solution.py:49
  255.0 58.5 %all_to_all.18 = bf16[4,4,1024,128]{3,1,0,2:T(4,128)(2,1)S(1)} all-to-all(bf16[4,4,1024,128]{3,1,0,2:T(4,128)(2,1)} %copy.48), channel_id=1, replica_groups=mesh['blk'=32,'pen'=4] {'blk','pen'}, dimensions={2} | all-to-all | bytes 8388608 | tf_op jit(solution)/shard_map/all_to_all | solution.py:50
  314.6 3.2 copy.50
  319.7 3.4 convolution_bitcast_fusion
  323.1 143.6 %all-reduce.7.cloned.1.call-done = f32[512,512]{1,0:T(8,128)} async-done(((f32[512,512]{1,0:T(8,128)}), f32[512,512]{1,0:T(8,128)}) %all-reduce.7.cloned.1.call-update) | async-done | bytes 1048592 | tf_op jit(solution)/shard_map/psum | solution.py:55
  469.4 2.9 cholesky.272
  476.7 2.9 cholesky.283
  486.3 2.9 cholesky.294
  516.2 3.0 fusion.10
  (116 shorter events, 59.4 us)
Async XLA Ops:
  7.2 459.6 %copy-start = (f32[512,32]{0,1:T(8,128)S(1)}, f32[512,32]{0,1:T(8,128)}, u32[]{:S(2)}) copy-start(f32[512,32]{0,1:T(8,128)} %param.11) | copy-start | bytes 196612
  7.2 152.0 %copy-start.4 = (f32[128,64]{0,1:T(8,128)S(1)}, f32[128,64]{0,1:T(8,128)}, u32[]{:S(2)}) copy-start(f32[128,64]{0,1:T(8,128)} %param.10) | copy-start | bytes 98308
  7.2 152.0 %all-reduce.5.cloned.1.call-start = ((), (), s32[]{:S(2)}) async-start(), calls=%async_computation.1 | async-start | bytes 131072 | tf_op jit(solution)/shard_map/psum | solution.py:33
  16.0 450.7 %all-reduce.7.cloned.1.call-start = ((), (), s32[]{:S(2)}) async-start(), calls=%async_computation.2 | async-start | bytes 2097152 | tf_op jit(solution)/shard_map/psum | solution.py:55
  317.8 1.9 copy-start.1
  466.7 33.8 %copy-start.2 = (f32[512,512]{1,0:T(8,128)S(1)}, f32[512,512]{1,0:T(8,128)}, u32[]{:S(2)}) copy-start(f32[512,512]{1,0:T(8,128)} %all-reduce.7.cloned.1.call-done) | copy-start | bytes 3145732
  516.1 3.8 copy-start.3
Sparse Core Ops, SparseCore 0:
  16.2 142.9 all-reduce.4
  323.3 143.4 all-reduce.6
where the time goes:
time: 528 us; the launch traced here: 527 us
  waiting for transfers between devices  287 us (54%)
  other arithmetic  113 us (21%)
  blocking collectives  58.5 us (11%)
  matrix products  38.5 us (7%)
  local copies, waits for them, and re-layouts  15.8 us (3%)
  between operations  14.5 us (3%)
    psum x1, waiting for transfers between devices, on_device(): gram_plane = lax.psum(partial_plane, ('blk', 'pen')) / column_total  144 us
    psum x1, waiting for transfers between devices, on_device(): lax.psum(partial_time, ('blk', 'pen'))  143 us
    another operation x36, other arithmetic, orthonormal(): lower_factor = jnp.linalg.cholesky(square_gram)  60.7 us
    all_to_all x1, blocking collectives, on_device(): lax.all_to_all(core_time, ('blk', 'pen'), split_axis=2, concat_axis=1, ti...  58.5 us
    another operation x24, other arithmetic, orthonormal(): jax.scipy.linalg.solve_triangular(lower_factor, matrix.T, lower=True)  52 us
  transfers between devices with their start and end apart: 2, of which 2 were waited for; matrix products, arithmetic and copies ran while one was open for 0% of the time, Pallas kernels for 0%

commit v1 on v0

--- a/solution.py
+++ b/solution.py
@@ -25,14 +25,65 @@
     return current
 
 
+class Torus:
+    def __init__(self):
+        self.blk = lax.axis_size("blk")
+        self.side = {"x": lax.axis_size("pen")}
+        self.side["y"] = 4
+        self.side["z"] = self.blk // 8
+        index = lax.axis_index("blk")
+        self.core = index % 2
+        self.place = {"x": lax.axis_index("pen"), "y": (index // 2) % 4, "z": index // 8}
+
+    def swap(self, value, axis, step):
+        if axis == "x":
+            return lax.ppermute(value, "pen", [(s, s ^ step) for s in range(self.side["x"])])
+        step = {"core": step, "y": step * 2, "z": step * 8}[axis]
+        return lax.ppermute(value, "blk", [(s, s ^ step) for s in range(self.blk)])
+
+    def all_sum(self, value, axis):
+        near, across, far = [self.swap(value, axis, step) for step in (1, 2, 3)]
+        return (value + near) + (across + far)
+
+    def scatter_sum(self, value, axis):
+        pieces = value.reshape((4, value.shape[0] // 4) + value.shape[1:])
+        place = self.place[axis]
+        take = lambda step: lax.dynamic_index_in_dim(pieces, place ^ step, 0, False)
+        near, across, far = [self.swap(take(step), axis, step) for step in (1, 2, 3)]
+        return (take(0) + near) + (across + far)
+
+    def gather(self, value, axis):
+        place = self.place[axis]
+        result = jnp.zeros((4,) + value.shape, value.dtype)
+        for step in range(4):
+            piece = value if step == 0 else self.swap(value, axis, step)
+            result = lax.dynamic_update_index_in_dim(result, piece, place ^ step, 0)
+        return result.reshape((4 * value.shape[0],) + value.shape[1:])
+
+    def core_scatter_sum(self, value):
+        pieces = value.reshape((2, value.shape[0] // 2) + value.shape[1:])
+        mine = lax.dynamic_index_in_dim(pieces, self.core, 0, False)
+        other = lax.dynamic_index_in_dim(pieces, 1 - self.core, 0, False)
+        return mine + self.swap(other, "core", 1)
+
+    def core_gather(self, value):
+        other = self.swap(value, "core", 1)
+        first = jnp.where(self.core == 0, value, other)
+        second = jnp.where(self.core == 0, other, value)
+        return jnp.concatenate([first, second])
+
+
 def on_device(snapshots, start_time, start_plane):
     variables, planes, cell_count, window = snapshots.shape
     devices_all = lax.axis_size("blk") * lax.axis_size("pen")
+    torus = Torus()
     row_matrix = snapshots.reshape(variables * planes * cell_count, window)
     partial_time = jnp.dot(row_matrix.T, row_matrix, preferred_element_type=jnp.float32)
-    gram_time = lax.psum(partial_time, ("blk", "pen")) / float(
-        variables * planes * cell_count * devices_all
-    )
+    total_time = torus.core_scatter_sum(partial_time)
+    for axis in "xyz":
+        total_time = torus.all_sum(total_time, axis)
+    total_time = torus.core_gather(total_time)
+    gram_time = total_time / float(variables * planes * cell_count * devices_all)
     time_basis = subspace(gram_time, start_time, ITT)
     time_narrow = time_basis.astype(jnp.bfloat16)
     zero_block = jnp.zeros_like(time_narrow)
@@ -52,7 +103,12 @@
     partial_plane = jnp.einsum(
         "vxpl,vypl->xy", pencils, pencils, preferred_element_type=jnp.float32
     )
-    gram_plane = lax.psum(partial_plane, ("blk", "pen")) / column_total
+    total_plane = torus.core_scatter_sum(partial_plane)
+    total_plane = torus.scatter_sum(total_plane, "x")
+    total_plane = torus.all_sum(total_plane, "y")
+    total_plane = torus.all_sum(total_plane, "z")
+    total_plane = torus.core_gather(torus.gather(total_plane, "x"))
+    gram_plane = total_plane / column_total
     plane_basis = subspace(gram_plane, start_plane, ITX)
     plane_narrow = plane_basis.astype(jnp.bfloat16)
     core_blocks = jnp.einsum(

time: 528 us -> 316 us (0.60)
  waiting for transfers between devices: 287 us -> 42.8 us
  starting transfers between devices: 0.26 us -> 38 us
  between operations: 14.5 us -> 1.71 us
  local copies, waits for them, and re-layouts: 15.8 us -> 25.9 us
  matrix products: 38.5 us -> 31.7 us
    psum x2 -> x0, waiting for transfers between devices: 286 us -> none  [the longest x1 144 us: on_device(): gram_plane = lax.psum(partial_plane, ('blk', 'pen')) / column_total]
    ppermute x0 -> x25, waiting for transfers between devices: none -> 42.8 us  [the longest x16 25.5 us: swap(): return lax.ppermute(value, 'blk', [(s, s ^ step) for s in range(self.blk)])]
    ppermute x0 -> x25, starting transfers between devices: none -> 38 us  [the longest x16 26.3 us: swap(): return lax.ppermute(value, 'blk', [(s, s ^ step) for s in range(self.blk)])]
    dot_general x0 -> x1, local copies, waits for them, and re-layouts: none -> 11.9 us  [on_device(): jnp.dot(row_matrix.T, row_matrix, preferred_element_type=jnp.float32)]
  transfers between devices with their start and end apart: 2 -> 25, of which waited for: 2 -> 20; matrix products, arithmetic and copies ran while one was open for 0% -> 0% of each run, Pallas kernels for 0% -> 0%
where the time goes in v1:
time: 316 us; the launch traced here: 311 us
  other arithmetic  113 us (36%)
  blocking collectives  57.6 us (18%)
  waiting for transfers between devices  42.8 us (14%)
  starting transfers between devices  38 us (12%)
  matrix products  31.7 us (10%)
  local copies, waits for them, and re-layouts  25.9 us (8%)
    another operation x36, other arithmetic, orthonormal(): lower_factor = jnp.linalg.cholesky(square_gram)  60.7 us
    all_to_all x1, blocking collectives, on_device(): lax.all_to_all(core_time, ('blk', 'pen'), split_axis=2, concat_axis=1, ti...  57.6 us
    another operation x24, other arithmetic, orthonormal(): jax.scipy.linalg.solve_triangular(lower_factor, matrix.T, lower=True)  52 us
    ppermute x16, starting transfers between devices, swap(): return lax.ppermute(value, 'blk', [(s, s ^ step) for s in range(self.blk)])  26.3 us
    ppermute x16, waiting for transfers between devices, swap(): return lax.ppermute(value, 'blk', [(s, s ^ step) for s in range(self.blk)])  25.5 us
    ppermute x9, waiting for transfers between devices, swap(): lax.ppermute(value, 'pen', [(s, s ^ step) for s in range(self.side['x'])])  17.3 us
    dot_general x1, local copies, waits for them, and re-layouts, on_device(): jnp.dot(row_matrix.T, row_matrix, preferred_element_type=jnp.float32)  11.9 us
    ppermute x9, starting transfers between devices, swap(): lax.ppermute(value, 'pen', [(s, s ^ step) for s in range(self.side['x'])])  11.7 us
  transfers between devices with their start and end apart: 25, of which 20 were waited for; matrix products, arithmetic and copies ran while one was open for 0% of the time, Pallas kernels for 0%

profile of v1, /device:TPU:1, one launch (start us, length us, event | category | flops | bytes accessed | tf_op | source)
XLA Modules:
  0.0 310.8 jit_solution(15906724469030911145)
XLA Ops:
  0.7 11.9 %copy.42 = bf16[128,32768]{1,0:T(8,128)(2,1)} copy(bf16[128,32768]{0,1:T(8,128)(2,1)} %bitcast.254) | data formatting | bytes 16777216 | tf_op jit(solution)/shard_map/dot_general | solution.py:81
  12.6 8.1 %fusion.116 = f32[2,64,128]{2,1,0:T(8,128)S(1)} fusion(bf16[2,64,32768]{2,1,0:T(8,128)(2,1)} %bitcast.257, bf16[32768,128,1]{1,0,2:T(8,128)(2,1)} %bitcast.255), kind=kOutput, calls=%fused_computation.184 | convolution fusion | flops 1073741824 | bytes 16842752 | tf_op jit(solution)/shard_map/dot_general | solution.py:81
  40.5 3.3 %collective-permute-start.8 = (f32[64,128]{1,0:T(8,128)S(1)}, f32[64,128]{1,0:T(8,128)S(1)}, u32[]{:S(2)}, u32[]{:S(2)}) collective-permute-start(f32[64,128]{1,0:T(8,128)S(1)} %add_add_fusion.3), channel_id=1, source_target_pairs={{0,64},{4,68},{8,72},{12,76},{16,80},{20,84},{24,88},{28,92},{32,9... | collective-permute-start | bytes 98312 | tf_op jit(solution)/shard_map/ppermute | solution.py:42
  47.8 5.7 %collective-permute-start.10 = (f32[64,128]{1,0:T(8,128)S(1)}, f32[64,128]{1,0:T(8,128)S(1)}, u32[]{:S(2)}, u32[]{:S(2)}) collective-permute-start(f32[64,128]{1,0:T(8,128)S(1)} %add_add_fusion.2), channel_id=1, source_target_pairs={{0,4},{4,0},{8,12},{12,8},{16,20},{20,16},{24,28},{28,24},{32,36},... | collective-permute-start | bytes 98312 | tf_op jit(solution)/shard_map/ppermute | solution.py:42
  54.9 5.8 %cholesky.206 = f32[64,64]{1,0:T(8,128)S(1)} custom-call(f32[64,64]{1,0:T(8,128)S(1)} %fusion.57), custom_call_target="Cholesky" | custom-call | tf_op jit(solution)/shard_map/jit(cholesky)/cholesky | solution.py:16
  62.1 4.9 %custom-call.20 = f32[1,64,64]{1,2,0:T(8,128)S(1)} custom-call(f32[1,64,64]{2,1,0:T(8,128)S(1)} %fusion.31), custom_call_target="InvertDiagBlocksLowerTriangular" | custom-call | tf_op jit(solution)/shard_map/jit(_solve_triangular)/triangular_solve | solution.py:17
  67.6 5.8 %cholesky.217 = f32[64,64]{1,0:T(8,128)S(1)} custom-call(f32[64,64]{1,0:T(8,128)S(1)} %fusion.53), custom_call_target="Cholesky" | custom-call | tf_op jit(solution)/shard_map/jit(cholesky)/cholesky | solution.py:16
  74.7 4.9 %custom-call.21 = f32[1,64,64]{1,2,0:T(8,128)S(1)} custom-call(f32[1,64,64]{2,1,0:T(8,128)S(1)} %fusion.32), custom_call_target="InvertDiagBlocksLowerTriangular" | custom-call | tf_op jit(solution)/shard_map/jit(_solve_triangular)/triangular_solve | solution.py:17
  80.4 5.8 %cholesky.228 = f32[64,64]{1,0:T(8,128)S(1)} custom-call(f32[64,64]{1,0:T(8,128)S(1)} %fusion.50), custom_call_target="Cholesky" | custom-call | tf_op jit(solution)/shard_map/jit(cholesky)/cholesky | solution.py:16
  87.6 4.9 %custom-call.22 = f32[1,64,64]{1,2,0:T(8,128)S(1)} custom-call(f32[1,64,64]{2,1,0:T(8,128)S(1)} %fusion.33), custom_call_target="InvertDiagBlocksLowerTriangular" | custom-call | tf_op jit(solution)/shard_map/jit(_solve_triangular)/triangular_solve | solution.py:17
  93.1 5.8 %cholesky.239 = f32[64,64]{1,0:T(8,128)S(1)} custom-call(f32[64,64]{1,0:T(8,128)S(1)} %fusion.46), custom_call_target="Cholesky" | custom-call | tf_op jit(solution)/shard_map/jit(cholesky)/cholesky | solution.py:16
  100.2 4.9 %custom-call.23 = f32[1,64,64]{1,2,0:T(8,128)S(1)} custom-call(f32[1,64,64]{2,1,0:T(8,128)S(1)} %fusion.34), custom_call_target="InvertDiagBlocksLowerTriangular" | custom-call | tf_op jit(solution)/shard_map/jit(_solve_triangular)/triangular_solve | solution.py:17
  105.9 5.8 %cholesky.250 = f32[64,64]{1,0:T(8,128)S(1)} custom-call(f32[64,64]{1,0:T(8,128)S(1)} %fusion.43), custom_call_target="Cholesky" | custom-call | tf_op jit(solution)/shard_map/jit(cholesky)/cholesky | solution.py:16
  113.1 4.9 %custom-call.24 = f32[1,64,64]{1,2,0:T(8,128)S(1)} custom-call(f32[1,64,64]{2,1,0:T(8,128)S(1)} %fusion.35), custom_call_target="InvertDiagBlocksLowerTriangular" | custom-call | tf_op jit(solution)/shard_map/jit(_solve_triangular)/triangular_solve | solution.py:17
  118.6 5.8 %cholesky.261 = f32[64,64]{1,0:T(8,128)S(1)} custom-call(f32[64,64]{1,0:T(8,128)S(1)} %fusion.39), custom_call_target="Cholesky" | custom-call | tf_op jit(solution)/shard_map/jit(cholesky)/cholesky | solution.py:16
  125.7 5.1 %custom-call.25 = f32[1,64,64]{1,2,0:T(8,128)S(1)} custom-call(f32[1,64,64]{2,1,0:T(8,128)S(1)} %fusion.36), custom_call_target="InvertDiagBlocksLowerTriangular" | custom-call | tf_op jit(solution)/shard_map/jit(_solve_triangular)/triangular_solve | solution.py:17
  131.7 8.2 %fusion.2 = bf16[4,4,1024,128]{2,3,1,0:T(8,128)(2,1)} fusion(bf16[4,4,1024,2,128]{4,3,2,1,0:T(2,128)(2,1)} %bitcast.256, bf16[1,128,128]{1,2,0:T(8,128)(2,1)S(1)} %get-tuple-element.17, bf16[1,128,128]{1,2,0:T(8,128)(2,1)S(1)} %get-tuple-element.16), kind=kOutput, calls=%fused_computation.3 | convolution fusion | flops 1075970048 | bytes 12648448 | tf_op jit(solution)/shard_map/vxpqt,qtl->vxpl/dot_general | solution.py:98
  139.9 7.8 %copy.50 = bf16[4,4,1024,128]{3,1,0,2:T(4,128)(2,1)} copy(bf16[4,4,1024,128]{2,3,1,0:T(8,128)(2,1)} %fusion.2) | data formatting | bytes 8388608 | tf_op jit(solution)/shard_map/convert_element_type | solution.py:100
  147.7 57.6 %all_to_all.18 = bf16[4,4,1024,128]{3,1,0,2:T(4,128)(2,1)S(1)} all-to-all(bf16[4,4,1024,128]{3,1,0,2:T(4,128)(2,1)} %copy.50), channel_id=1, replica_groups=mesh['blk'=32,'pen'=4] {'blk','pen'}, dimensions={2} | all-to-all | bytes 8388608 | tf_op jit(solution)/shard_map/all_to_all | solution.py:101
  206.4 3.2 %copy.52 = bf16[4,128,4,8,128]{4,2,1,0,3:T(4,128)(2,1)S(1)} copy(bf16[4,128,4,8,128]{4,3,1,2,0:T(8,128)(2,1)S(1)} %bitcast.261) | data formatting | bytes 8388608 | tf_op jit(solution)/shard_map/all_to_all | solution.py:101
  219.0 3.7 %collective-permute-done.13 = f32[64,512]{1,0:T(8,128)S(1)} collective-permute-done((f32[64,512]{1,0:T(8,128)S(1)}, f32[64,512]{1,0:T(8,128)S(1)}, u32[]{:S(2)}, u32[]{:S(2)}) %collective-permute-start.13) | collective-permute-done | bytes 131104 | tf_op jit(solution)/shard_map/ppermute | solution.py:40
  229.3 3.2 %collective-permute-done.16 = f32[64,512]{1,0:T(8,128)S(1)} collective-permute-done((f32[64,512]{1,0:T(8,128)S(1)}, f32[64,512]{1,0:T(8,128)S(1)}, u32[]{:S(2)}, u32[]{:S(2)}) %collective-permute-start.16) | collective-permute-done | bytes 131104 | tf_op jit(solution)/shard_map/ppermute | solution.py:42
  239.3 3.9 %collective-permute-done.19 = f32[64,512]{1,0:T(8,128)S(1)} collective-permute-done((f32[64,512]{1,0:T(8,128)S(1)}, f32[64,512]{1,0:T(8,128)S(1)}, u32[]{:S(2)}, u32[]{:S(2)}) %collective-permute-start.19) | collective-permute-done | bytes 131104 | tf_op jit(solution)/shard_map/ppermute | solution.py:42
  243.2 3.1 collective-permute-done.20
  (176 shorter events, 124.6 us)
Async XLA Ops:
  20.7 2.3 collective-permute-start
  23.0 3.9 %collective-permute-start.1 = (f32[64,128]{1,0:T(8,128)S(1)}, f32[64,128]{1,0:T(8,128)S(1)}, u32[]{:S(2)}, u32[]{:S(2)}) collective-permute-start(f32[64,128]{1,0:T(8,128)S(1)} %bitcast_add_fusion.8), channel_id=1, source_target_pairs={{0,1},{1,0},{2,3},{3,2},{4,5},{5,4},{6,7},{7,6},{8,9},{9,8},{10,11... | collective-permute-start | bytes 98312 | tf_op jit(solution)/shard_map/ppermute | solution.py:40
  24.4 4.3 %collective-permute-start.2 = (f32[64,128]{1,0:T(8,128)S(1)}, f32[64,128]{1,0:T(8,128)S(1)}, u32[]{:S(2)}, u32[]{:S(2)}) collective-permute-start(f32[64,128]{1,0:T(8,128)S(1)} %bitcast_add_fusion.8), channel_id=1, source_target_pairs={{0,2},{1,3},{2,0},{3,1},{4,6},{5,7},{6,4},{7,5},{8,10},{9,11},{10,... | collective-permute-start | bytes 98312 | tf_op jit(solution)/shard_map/ppermute | solution.py:40
  26.8 4.0 %collective-permute-start.3 = (f32[64,128]{1,0:T(8,128)S(1)}, f32[64,128]{1,0:T(8,128)S(1)}, u32[]{:S(2)}, u32[]{:S(2)}) collective-permute-start(f32[64,128]{1,0:T(8,128)S(1)} %bitcast_add_fusion.8), channel_id=1, source_target_pairs={{0,3},{1,2},{2,1},{3,0},{4,7},{5,6},{6,5},{7,4},{8,11},{9,10},{10,... | collective-permute-start | bytes 98312 | tf_op jit(solution)/shard_map/ppermute | solution.py:40
  30.8 4.0 %collective-permute-start.4 = (f32[64,128]{1,0:T(8,128)S(1)}, f32[64,128]{1,0:T(8,128)S(1)}, u32[]{:S(2)}, u32[]{:S(2)}) collective-permute-start(f32[64,128]{1,0:T(8,128)S(1)} %add_add_fusion.4), channel_id=1, source_target_pairs={{0,8},{4,12},{8,0},{12,4},{16,24},{20,28},{24,16},{28,20},{32,40},... | collective-permute-start | bytes 98312 | tf_op jit(solution)/shard_map/ppermute | solution.py:42
  32.2 4.3 %collective-permute-start.5 = (f32[64,128]{1,0:T(8,128)S(1)}, f32[64,128]{1,0:T(8,128)S(1)}, u32[]{:S(2)}, u32[]{:S(2)}) collective-permute-start(f32[64,128]{1,0:T(8,128)S(1)} %add_add_fusion.4), channel_id=1, source_target_pairs={{0,16},{4,20},{8,24},{12,28},{16,0},{20,4},{24,8},{28,12},{32,48},... | collective-permute-start | bytes 98312 | tf_op jit(solution)/shard_map/ppermute | solution.py:42
  34.8 4.0 %collective-permute-start.6 = (f32[64,128]{1,0:T(8,128)S(1)}, f32[64,128]{1,0:T(8,128)S(1)}, u32[]{:S(2)}, u32[]{:S(2)}) collective-permute-start(f32[64,128]{1,0:T(8,128)S(1)} %add_add_fusion.4), channel_id=1, source_target_pairs={{0,24},{4,28},{8,16},{12,20},{16,8},{20,12},{24,0},{28,4},{32,56},... | collective-permute-start | bytes 98312 | tf_op jit(solution)/shard_map/ppermute | solution.py:42
  38.8 5.0 %collective-permute-start.7 = (f32[64,128]{1,0:T(8,128)S(1)}, f32[64,128]{1,0:T(8,128)S(1)}, u32[]{:S(2)}, u32[]{:S(2)}) collective-permute-start(f32[64,128]{1,0:T(8,128)S(1)} %add_add_fusion.3), channel_id=1, source_target_pairs={{0,32},{4,36},{8,40},{12,44},{16,48},{20,52},{24,56},{28,60},{32,0... | collective-permute-start | bytes 98312 | tf_op jit(solution)/shard_map/ppermute | solution.py:42
  40.5 5.0 %collective-permute-start.8 = (f32[64,128]{1,0:T(8,128)S(1)}, f32[64,128]{1,0:T(8,128)S(1)}, u32[]{:S(2)}, u32[]{:S(2)}) collective-permute-start(f32[64,128]{1,0:T(8,128)S(1)} %add_add_fusion.3), channel_id=1, source_target_pairs={{0,64},{4,68},{8,72},{12,76},{16,80},{20,84},{24,88},{28,92},{32,9... | collective-permute-start | bytes 98312 | tf_op jit(solution)/shard_map/ppermute | solution.py:42
  43.8 4.0 %collective-permute-start.9 = (f32[64,128]{1,0:T(8,128)S(1)}, f32[64,128]{1,0:T(8,128)S(1)}, u32[]{:S(2)}, u32[]{:S(2)}) collective-permute-start(f32[64,128]{1,0:T(8,128)S(1)} %add_add_fusion.3), channel_id=1, source_target_pairs={{0,96},{4,100},{8,104},{12,108},{16,112},{20,116},{24,120},{28,124... | collective-permute-start | bytes 98312 | tf_op jit(solution)/shard_map/ppermute | solution.py:42
  47.8 6.6 %collective-permute-start.10 = (f32[64,128]{1,0:T(8,128)S(1)}, f32[64,128]{1,0:T(8,128)S(1)}, u32[]{:S(2)}, u32[]{:S(2)}) collective-permute-start(f32[64,128]{1,0:T(8,128)S(1)} %add_add_fusion.2), channel_id=1, source_target_pairs={{0,4},{4,0},{8,12},{12,8},{16,20},{20,16},{24,28},{28,24},{32,36},... | collective-permute-start | bytes 98312 | tf_op jit(solution)/shard_map/ppermute | solution.py:42
  214.3 4.8 %collective-permute-start.12 = (f32[64,512]{1,0:T(8,128)S(1)}, f32[64,512]{1,0:T(8,128)S(1)}, u32[]{:S(2)}, u32[]{:S(2)}) collective-permute-start(f32[64,512]{1,0:T(8,128)S(1)} %get-tuple-element.13), channel_id=1, source_target_pairs={{0,1},{1,0},{2,3},{3,2},{4,5},{5,4},{6,7},{7,6},{8,9},{9,8},{10,11... | collective-permute-start | bytes 393224 | tf_op jit(solution)/shard_map/ppermute | solution.py:40
  214.4 8.4 %collective-permute-start.13 = (f32[64,512]{1,0:T(8,128)S(1)}, f32[64,512]{1,0:T(8,128)S(1)}, u32[]{:S(2)}, u32[]{:S(2)}) collective-permute-start(f32[64,512]{1,0:T(8,128)S(1)} %get-tuple-element.12), channel_id=1, source_target_pairs={{0,2},{1,3},{2,0},{3,1},{4,6},{5,7},{6,4},{7,5},{8,10},{9,11},{10,... | collective-permute-start | bytes 393224 | tf_op jit(solution)/shard_map/ppermute | solution.py:40
  216.7 8.6 %collective-permute-start.14 = (f32[64,512]{1,0:T(8,128)S(1)}, f32[64,512]{1,0:T(8,128)S(1)}, u32[]{:S(2)}, u32[]{:S(2)}) collective-permute-start(f32[64,512]{1,0:T(8,128)S(1)} %get-tuple-element.11), channel_id=1, source_target_pairs={{0,3},{1,2},{2,1},{3,0},{4,7},{5,6},{6,5},{7,4},{8,11},{9,10},{10,... | collective-permute-start | bytes 393224 | tf_op jit(solution)/shard_map/ppermute | solution.py:40
  225.4 3.9 %collective-permute-start.15 = (f32[64,512]{1,0:T(8,128)S(1)}, f32[64,512]{1,0:T(8,128)S(1)}, u32[]{:S(2)}, u32[]{:S(2)}) collective-permute-start(f32[64,512]{1,0:T(8,128)S(1)} %fusion.19), channel_id=1, source_target_pairs={{0,8},{4,12},{8,0},{12,4},{16,24},{20,28},{24,16},{28,20},{32,40},... | collective-permute-start | bytes 393224 | tf_op jit(solution)/shard_map/ppermute | solution.py:42
  225.4 7.1 %collective-permute-start.16 = (f32[64,512]{1,0:T(8,128)S(1)}, f32[64,512]{1,0:T(8,128)S(1)}, u32[]{:S(2)}, u32[]{:S(2)}) collective-permute-start(f32[64,512]{1,0:T(8,128)S(1)} %fusion.19), channel_id=1, source_target_pairs={{0,16},{4,20},{8,24},{12,28},{16,0},{20,4},{24,8},{28,12},{32,48},... | collective-permute-start | bytes 393224 | tf_op jit(solution)/shard_map/ppermute | solution.py:42
  226.9 8.2 %collective-permute-start.17 = (f32[64,512]{1,0:T(8,128)S(1)}, f32[64,512]{1,0:T(8,128)S(1)}, u32[]{:S(2)}, u32[]{:S(2)}) collective-permute-start(f32[64,512]{1,0:T(8,128)S(1)} %fusion.19), channel_id=1, source_target_pairs={{0,24},{4,28},{8,16},{12,20},{16,8},{20,12},{24,0},{28,4},{32,56},... | collective-permute-start | bytes 393224 | tf_op jit(solution)/shard_map/ppermute | solution.py:42
  235.1 4.2 %collective-permute-start.18 = (f32[64,512]{1,0:T(8,128)S(1)}, f32[64,512]{1,0:T(8,128)S(1)}, u32[]{:S(2)}, u32[]{:S(2)}) collective-permute-start(f32[64,512]{1,0:T(8,128)S(1)} %add_add_fusion.1), channel_id=1, source_target_pairs={{0,32},{4,36},{8,40},{12,44},{16,48},{20,52},{24,56},{28,60},{32,0... | collective-permute-start | bytes 393224 | tf_op jit(solution)/shard_map/ppermute | solution.py:42
  236.3 6.9 %collective-permute-start.19 = (f32[64,512]{1,0:T(8,128)S(1)}, f32[64,512]{1,0:T(8,128)S(1)}, u32[]{:S(2)}, u32[]{:S(2)}) collective-permute-start(f32[64,512]{1,0:T(8,128)S(1)} %add_add_fusion.1), channel_id=1, source_target_pairs={{0,64},{4,68},{8,72},{12,76},{16,80},{20,84},{24,88},{28,92},{32,9... | collective-permute-start | bytes 393224 | tf_op jit(solution)/shard_map/ppermute | solution.py:42
  237.3 9.0 %collective-permute-start.20 = (f32[64,512]{1,0:T(8,128)S(1)}, f32[64,512]{1,0:T(8,128)S(1)}, u32[]{:S(2)}, u32[]{:S(2)}) collective-permute-start(f32[64,512]{1,0:T(8,128)S(1)} %add_add_fusion.1), channel_id=1, source_target_pairs={{0,96},{4,100},{8,104},{12,108},{16,112},{20,116},{24,120},{28,124... | collective-permute-start | bytes 393224 | tf_op jit(solution)/shard_map/ppermute | solution.py:42
  246.4 4.4 %collective-permute-start.21 = (f32[64,512]{1,0:T(8,128)S(1)}, f32[64,512]{1,0:T(8,128)S(1)}, u32[]{:S(2)}, u32[]{:S(2)}) collective-permute-start(f32[64,512]{1,0:T(8,128)S(1)} %get-tuple-element.8), channel_id=1, source_target_pairs={{0,1},{1,0},{2,3},{3,2},{4,5},{5,4},{6,7},{7,6},{8,9},{9,8},{10,11... | collective-permute-start | bytes 393224 | tf_op jit(solution)/shard_map/ppermute | solution.py:40
  246.5 7.3 %collective-permute-start.22 = (f32[64,512]{1,0:T(8,128)S(1)}, f32[64,512]{1,0:T(8,128)S(1)}, u32[]{:S(2)}, u32[]{:S(2)}) collective-permute-start(f32[64,512]{1,0:T(8,128)S(1)} %get-tuple-element.8), channel_id=1, source_target_pairs={{0,2},{1,3},{2,0},{3,1},{4,6},{5,7},{6,4},{7,5},{8,10},{9,11},{10,... | collective-permute-start | bytes 393224 | tf_op jit(solution)/shard_map/ppermute | solution.py:40
  248.7 8.0 %collective-permute-start.23 = (f32[64,512]{1,0:T(8,128)S(1)}, f32[64,512]{1,0:T(8,128)S(1)}, u32[]{:S(2)}, u32[]{:S(2)}) collective-permute-start(f32[64,512]{1,0:T(8,128)S(1)} %get-tuple-element.8), channel_id=1, source_target_pairs={{0,3},{1,2},{2,1},{3,0},{4,7},{5,6},{6,5},{7,4},{8,11},{9,10},{10,... | collective-permute-start | bytes 393224 | tf_op jit(solution)/shard_map/ppermute | solution.py:40
  256.7 2.9 collective-permute-start.24
  (5 other events, 309.2 us)

commit v2 on v1

v2 whole, which is shorter than its diff:
```python
import jax
import jax.numpy as jnp
from jax import lax
from jax.experimental import pallas as pl
from jax.experimental.pallas import tpu as pltpu
from jax.sharding import PartitionSpec as P

ITT = 3
ITX = 3

F32, BF16 = jnp.float32, jnp.bfloat16
HIGHEST = lax.Precision.HIGHEST
VMEM = pl.BlockSpec(memory_space=pltpu.VMEM)


class Torus:
    def __init__(self):
        self.blk = lax.axis_size("blk")
        self.pen = lax.axis_size("pen")
        index = lax.axis_index("blk")
        self.core = index % 2
        self.place = {"x": lax.axis_index("pen"), "y": (index // 2) % 4, "z": index // 8}

    def swap(self, value, axis, step):
        if axis == "x":
            return lax.ppermute(value, "pen", [(s, s ^ step) for s in range(self.pen)])
        step = {"core": step, "y": step * 2, "z": step * 8}[axis]
        return lax.ppermute(value, "blk", [(s, s ^ step) for s in range(self.blk)])

    def all_sum(self, value, axis):
        near, across, far = [self.swap(value, axis, step) for step in (1, 2, 3)]
        return (value + near) + (across + far)

    def scatter_sum(self, value, axis):
        pieces = value.reshape((4, value.shape[0] // 4) + value.shape[1:])
        place = self.place[axis]
        take = lambda step: lax.dynamic_index_in_dim(pieces, place ^ step, 0, False)
        near, across, far = [self.swap(take(step), axis, step) for step in (1, 2, 3)]
        return (take(0) + near) + (across + far)

    def gather(self, value, axis):
        place = self.place[axis]
        result = jnp.zeros((4,) + value.shape, value.dtype)
        for step in range(4):
            piece = value if step == 0 else self.swap(value, axis, step)
            result = lax.dynamic_update_index_in_dim(result, piece, place ^ step, 0)
        return result.reshape((4 * value.shape[0],) + value.shape[1:])

    def core_scatter_sum(self, value):
        pieces = value.reshape((2, value.shape[0] // 2) + value.shape[1:])
        mine = lax.dynamic_index_in_dim(pieces, self.core, 0, False)
        other = lax.dynamic_index_in_dim(pieces, 1 - self.core, 0, False)
        return mine + self.swap(other, "core", 1)

    def core_gather(self, value):
        other = self.swap(value, "core", 1)
        first = jnp.where(self.core == 0, value, other)
        second = jnp.where(self.core == 0, other, value)
        return jnp.concatenate([first, second])


def product(a, b, dim_a, dim_b, precision=HIGHEST):
    dims = (((dim_a,), (dim_b,)), ((), ()))
    return lax.dot_general(a, b, dims, precision=precision, preferred_element_type=F32)


def narrow_product(a, b, dim_a, dim_b):
    return product(a, b, dim_a, dim_b, None)


def identity(size):
    shape = (size, size)
    same = lax.broadcasted_iota(jnp.int32, shape, 0) == lax.broadcasted_iota(jnp.int32, shape, 1)
    return jnp.where(same, 1.0, 0.0).astype(F32)


def inverse_factor(square):
    size = square.shape[0]
    width = 2 * size
    wide = jnp.concatenate([square, identity(size)], axis=1)
    rows = [wide[8 * i : 8 * i + 8] for i in range(size // 8)]
    place = lax.broadcasted_iota(jnp.int32, (8, 1), 0)
    for block in range(size // 8):
        held = rows[block]
        splats = [
            jnp.broadcast_to(held[:, 8 * block + j : 8 * block + j + 1], (8, width)) for j in range(8)
        ]
        for j in range(8):
            factor = jnp.where(place > j, splats[j] * (1.0 / splats[j][j : j + 1]), 0.0)
            held = held - factor * held[j : j + 1]
            for m in range(j + 1, 8):
                splats[m] = splats[m] - factor * splats[m][j : j + 1]
        pivots = jnp.concatenate([splats[j][j : j + 1] for j in range(8)], axis=0)
        held = held * lax.rsqrt(pivots)
        rows[block] = held
        for i in range(block + 1, size // 8):
            column = held[:, 8 * i : 8 * i + 8].T
            total = rows[i]
            for j in range(8):
                total = total - column[:, j : j + 1] * held[j : j + 1]
            rows[i] = total
    return jnp.concatenate(rows, axis=0)[:, size:]


def subspace(gram, flat, sweeps):
    for sweep in range(sweeps):
        flat = product(flat, gram, 1, 0)
        for repeat in range(2 if sweep == sweeps - 1 else 1):
            flat = product(inverse_factor(product(flat, flat, 1, 1)), flat, 1, 0)
    return flat


def time_gram(snapshots):
    variables, planes, cells, window = snapshots.shape
    half = variables // 2
    steps = planes * half

    def kernel(low_ref, high_ref, out_ref, total):
        step = pl.program_id(0) * half + pl.program_id(1)
        both = jnp.concatenate([low_ref[0, 0], high_ref[0, 0]], axis=1)
        part = narrow_product(both, both, 0, 0)

        @pl.when(step == 0)
        def _():
            total[...] = part

        @pl.when(step > 0)
        def _():
            total[...] += part

        @pl.when(step == steps - 1)
        def _():
            out_ref[...] = total[:window, :window] + total[window:, window:]

    block = (1, 1, cells, window)
    return pl.pallas_call(
        kernel,
        grid=(planes, half),
        in_specs=[
            pl.BlockSpec(block, lambda x, v: (v, x, 0, 0)),
            pl.BlockSpec(block, lambda x, v: (v + half, x, 0, 0)),
        ],
        out_specs=pl.BlockSpec((window, window), lambda x, v: (0, 0)),
        out_shape=jax.ShapeDtypeStruct((window, window), F32),
        scratch_shapes=[pltpu.VMEM((2 * window, 2 * window), F32)],
    )(snapshots, snapshots)


def time_subspace(total, start, scale):
    rank, window = start.shape

    def kernel(gram_ref, start_ref, basis_ref, pair_ref):
        flat = subspace(gram_ref[...] * scale, start_ref[...], ITT)
        basis_ref[...] = flat
        narrow = flat.T.astype(BF16)
        zero = jnp.zeros_like(narrow)
        pair_ref[:window] = jnp.concatenate([narrow, zero], axis=1)
        pair_ref[window:] = jnp.concatenate([zero, narrow], axis=1)

    return pl.pallas_call(
        kernel,
        in_specs=[VMEM, VMEM],
        out_specs=[VMEM, VMEM],
        out_shape=[
            jax.ShapeDtypeStruct((rank, window), F32),
            jax.ShapeDtypeStruct((2 * window, 2 * rank), BF16),
        ],
    )(total, start)


def truncate_time(snapshots, pair_basis, owners):
    variables, planes, cells, window = snapshots.shape
    half = variables // 2
    lanes = pair_basis.shape[1]
    mine = cells // owners

    def kernel(low_ref, high_ref, basis_ref, out_ref):
        both = jnp.concatenate([low_ref[0, 0], high_ref[0, 0]], axis=1)
        core = narrow_product(both, basis_ref[...], 1, 0).astype(BF16)
        out_ref[...] = core.reshape(owners, 1, 1, mine, lanes)

    block = (1, 1, cells, window)
    return pl.pallas_call(
        kernel,
        grid=(planes, half),
        in_specs=[
            pl.BlockSpec(block, lambda x, v: (v, x, 0, 0)),
            pl.BlockSpec(block, lambda x, v: (v + half, x, 0, 0)),
            pl.BlockSpec(pair_basis.shape, lambda x, v: (0, 0)),
        ],
        out_specs=pl.BlockSpec((owners, 1, 1, mine, lanes), lambda x, v: (0, x, v, 0, 0)),
        out_shape=jax.ShapeDtypeStruct((owners, planes, half, mine, lanes), BF16),
    )(snapshots, snapshots, pair_basis)


def plane_gram(pencils):
    planes, groups, lanes = pencils.shape
    taken = 16

    def kernel(pencil_ref, gram_ref, group_ref):
        step = pl.program_id(0)
        turned = jnp.swapaxes(pencil_ref[...], 0, 1)
        group_ref[...] = turned
        total = None
        for j in range(0, taken, 2):
            both = jnp.concatenate([turned[j], turned[j + 1]], axis=1)
            part = narrow_product(both, both, 1, 1)
            total = part if total is None else total + part

        @pl.when(step == 0)
        def _():
            gram_ref[...] = total

        @pl.when(step > 0)
        def _():
            gram_ref[...] += total

    return pl.pallas_call(
        kernel,
        grid=(groups // taken,),
        in_specs=[pl.BlockSpec((planes, taken, lanes), lambda i: (0, i, 0))],
        out_specs=[
            pl.BlockSpec((planes, planes), lambda i: (0, 0)),
            pl.BlockSpec((taken, planes, lanes), lambda i: (i, 0, 0)),
        ],
        out_shape=[
            jax.ShapeDtypeStruct((planes, planes), F32),
            jax.ShapeDtypeStruct((groups, planes, lanes), BF16),
        ],
    )(pencils)


def plane_subspace(total, start, groups, scale, half):
    rank, planes = start.shape
    count, _, lanes = groups.shape
    mine = count // half
    ranks = lanes // 2

    def kernel(gram_ref, start_ref, groups_ref, basis_ref, core_ref, held, arrived):
        fetch = pltpu.make_async_copy(groups_ref, held, arrived)
        fetch.start()
        flat = subspace(gram_ref[...] * scale, start_ref[...], ITX)
        basis_ref[...] = flat
        narrow = flat.astype(BF16)
        fetch.wait()
        first = lax.broadcasted_iota(jnp.int32, (rank, lanes), 1) < ranks
        for v in range(half):
            for pair in range(mine // 2):
                even = narrow_product(narrow, held[v * mine + 2 * pair], 1, 0)
                odd = narrow_product(narrow, held[v * mine + 2 * pair + 1], 1, 0)
                low = jnp.where(first, even, pltpu.roll(odd, ranks, 1))
                high = jnp.where(first, pltpu.roll(even, ranks, 1), odd)
                place = slice(pair * lanes, (pair + 1) * lanes)
                core_ref[v, :, place] = low.astype(BF16)
                core_ref[v + half, :, place] = high.astype(BF16)

    return pl.pallas_call(
        kernel,
        in_specs=[VMEM, VMEM, pl.BlockSpec(memory_space=pl.ANY)],
        out_specs=[VMEM, VMEM],
        out_shape=[
            jax.ShapeDtypeStruct((rank, planes), F32),
            jax.ShapeDtypeStruct((2 * half, rank, mine * ranks), BF16),
        ],
        scratch_shapes=[pltpu.VMEM(groups.shape, BF16), pltpu.SemaphoreType.DMA],
    )(total, start, groups)


def on_device(snapshots, start_time, start_plane):
    variables, planes, cells, window = snapshots.shape
    devices_all = lax.axis_size("blk") * lax.axis_size("pen")
    half = variables // 2
    rank = start_time.shape[1]
    torus = Torus()

    total_time = torus.core_scatter_sum(time_gram(snapshots))
    for axis in "xyz":
        total_time = torus.all_sum(total_time, axis)
    total_time = torus.core_gather(total_time)
    scale_time = 1.0 / float(variables * planes * cells * devices_all)
    time_basis, pair_basis = time_subspace(total_time, start_time.T, scale_time)

    core_time = truncate_time(snapshots, pair_basis, devices_all)
    pencils = lax.all_to_all(core_time, ("blk", "pen"), split_axis=0, concat_axis=0, tiled=True)
    partial_plane, groups = plane_gram(pencils.reshape(devices_all * planes, -1, 2 * rank))

    total_plane = torus.core_scatter_sum(partial_plane)
    total_plane = torus.scatter_sum(total_plane, "x")
    total_plane = torus.all_sum(total_plane, "y")
    total_plane = torus.all_sum(total_plane, "z")
    total_plane = torus.core_gather(torus.gather(total_plane, "x"))
    scale_plane = 1.0 / float(variables * cells * rank)
    plane_basis, core_tensor = plane_subspace(total_plane, start_plane.T, groups, scale_plane, half)
    return (time_basis.T, plane_basis.T, core_tensor)


def solution(mesh):
    return jax.shard_map(
        on_device,
        mesh=mesh,
        in_specs=(P(None, ("blk", "pen"), None, None), P(), P()),
        out_specs=(P(), P(), P(None, None, ("blk", "pen"))),
        check_vma=False,
    )
```

time: 316 us -> 200 us (0.63); the launches traced: 311 us -> 199 us
  other arithmetic: 113 us -> 3.86 us
  Pallas kernels: 0 us -> 54.5 us
  matrix products: 31.7 us -> 0 us
  local copies, waits for them, and re-layouts: 25.9 us -> 1.96 us
    another operation x60 -> x0, other arithmetic: 113 us -> none  [the longest x36 60.7 us: orthonormal(): lower_factor = jnp.linalg.cholesky(square_gram)]
    pallas_call x0 -> x5, Pallas kernels: none -> 54.5 us  [the longest x1 17.4 us: time_subspace(): pl.pallas_call(kernel, in_specs=[VMEM, VMEM], out_specs=[VMEM, VMEM], out...]
    dot_general x22 -> x0, matrix products: 27.9 us -> none  [the longest x1 8.2 us: on_device(): jnp.einsum('vxpqt,qtl->vxpl', paired, pair_basis, preferred_element_type=...]
    dot_general x13 -> x0, local copies, waits for them, and re-layouts: 12.8 us -> none  [the longest x1 11.9 us: on_device(): jnp.dot(row_matrix.T, row_matrix, preferred_element_type=jnp.float32)]
    convert_element_type x1 -> x0, local copies, waits for them, and re-layouts: 7.85 us -> none  [on_device(): core_time = jnp.einsum('vxpqt,qtl->vxpl', paired, pair_basis, preferred_e...]
    all_to_all x2 -> x0, local copies, waits for them, and re-layouts: 4.32 us -> none  [on_device(): lax.all_to_all(core_time, ('blk', 'pen'), split_axis=2, concat_axis=1, ti...]
    another operation x12 -> x0, matrix products: 3.8 us -> none  [orthonormal(): jax.scipy.linalg.solve_triangular(lower_factor, matrix.T, lower=True)]
  transfers between devices with their start and end apart: 25 -> 25, of which waited for: 20 -> 19; matrix products, arithmetic and copies ran while one was open for 0% -> 0% of each run, Pallas kernels for 0% -> 0%
where the time goes in v2:
time: 200 us; the launch traced here: 199 us
  blocking collectives  58.3 us (29%)
  Pallas kernels  54.5 us (27%)
  waiting for transfers between devices  42.3 us (21%)
  starting transfers between devices  37.6 us (19%)
  other arithmetic  3.86 us (2%)
    all_to_all x1, blocking collectives, on_device(): lax.all_to_all(core_time, ('blk', 'pen'), split_axis=0, concat_axis=0, ti...  58.3 us
    ppermute x16, starting transfers between devices, swap(): return lax.ppermute(value, 'blk', [(s, s ^ step) for s in range(self.blk)])  25.9 us
    ppermute x16, waiting for transfers between devices, swap(): return lax.ppermute(value, 'blk', [(s, s ^ step) for s in range(self.blk)])  25.2 us
    pallas_call x1, Pallas kernels, time_subspace(): pl.pallas_call(kernel, in_specs=[VMEM, VMEM], out_specs=[VMEM, VMEM], out...  17.4 us
    ppermute x9, waiting for transfers between devices, swap(): return lax.ppermute(value, 'pen', [(s, s ^ step) for s in range(self.pen)])  17.1 us
    pallas_call x1, Pallas kernels, plane_subspace(): pl.pallas_call(kernel, in_specs=[VMEM, VMEM, pl.BlockSpec(memory_space=pl...  13.8 us
    ppermute x9, starting transfers between devices, swap(): return lax.ppermute(value, 'pen', [(s, s ^ step) for s in range(self.pen)])  11.7 us
    pallas_call x1, Pallas kernels, truncate_time(): pl.pallas_call(kernel, grid=(planes, half), in_specs=[pl.BlockSpec(block,...  8.87 us
  transfers between devices with their start and end apart: 25, of which 19 were waited for; matrix products, arithmetic and copies ran while one was open for 0% of the time, Pallas kernels for 0%

profile of v2, /device:TPU:1, one launch (start us, length us, event | category | flops | bytes accessed | tf_op | source)
XLA Modules:
  0.0 199.4 jit_solution(1892819774144819121)
XLA Ops:
  0.6 8.3 %shard_map.58 = f32[128,128]{1,0:T(8,128)} custom-call(bf16[4,4,2048,128]{3,2,1,0:T(8,128)(2,1)} %high_ref.3, bf16[4,4,2048,128]{3,2,1,0:T(8,128)(2,1)} %high_ref.3), custom_call_target="tpu_custom_call" | custom-call | tf_op jit(solution)/shard_map/pallas_call | solution.py:136
  14.0 2.4 %collective-permute-start.2 = (f32[64,128]{1,0:T(8,128)S(1)}, f32[64,128]{1,0:T(8,128)S(1)}, u32[]{:S(2)}, u32[]{:S(2)}) collective-permute-start(f32[64,128]{1,0:T(8,128)S(1)} %bitcast_add_fusion.2), channel_id=1, source_target_pairs={{0,2},{1,3},{2,0},{3,1},{4,6},{5,7},{6,4},{7,5},{8,10},{9,11},{10,... | collective-permute-start | bytes 98312 | tf_op jit(solution)/shard_map/ppermute | solution.py:26
  18.4 2.1 %collective-permute-done.3 = f32[64,128]{1,0:T(8,128)S(1)} collective-permute-done((f32[64,128]{1,0:T(8,128)S(1)}, f32[64,128]{1,0:T(8,128)S(1)}, u32[]{:S(2)}, u32[]{:S(2)}) %collective-permute-start.3) | collective-permute-done | bytes 32800 | tf_op jit(solution)/shard_map/ppermute | solution.py:26
  21.8 2.6 %collective-permute-start.5 = (f32[64,128]{1,0:T(8,128)S(1)}, f32[64,128]{1,0:T(8,128)S(1)}, u32[]{:S(2)}, u32[]{:S(2)}) collective-permute-start(f32[64,128]{1,0:T(8,128)S(1)} %add_add_fusion.4), channel_id=1, source_target_pairs={{0,16},{4,20},{8,24},{12,28},{16,0},{20,4},{24,8},{28,12},{32,48},... | collective-permute-start | bytes 98312 | tf_op jit(solution)/shard_map/ppermute | solution.py:28
  26.1 2.3 %collective-permute-done.6 = f32[64,128]{1,0:T(8,128)S(1)} collective-permute-done((f32[64,128]{1,0:T(8,128)S(1)}, f32[64,128]{1,0:T(8,128)S(1)}, u32[]{:S(2)}, u32[]{:S(2)}) %collective-permute-start.6) | collective-permute-done | bytes 32800 | tf_op jit(solution)/shard_map/ppermute | solution.py:28
  30.2 3.3 %collective-permute-start.8 = (f32[64,128]{1,0:T(8,128)S(1)}, f32[64,128]{1,0:T(8,128)S(1)}, u32[]{:S(2)}, u32[]{:S(2)}) collective-permute-start(f32[64,128]{1,0:T(8,128)S(1)} %add_add_fusion.3), channel_id=1, source_target_pairs={{0,64},{4,68},{8,72},{12,76},{16,80},{20,84},{24,88},{28,92},{32,9... | collective-permute-start | bytes 98312 | tf_op jit(solution)/shard_map/ppermute | solution.py:28
  35.1 2.3 %collective-permute-done.9 = f32[64,128]{1,0:T(8,128)S(1)} collective-permute-done((f32[64,128]{1,0:T(8,128)S(1)}, f32[64,128]{1,0:T(8,128)S(1)}, u32[]{:S(2)}, u32[]{:S(2)}) %collective-permute-start.9) | collective-permute-done | bytes 32800 | tf_op jit(solution)/shard_map/ppermute | solution.py:28
  37.5 5.6 %collective-permute-start.10 = (f32[64,128]{1,0:T(8,128)S(1)}, f32[64,128]{1,0:T(8,128)S(1)}, u32[]{:S(2)}, u32[]{:S(2)}) collective-permute-start(f32[64,128]{1,0:T(8,128)S(1)} %add_add_fusion.2), channel_id=1, source_target_pairs={{0,4},{4,0},{8,12},{12,8},{16,20},{20,16},{24,28},{28,24},{32,36},... | collective-permute-start | bytes 98312 | tf_op jit(solution)/shard_map/ppermute | solution.py:28
  44.5 17.4 %shard_map.59 = (f32[64,128]{1,0:T(8,128)}, bf16[256,128]{1,0:T(8,128)(2,1)}) custom-call(f32[128,128]{1,0:T(8,128)} %pad_maximum_fusion.1.gram_ref, f32[64,128]{1,0:T(8,128)} %bitcast.46), custom_call_target="tpu_custom_call" | custom-call | tf_op jit(solution)/shard_map/pallas_call | solution.py:160
  62.0 8.9 %shard_map.60 = bf16[128,4,2,16,128]{4,3,2,1,0:T(8,128)(2,1)} custom-call(bf16[4,4,2048,128]{3,2,1,0:T(8,128)(2,1)} %high_ref.3, bf16[4,4,2048,128]{3,2,1,0:T(8,128)(2,1)} %high_ref.3, bf16[256,128]{1,0:T(8,128)(2,1)} %get-tuple-element.10.basis_ref), custom_call_target="tpu_custom_call" | custom-call | tf_op jit(solution)/shard_map/pallas_call | solution.py:183
  70.8 58.3 %all_to_all.5 = bf16[128,4,2,16,128]{4,3,2,1,0:T(8,128)(2,1)} all-to-all(bf16[128,4,2,16,128]{4,3,2,1,0:T(8,128)(2,1)} %shard_map.60), channel_id=1, replica_groups=mesh['blk'=32,'pen'=4] {'blk','pen'}, dimensions={0} | all-to-all | bytes 8388608 | tf_op jit(solution)/shard_map/all_to_all | solution.py:284
  129.1 6.1 %shard_map.61 = (f32[512,512]{1,0:T(8,128)}, bf16[32,512,128]{2,1,0:T(8,128)(2,1)}) custom-call(bf16[512,32,128]{2,1,0:T(8,128)(2,1)} %bitcast.37), custom_call_target="tpu_custom_call" | custom-call | tf_op jit(solution)/shard_map/pallas_call | solution.py:218
  139.7 2.3 %collective-permute-start.13 = (f32[64,512]{1,0:T(8,128)S(1)}, f32[64,512]{1,0:T(8,128)S(1)}, u32[]{:S(2)}, u32[]{:S(2)}) collective-permute-start(f32[64,512]{1,0:T(8,128)S(1)} %get-tuple-element.20), channel_id=1, source_target_pairs={{0,2},{1,3},{2,0},{3,1},{4,6},{5,7},{6,4},{7,5},{8,10},{9,11},{10,... | collective-permute-start | bytes 393224 | tf_op jit(solution)/shard_map/ppermute | solution.py:26
  144.4 3.7 %collective-permute-done.13 = f32[64,512]{1,0:T(8,128)S(1)} collective-permute-done((f32[64,512]{1,0:T(8,128)S(1)}, f32[64,512]{1,0:T(8,128)S(1)}, u32[]{:S(2)}, u32[]{:S(2)}) %collective-permute-start.13) | collective-permute-done | bytes 131104 | tf_op jit(solution)/shard_map/ppermute | solution.py:26
  148.1 2.5 %collective-permute-done.14 = f32[64,512]{1,0:T(8,128)S(1)} collective-permute-done((f32[64,512]{1,0:T(8,128)S(1)}, f32[64,512]{1,0:T(8,128)S(1)}, u32[]{:S(2)}, u32[]{:S(2)}) %collective-permute-start.14) | collective-permute-done | bytes 131104 | tf_op jit(solution)/shard_map/ppermute | solution.py:26
  152.2 2.4 %collective-permute-start.17 = (f32[64,512]{1,0:T(8,128)S(1)}, f32[64,512]{1,0:T(8,128)S(1)}, u32[]{:S(2)}, u32[]{:S(2)}) collective-permute-start(f32[64,512]{1,0:T(8,128)S(1)} %fusion), channel_id=1, source_target_pairs={{0,24},{4,28},{8,16},{12,20},{16,8},{20,12},{24,0},{28,4},{32,56},... | collective-permute-start | bytes 393224 | tf_op jit(solution)/shard_map/ppermute | solution.py:28
  154.6 3.2 %collective-permute-done.16 = f32[64,512]{1,0:T(8,128)S(1)} collective-permute-done((f32[64,512]{1,0:T(8,128)S(1)}, f32[64,512]{1,0:T(8,128)S(1)}, u32[]{:S(2)}, u32[]{:S(2)}) %collective-permute-start.16) | collective-permute-done | bytes 131104 | tf_op jit(solution)/shard_map/ppermute | solution.py:28
  157.9 2.6 %collective-permute-done.17 = f32[64,512]{1,0:T(8,128)S(1)} collective-permute-done((f32[64,512]{1,0:T(8,128)S(1)}, f32[64,512]{1,0:T(8,128)S(1)}, u32[]{:S(2)}, u32[]{:S(2)}) %collective-permute-start.17) | collective-permute-done | bytes 131104 | tf_op jit(solution)/shard_map/ppermute | solution.py:28
  164.4 4.2 %collective-permute-done.19 = f32[64,512]{1,0:T(8,128)S(1)} collective-permute-done((f32[64,512]{1,0:T(8,128)S(1)}, f32[64,512]{1,0:T(8,128)S(1)}, u32[]{:S(2)}, u32[]{:S(2)}) %collective-permute-start.19) | collective-permute-done | bytes 131104 | tf_op jit(solution)/shard_map/ppermute | solution.py:28
  168.6 2.5 %collective-permute-done.20 = f32[64,512]{1,0:T(8,128)S(1)} collective-permute-done((f32[64,512]{1,0:T(8,128)S(1)}, f32[64,512]{1,0:T(8,128)S(1)}, u32[]{:S(2)}, u32[]{:S(2)}) %collective-permute-start.20) | collective-permute-done | bytes 131104 | tf_op jit(solution)/shard_map/ppermute | solution.py:28
  171.2 2.3 %collective-permute-start.22 = (f32[64,512]{1,0:T(8,128)S(1)}, f32[64,512]{1,0:T(8,128)S(1)}, u32[]{:S(2)}, u32[]{:S(2)}) collective-permute-start(f32[64,512]{1,0:T(8,128)S(1)} %get-tuple-element.16), channel_id=1, source_target_pairs={{0,2},{1,3},{2,0},{3,1},{4,6},{5,7},{6,4},{7,5},{8,10},{9,11},{10,... | collective-permute-start | bytes 393224 | tf_op jit(solution)/shard_map/ppermute | solution.py:26
  175.1 3.3 %collective-permute-done.22 = f32[64,512]{1,0:T(8,128)S(1)} collective-permute-done((f32[64,512]{1,0:T(8,128)S(1)}, f32[64,512]{1,0:T(8,128)S(1)}, u32[]{:S(2)}, u32[]{:S(2)}) %collective-permute-start.22) | collective-permute-done | bytes 131104 | tf_op jit(solution)/shard_map/ppermute | solution.py:26
  178.4 2.9 %collective-permute-done.23 = f32[64,512]{1,0:T(8,128)S(1)} collective-permute-done((f32[64,512]{1,0:T(8,128)S(1)}, f32[64,512]{1,0:T(8,128)S(1)}, u32[]{:S(2)}, u32[]{:S(2)}) %collective-permute-start.23) | collective-permute-done | bytes 131104 | tf_op jit(solution)/shard_map/ppermute | solution.py:26
  185.5 13.8 %shard_map.62 = (f32[32,512]{1,0:T(8,128)}, bf16[4,32,1024]{2,1,0:T(8,128)(2,1)}) custom-call(f32[512,512]{1,0:T(8,128)} %pad_maximum_fusion.gram_ref, f32[32,512]{1,0:T(8,128)} %bitcast.45, bf16[32,512,128]{2,1,0:T(8,128)(2,1)} %get-tuple-element.12.groups_ref), custom_call_target="tpu_custom_call" | custom-call | tf_op jit(solution)/shard_map/pallas_call | solution.py:257
  (51 shorter events, 33.3 us)
Async XLA Ops:
  9.7 2.2 %collective-permute-start = (f32[64,128]{1,0:T(8,128)S(1)}, f32[64,128]{1,0:T(8,128)S(1)}, u32[]{:S(2)}, u32[]{:S(2)}) collective-permute-start(f32[64,128]{1,0:T(8,128)S(1)} %dynamic-slice_bitcast_fusion.4), channel_id=1, source_target_pairs={{0,4},{4,0},{8,12},{12,8},{16,20},{20,16},{24,28},{28,24},{32,36},... | collective-permute-start | bytes 98312 | tf_op jit(solution)/shard_map/ppermute | solution.py:28
  12.7 3.9 %collective-permute-start.1 = (f32[64,128]{1,0:T(8,128)S(1)}, f32[64,128]{1,0:T(8,128)S(1)}, u32[]{:S(2)}, u32[]{:S(2)}) collective-permute-start(f32[64,128]{1,0:T(8,128)S(1)} %bitcast_add_fusion.2), channel_id=1, source_target_pairs={{0,1},{1,0},{2,3},{3,2},{4,5},{5,4},{6,7},{7,6},{8,9},{9,8},{10,11... | collective-permute-start | bytes 98312 | tf_op jit(solution)/shard_map/ppermute | solution.py:26
  14.0 4.3 %collective-permute-start.2 = (f32[64,128]{1,0:T(8,128)S(1)}, f32[64,128]{1,0:T(8,128)S(1)}, u32[]{:S(2)}, u32[]{:S(2)}) collective-permute-start(f32[64,128]{1,0:T(8,128)S(1)} %bitcast_add_fusion.2), channel_id=1, source_target_pairs={{0,2},{1,3},{2,0},{3,1},{4,6},{5,7},{6,4},{7,5},{8,10},{9,11},{10,... | collective-permute-start | bytes 98312 | tf_op jit(solution)/shard_map/ppermute | solution.py:26
  16.5 4.0 %collective-permute-start.3 = (f32[64,128]{1,0:T(8,128)S(1)}, f32[64,128]{1,0:T(8,128)S(1)}, u32[]{:S(2)}, u32[]{:S(2)}) collective-permute-start(f32[64,128]{1,0:T(8,128)S(1)} %bitcast_add_fusion.2), channel_id=1, source_target_pairs={{0,3},{1,2},{2,1},{3,0},{4,7},{5,6},{6,5},{7,4},{8,11},{9,10},{10,... | collective-permute-start | bytes 98312 | tf_op jit(solution)/shard_map/ppermute | solution.py:26
  20.5 4.0 %collective-permute-start.4 = (f32[64,128]{1,0:T(8,128)S(1)}, f32[64,128]{1,0:T(8,128)S(1)}, u32[]{:S(2)}, u32[]{:S(2)}) collective-permute-start(f32[64,128]{1,0:T(8,128)S(1)} %add_add_fusion.4), channel_id=1, source_target_pairs={{0,8},{4,12},{8,0},{12,4},{16,24},{20,28},{24,16},{28,20},{32,40},... | collective-permute-start | bytes 98312 | tf_op jit(solution)/shard_map/ppermute | solution.py:28
  21.8 4.3 %collective-permute-start.5 = (f32[64,128]{1,0:T(8,128)S(1)}, f32[64,128]{1,0:T(8,128)S(1)}, u32[]{:S(2)}, u32[]{:S(2)}) collective-permute-start(f32[64,128]{1,0:T(8,128)S(1)} %add_add_fusion.4), channel_id=1, source_target_pairs={{0,16},{4,20},{8,24},{12,28},{16,0},{20,4},{24,8},{28,12},{32,48},... | collective-permute-start | bytes 98312 | tf_op jit(solution)/shard_map/ppermute | solution.py:28
  24.5 4.0 %collective-permute-start.6 = (f32[64,128]{1,0:T(8,128)S(1)}, f32[64,128]{1,0:T(8,128)S(1)}, u32[]{:S(2)}, u32[]{:S(2)}) collective-permute-start(f32[64,128]{1,0:T(8,128)S(1)} %add_add_fusion.4), channel_id=1, source_target_pairs={{0,24},{4,28},{8,16},{12,20},{16,8},{20,12},{24,0},{28,4},{32,56},... | collective-permute-start | bytes 98312 | tf_op jit(solution)/shard_map/ppermute | solution.py:28
  28.5 5.0 %collective-permute-start.7 = (f32[64,128]{1,0:T(8,128)S(1)}, f32[64,128]{1,0:T(8,128)S(1)}, u32[]{:S(2)}, u32[]{:S(2)}) collective-permute-start(f32[64,128]{1,0:T(8,128)S(1)} %add_add_fusion.3), channel_id=1, source_target_pairs={{0,32},{4,36},{8,40},{12,44},{16,48},{20,52},{24,56},{28,60},{32,0... | collective-permute-start | bytes 98312 | tf_op jit(solution)/shard_map/ppermute | solution.py:28
  30.2 5.0 %collective-permute-start.8 = (f32[64,128]{1,0:T(8,128)S(1)}, f32[64,128]{1,0:T(8,128)S(1)}, u32[]{:S(2)}, u32[]{:S(2)}) collective-permute-start(f32[64,128]{1,0:T(8,128)S(1)} %add_add_fusion.3), channel_id=1, source_target_pairs={{0,64},{4,68},{8,72},{12,76},{16,80},{20,84},{24,88},{28,92},{32,9... | collective-permute-start | bytes 98312 | tf_op jit(solution)/shard_map/ppermute | solution.py:28
  33.5 4.0 %collective-permute-start.9 = (f32[64,128]{1,0:T(8,128)S(1)}, f32[64,128]{1,0:T(8,128)S(1)}, u32[]{:S(2)}, u32[]{:S(2)}) collective-permute-start(f32[64,128]{1,0:T(8,128)S(1)} %add_add_fusion.3), channel_id=1, source_target_pairs={{0,96},{4,100},{8,104},{12,108},{16,112},{20,116},{24,120},{28,124... | collective-permute-start | bytes 98312 | tf_op jit(solution)/shard_map/ppermute | solution.py:28
  37.5 6.4 %collective-permute-start.10 = (f32[64,128]{1,0:T(8,128)S(1)}, f32[64,128]{1,0:T(8,128)S(1)}, u32[]{:S(2)}, u32[]{:S(2)}) collective-permute-start(f32[64,128]{1,0:T(8,128)S(1)} %add_add_fusion.2), channel_id=1, source_target_pairs={{0,4},{4,0},{8,12},{12,8},{16,20},{20,16},{24,28},{28,24},{32,36},... | collective-permute-start | bytes 98312 | tf_op jit(solution)/shard_map/ppermute | solution.py:28
  139.6 4.8 %collective-permute-start.12 = (f32[64,512]{1,0:T(8,128)S(1)}, f32[64,512]{1,0:T(8,128)S(1)}, u32[]{:S(2)}, u32[]{:S(2)}) collective-permute-start(f32[64,512]{1,0:T(8,128)S(1)} %get-tuple-element.21), channel_id=1, source_target_pairs={{0,1},{1,0},{2,3},{3,2},{4,5},{5,4},{6,7},{7,6},{8,9},{9,8},{10,11... | collective-permute-start | bytes 393224 | tf_op jit(solution)/shard_map/ppermute | solution.py:26
  139.7 8.4 %collective-permute-start.13 = (f32[64,512]{1,0:T(8,128)S(1)}, f32[64,512]{1,0:T(8,128)S(1)}, u32[]{:S(2)}, u32[]{:S(2)}) collective-permute-start(f32[64,512]{1,0:T(8,128)S(1)} %get-tuple-element.20), channel_id=1, source_target_pairs={{0,2},{1,3},{2,0},{3,1},{4,6},{5,7},{6,4},{7,5},{8,10},{9,11},{10,... | collective-permute-start | bytes 393224 | tf_op jit(solution)/shard_map/ppermute | solution.py:26
  142.0 8.6 %collective-permute-start.14 = (f32[64,512]{1,0:T(8,128)S(1)}, f32[64,512]{1,0:T(8,128)S(1)}, u32[]{:S(2)}, u32[]{:S(2)}) collective-permute-start(f32[64,512]{1,0:T(8,128)S(1)} %get-tuple-element.19), channel_id=1, source_target_pairs={{0,3},{1,2},{2,1},{3,0},{4,7},{5,6},{6,5},{7,4},{8,11},{9,10},{10,... | collective-permute-start | bytes 393224 | tf_op jit(solution)/shard_map/ppermute | solution.py:26
  150.7 3.9 %collective-permute-start.15 = (f32[64,512]{1,0:T(8,128)S(1)}, f32[64,512]{1,0:T(8,128)S(1)}, u32[]{:S(2)}, u32[]{:S(2)}) collective-permute-start(f32[64,512]{1,0:T(8,128)S(1)} %fusion), channel_id=1, source_target_pairs={{0,8},{4,12},{8,0},{12,4},{16,24},{20,28},{24,16},{28,20},{32,40},... | collective-permute-start | bytes 393224 | tf_op jit(solution)/shard_map/ppermute | solution.py:28
  150.8 7.1 %collective-permute-start.16 = (f32[64,512]{1,0:T(8,128)S(1)}, f32[64,512]{1,0:T(8,128)S(1)}, u32[]{:S(2)}, u32[]{:S(2)}) collective-permute-start(f32[64,512]{1,0:T(8,128)S(1)} %fusion), channel_id=1, source_target_pairs={{0,16},{4,20},{8,24},{12,28},{16,0},{20,4},{24,8},{28,12},{32,48},... | collective-permute-start | bytes 393224 | tf_op jit(solution)/shard_map/ppermute | solution.py:28
  152.2 8.2 %collective-permute-start.17 = (f32[64,512]{1,0:T(8,128)S(1)}, f32[64,512]{1,0:T(8,128)S(1)}, u32[]{:S(2)}, u32[]{:S(2)}) collective-permute-start(f32[64,512]{1,0:T(8,128)S(1)} %fusion), channel_id=1, source_target_pairs={{0,24},{4,28},{8,16},{12,20},{16,8},{20,12},{24,0},{28,4},{32,56},... | collective-permute-start | bytes 393224 | tf_op jit(solution)/shard_map/ppermute | solution.py:28
  160.5 3.9 %collective-permute-start.18 = (f32[64,512]{1,0:T(8,128)S(1)}, f32[64,512]{1,0:T(8,128)S(1)}, u32[]{:S(2)}, u32[]{:S(2)}) collective-permute-start(f32[64,512]{1,0:T(8,128)S(1)} %add_add_fusion.1), channel_id=1, source_target_pairs={{0,32},{4,36},{8,40},{12,44},{16,48},{20,52},{24,56},{28,60},{32,0... | collective-permute-start | bytes 393224 | tf_op jit(solution)/shard_map/ppermute | solution.py:28
  161.5 7.1 %collective-permute-start.19 = (f32[64,512]{1,0:T(8,128)S(1)}, f32[64,512]{1,0:T(8,128)S(1)}, u32[]{:S(2)}, u32[]{:S(2)}) collective-permute-start(f32[64,512]{1,0:T(8,128)S(1)} %add_add_fusion.1), channel_id=1, source_target_pairs={{0,64},{4,68},{8,72},{12,76},{16,80},{20,84},{24,88},{28,92},{32,9... | collective-permute-start | bytes 393224 | tf_op jit(solution)/shard_map/ppermute | solution.py:28
  162.4 8.7 %collective-permute-start.20 = (f32[64,512]{1,0:T(8,128)S(1)}, f32[64,512]{1,0:T(8,128)S(1)}, u32[]{:S(2)}, u32[]{:S(2)}) collective-permute-start(f32[64,512]{1,0:T(8,128)S(1)} %add_add_fusion.1), channel_id=1, source_target_pairs={{0,96},{4,100},{8,104},{12,108},{16,112},{20,116},{24,120},{28,124... | collective-permute-start | bytes 393224 | tf_op jit(solution)/shard_map/ppermute | solution.py:28
  171.2 3.9 %collective-permute-start.21 = (f32[64,512]{1,0:T(8,128)S(1)}, f32[64,512]{1,0:T(8,128)S(1)}, u32[]{:S(2)}, u32[]{:S(2)}) collective-permute-start(f32[64,512]{1,0:T(8,128)S(1)} %get-tuple-element.16), channel_id=1, source_target_pairs={{0,1},{1,0},{2,3},{3,2},{4,5},{5,4},{6,7},{7,6},{8,9},{9,8},{10,11... | collective-permute-start | bytes 393224 | tf_op jit(solution)/shard_map/ppermute | solution.py:26
  171.2 7.1 %collective-permute-start.22 = (f32[64,512]{1,0:T(8,128)S(1)}, f32[64,512]{1,0:T(8,128)S(1)}, u32[]{:S(2)}, u32[]{:S(2)}) collective-permute-start(f32[64,512]{1,0:T(8,128)S(1)} %get-tuple-element.16), channel_id=1, source_target_pairs={{0,2},{1,3},{2,0},{3,1},{4,6},{5,7},{6,4},{7,5},{8,10},{9,11},{10,... | collective-permute-start | bytes 393224 | tf_op jit(solution)/shard_map/ppermute | solution.py:26
  173.5 7.7 %collective-permute-start.23 = (f32[64,512]{1,0:T(8,128)S(1)}, f32[64,512]{1,0:T(8,128)S(1)}, u32[]{:S(2)}, u32[]{:S(2)}) collective-permute-start(f32[64,512]{1,0:T(8,128)S(1)} %get-tuple-element.16), channel_id=1, source_target_pairs={{0,3},{1,2},{2,1},{3,0},{4,7},{5,6},{6,5},{7,4},{8,11},{9,10},{10,... | collective-permute-start | bytes 393224 | tf_op jit(solution)/shard_map/ppermute | solution.py:26
  181.3 3.0 %collective-permute-start.24 = (f32[256,512]{1,0:T(8,128)S(1)}, f32[256,512]{1,0:T(8,128)S(1)}, u32[]{:S(2)}, u32[]{:S(2)}) collective-permute-start(f32[256,512]{1,0:T(8,128)S(1)} %bitcast.38), channel_id=1, source_target_pairs={{0,4},{4,0},{8,12},{12,8},{16,20},{20,16},{24,28},{28,24},{32,36},... | collective-permute-start | bytes 1572872 | tf_op jit(solution)/shard_map/ppermute | solution.py:28
  (1 other events, 2.1 us)

commit v3 on v2

v3 whole, which is shorter than its diff:
```python
import jax
import jax.numpy as jnp
from jax import lax
from jax.experimental import pallas as pl
from jax.experimental.pallas import tpu as pltpu
from jax.sharding import PartitionSpec as P

ITT = 3
ITX = 3

F32, BF16 = jnp.float32, jnp.bfloat16
HIGHEST = lax.Precision.HIGHEST
VMEM = pl.BlockSpec(memory_space=pltpu.VMEM)
SMEM = pl.BlockSpec(memory_space=pltpu.SMEM)
HBM = pl.BlockSpec(memory_space=pltpu.HBM)


class Torus:
    def __init__(self):
        self.blk = lax.axis_size("blk")
        self.pen = lax.axis_size("pen")
        index = lax.axis_index("blk")
        self.core = index % 2
        self.place = {"x": lax.axis_index("pen"), "y": (index // 2) % 4, "z": index // 8}

    def swap(self, value, axis, step):
        if axis == "x":
            return lax.ppermute(value, "pen", [(s, s ^ step) for s in range(self.pen)])
        step = {"core": step, "y": step * 2, "z": step * 8}[axis]
        return lax.ppermute(value, "blk", [(s, s ^ step) for s in range(self.blk)])

    def all_sum(self, value, axis):
        near, across, far = [self.swap(value, axis, step) for step in (1, 2, 3)]
        return (value + near) + (across + far)

    def scatter_sum(self, value, axis):
        pieces = value.reshape((4, value.shape[0] // 4) + value.shape[1:])
        place = self.place[axis]
        take = lambda step: lax.dynamic_index_in_dim(pieces, place ^ step, 0, False)
        near, across, far = [self.swap(take(step), axis, step) for step in (1, 2, 3)]
        return (take(0) + near) + (across + far)

    def gather(self, value, axis):
        place = self.place[axis]
        result = jnp.zeros((4,) + value.shape, value.dtype)
        for step in range(4):
            piece = value if step == 0 else self.swap(value, axis, step)
            result = lax.dynamic_update_index_in_dim(result, piece, place ^ step, 0)
        return result.reshape((4 * value.shape[0],) + value.shape[1:])


def limit(mebibytes):
    return pltpu.CompilerParams(vmem_limit_bytes=mebibytes << 20)


def product(a, b, dim_a, dim_b, precision=HIGHEST):
    dims = (((dim_a,), (dim_b,)), ((), ()))
    return lax.dot_general(a, b, dims, precision=precision, preferred_element_type=F32)


def narrow_product(a, b, dim_a, dim_b):
    return product(a, b, dim_a, dim_b, None)


def identity(size):
    shape = (size, size)
    same = lax.broadcasted_iota(jnp.int32, shape, 0) == lax.broadcasted_iota(jnp.int32, shape, 1)
    return jnp.where(same, 1.0, 0.0).astype(F32)


def inverse_factor(square):
    size = square.shape[0]
    width = 2 * size
    wide = jnp.concatenate([square, identity(size)], axis=1)
    rows = [wide[8 * i : 8 * i + 8] for i in range(size // 8)]
    place = lax.broadcasted_iota(jnp.int32, (8, 1), 0)
    for block in range(size // 8):
        held = rows[block]
        splats = [
            jnp.broadcast_to(held[:, 8 * block + j : 8 * block + j + 1], (8, width)) for j in range(8)
        ]
        for j in range(8):
            factor = jnp.where(place > j, splats[j] * (1.0 / splats[j][j : j + 1]), 0.0)
            held = held - factor * held[j : j + 1]
            for m in range(j + 1, 8):
                splats[m] = splats[m] - factor * splats[m][j : j + 1]
        pivots = jnp.concatenate([splats[j][j : j + 1] for j in range(8)], axis=0)
        held = held * lax.rsqrt(pivots)
        rows[block] = held
        for i in range(block + 1, size // 8):
            column = held[:, 8 * i : 8 * i + 8].T
            total = rows[i]
            for j in range(8):
                total = total - column[:, j : j + 1] * held[j : j + 1]
            rows[i] = total
    return jnp.concatenate(rows, axis=0)[:, size:]


def subspace(gram, flat, sweeps):
    for sweep in range(sweeps):
        flat = product(flat, gram, 1, 0)
        for repeat in range(2 if sweep == sweeps - 1 else 1):
            flat = product(inverse_factor(product(flat, flat, 1, 1)), flat, 1, 0)
    return flat


def time_gram(core, snapshots):
    variables, planes, cells, window = snapshots.shape
    pieces = 8
    rows = variables * planes * cells // pieces

    def kernel(core_ref, far_ref, mine_ref, other_ref, near_ref, arrived):
        fetches = []
        for i in range(pieces):
            place = pl.ds(i * rows, rows)
            fetches.append(
                pltpu.make_async_copy(far_ref.at[place], near_ref.at[place], arrived.at[i])
            )
            fetches[-1].start()
        total = None
        for i in range(pieces):
            fetches[i].wait()
            first, second = [
                near_ref[i * rows + j * rows // 2 : i * rows + (j + 1) * rows // 2] for j in range(2)
            ]
            both = jnp.concatenate([first, second], axis=1)
            part = narrow_product(both, both, 0, 0)
            total = part if total is None else total + part
        total = total[:window, :window] + total[window:, window:]
        split_halves(core_ref, total, mine_ref, other_ref)

    half = jax.ShapeDtypeStruct((window // 2, window), F32)
    return pl.pallas_call(
        kernel,
        in_specs=[SMEM, HBM],
        out_specs=[VMEM, VMEM, VMEM],
        out_shape=[half, half, pltpu.VMEM((pieces * rows, window), BF16)],
        scratch_shapes=[pltpu.SemaphoreType.DMA((pieces,))],
        compiler_params=limit(24),
    )(core, pltpu.with_memory_space_constraint(snapshots.reshape(pieces * rows, window), pltpu.HBM))


def split_halves(core_ref, total, mine_ref, other_ref):
    first = core_ref[0] == 0
    rows = total.shape[0] // 2
    mine_ref[...] = jnp.where(first, total[:rows], total[rows:])
    other_ref[...] = jnp.where(first, total[rows:], total[:rows])


def join_halves(core_ref, mine_ref, other_ref, scale):
    first = core_ref[0] == 0
    mine, other = mine_ref[...] * scale, other_ref[...] * scale
    return jnp.concatenate([jnp.where(first, mine, other), jnp.where(first, other, mine)])


def time_subspace(core, mine, other, start, scale):
    rank, window = start.shape

    def kernel(core_ref, mine_ref, other_ref, start_ref, basis_ref, pair_ref):
        gram = join_halves(core_ref, mine_ref, other_ref, scale)
        flat = subspace(gram, start_ref[...], ITT)
        basis_ref[...] = flat
        narrow = flat.T.astype(BF16)
        zero = jnp.zeros_like(narrow)
        pair_ref[:window] = jnp.concatenate([narrow, zero], axis=1)
        pair_ref[window:] = jnp.concatenate([zero, narrow], axis=1)

    return pl.pallas_call(
        kernel,
        in_specs=[SMEM, VMEM, VMEM, VMEM],
        out_specs=[VMEM, VMEM],
        out_shape=[
            jax.ShapeDtypeStruct((rank, window), F32),
            jax.ShapeDtypeStruct((2 * window, 2 * rank), BF16),
        ],
        compiler_params=limit(6),
    )(core, mine, other, start)


def truncate_time(shape, near, pair_basis, owners):
    variables, planes, cells, window = shape
    half = variables // 2
    lanes = pair_basis.shape[1]
    own = cells // owners

    def kernel(near_ref, basis_ref, out_ref):
        basis = basis_ref[...]
        for v in range(half):
            for x in range(planes):
                low, high = [((v + side) * planes + x) * cells for side in (0, half)]
                both = jnp.concatenate(
                    [near_ref[low : low + cells], near_ref[high : high + cells]], axis=1
                )
                core = narrow_product(both, basis, 1, 0).astype(BF16)
                out_ref[:, x, v] = core.reshape(owners, own, lanes)

    return pl.pallas_call(
        kernel,
        in_specs=[VMEM, VMEM],
        out_specs=VMEM,
        out_shape=jax.ShapeDtypeStruct((owners, planes, half, own, lanes), BF16),
        compiler_params=limit(24),
    )(pltpu.with_memory_space_constraint(near, pltpu.VMEM), pair_basis)


def plane_gram(core, pencils):
    planes, groups, lanes = pencils.shape

    def kernel(core_ref, pencil_ref, mine_ref, other_ref, group_ref, held, sent):
        total, sends = None, []
        for i in range(0, groups, 16):
            turned = jnp.swapaxes(pencil_ref[:, i : i + 16], 0, 1)
            place = pl.ds(i, 16)
            held[place] = turned
            sends.append(pltpu.make_async_copy(held.at[place], group_ref.at[place], sent.at[i // 16]))
            sends[-1].start()
            for j in range(0, 16, 2):
                both = jnp.concatenate([turned[j], turned[j + 1]], axis=1)
                part = narrow_product(both, both, 1, 1)
                total = part if total is None else total + part
        split_halves(core_ref, total, mine_ref, other_ref)
        for send in sends:
            send.wait()

    half = jax.ShapeDtypeStruct((planes // 2, planes), F32)
    return pl.pallas_call(
        kernel,
        in_specs=[SMEM, VMEM],
        out_specs=[VMEM, VMEM, HBM],
        out_shape=[half, half, pltpu.HBM((groups, planes, lanes), BF16)],
        scratch_shapes=[
            pltpu.VMEM((groups, planes, lanes), BF16),
            pltpu.SemaphoreType.DMA((groups // 16,)),
        ],
        compiler_params=limit(24),
    )(core, pencils)


def plane_subspace(core, mine, other, start, groups, scale, half):
    rank, planes = start.shape
    count, _, lanes = groups.shape
    own = count // half
    ranks = lanes // 2

    def kernel(core_ref, mine_ref, other_ref, start_ref, far_ref, basis_ref, out_ref, group_ref, arrived):
        fetch = pltpu.make_async_copy(far_ref, group_ref, arrived)
        fetch.start()
        gram = join_halves(core_ref, mine_ref, other_ref, scale)
        flat = subspace(gram, start_ref[...], ITX)
        basis_ref[...] = flat
        narrow = flat.astype(BF16)
        fetch.wait()
        first = lax.broadcasted_iota(jnp.int32, (rank, lanes), 1) < ranks
        for v in range(half):
            for pair in range(own // 2):
                even = narrow_product(narrow, group_ref[v * own + 2 * pair], 1, 0)
                odd = narrow_product(narrow, group_ref[v * own + 2 * pair + 1], 1, 0)
                low = jnp.where(first, even, pltpu.roll(odd, ranks, 1))
                high = jnp.where(first, pltpu.roll(even, ranks, 1), odd)
                place = slice(pair * lanes, (pair + 1) * lanes)
                out_ref[v, :, place] = low.astype(BF16)
                out_ref[v + half, :, place] = high.astype(BF16)

    return pl.pallas_call(
        kernel,
        in_specs=[SMEM, VMEM, VMEM, VMEM, HBM],
        out_specs=[VMEM, VMEM],
        out_shape=[
            jax.ShapeDtypeStruct((rank, planes), F32),
            jax.ShapeDtypeStruct((2 * half, rank, own * ranks), BF16),
        ],
        scratch_shapes=[pltpu.VMEM(groups.shape, BF16), pltpu.SemaphoreType.DMA],
        compiler_params=limit(16),
    )(core, mine, other, start, pltpu.with_memory_space_constraint(groups, pltpu.HBM))


def on_device(snapshots, start_time, start_plane):
    variables, planes, cells, window = snapshots.shape
    devices_all = lax.axis_size("blk") * lax.axis_size("pen")
    half = variables // 2
    rank = start_time.shape[1]
    torus = Torus()
    core = torus.core.reshape(1)

    mine, other, near = time_gram(core, snapshots)
    total = mine + torus.swap(other, "core", 1)
    for axis in "xyz":
        total = torus.all_sum(total, axis)
    scale_time = 1.0 / float(variables * planes * cells * devices_all)
    time_basis, pair_basis = time_subspace(
        core, total, torus.swap(total, "core", 1), start_time.T, scale_time
    )

    core_time = truncate_time(snapshots.shape, near, pair_basis, devices_all)
    pencils = lax.all_to_all(core_time, ("blk", "pen"), split_axis=0, concat_axis=0, tiled=True)
    mine, other, groups = plane_gram(core, pencils.reshape(devices_all * planes, -1, 2 * rank))

    total = mine + torus.swap(other, "core", 1)
    total = torus.scatter_sum(total, "x")
    total = torus.all_sum(total, "y")
    total = torus.all_sum(total, "z")
    total = torus.gather(total, "x")
    scale_plane = 1.0 / float(variables * cells * rank)
    plane_basis, core_tensor = plane_subspace(
        core, total, torus.swap(total, "core", 1), start_plane.T, groups, scale_plane, half
    )
    return (time_basis.T, plane_basis.T, core_tensor)


def solution(mesh):
    return jax.shard_map(
        on_device,
        mesh=mesh,
        in_specs=(P(None, ("blk", "pen"), None, None), P(), P()),
        out_specs=(P(), P(), P(None, None, ("blk", "pen"))),
        check_vma=False,
    )
```

time: 200 us -> 181 us (0.905)
  Pallas kernels: 54.5 us -> 42.1 us
  other arithmetic: 3.86 us -> 0.23 us
    pallas_call x5, Pallas kernels: 54.5 us -> 42.1 us  [the longest x1 16.4 us: time_subspace(): pl.pallas_call(kernel, in_specs=[SMEM, VMEM, VMEM, VMEM], out_specs=[VMEM...]
  transfers between devices with their start and end apart: 25 -> 25, of which waited for: 19 -> 20; matrix products, arithmetic and copies ran while one was open for 0% -> 0% of each run, Pallas kernels for 0% -> 0%
where the time goes in v3:
time: 181 us; the launch traced here: 180 us
  blocking collectives  56.7 us (31%)
  waiting for transfers between devices  42.3 us (23%)
  Pallas kernels  42.1 us (23%)
  starting transfers between devices  38.1 us (21%)
    all_to_all x1, blocking collectives, on_device(): lax.all_to_all(core_time, ('blk', 'pen'), split_axis=0, concat_axis=0, ti...  56.7 us
    ppermute x16, starting transfers between devices, swap(): return lax.ppermute(value, 'blk', [(s, s ^ step) for s in range(self.blk)])  26.4 us
    ppermute x16, waiting for transfers between devices, swap(): return lax.ppermute(value, 'blk', [(s, s ^ step) for s in range(self.blk)])  25.3 us
    ppermute x9, waiting for transfers between devices, swap(): return lax.ppermute(value, 'pen', [(s, s ^ step) for s in range(self.pen)])  17 us
    pallas_call x1, Pallas kernels, time_subspace(): pl.pallas_call(kernel, in_specs=[SMEM, VMEM, VMEM, VMEM], out_specs=[VMEM...  16.4 us
    pallas_call x1, Pallas kernels, plane_subspace(): pl.pallas_call(kernel, in_specs=[SMEM, VMEM, VMEM, VMEM, HBM], out_specs=...  12.6 us
    ppermute x9, starting transfers between devices, swap(): return lax.ppermute(value, 'pen', [(s, s ^ step) for s in range(self.pen)])  11.7 us
    pallas_call x1, Pallas kernels, time_gram(): pl.pallas_call(kernel, in_specs=[SMEM, HBM], out_specs=[VMEM, VMEM, VMEM]...  6.55 us
  transfers between devices with their start and end apart: 25, of which 20 were waited for; matrix products, arithmetic and copies ran while one was open for 0% of the time, Pallas kernels for 0%

profile of v3, /device:TPU:1, one launch (start us, length us, event | category | flops | bytes accessed | tf_op | source)
XLA Modules:
  0.0 180.5 jit_solution(5447860106102535802)
XLA Ops:
  0.7 6.5 %shard_map.58 = (f32[64,128]{1,0:T(8,128)S(1)}, f32[64,128]{1,0:T(8,128)S(1)}, bf16[32768,128]{1,0:T(8,128)(2,1)S(1)}) custom-call(s32[1]{0:T(128)} %bitcast.core_ref, bf16[32768,128]{1,0:T(8,128)(2,1)} %bitcast.32), custom_call_target="tpu_custom_call" | custom-call | tf_op jit(solution)/shard_map/pallas_call | solution.py:133
  10.9 2.5 %collective-permute-start.2 = (f32[64,128]{1,0:T(8,128)S(1)}, f32[64,128]{1,0:T(8,128)S(1)}, u32[]{:S(2)}, u32[]{:S(2)}) collective-permute-start(f32[64,128]{1,0:T(8,128)S(1)} %add.83), channel_id=1, source_target_pairs={{0,2},{1,3},{2,0},{3,1},{4,6},{5,7},{6,4},{7,5},{8,10},{9,11},{10,... | collective-permute-start | bytes 98312 | tf_op jit(solution)/shard_map/ppermute | solution.py:28
  15.2 2.1 %collective-permute-done.3 = f32[64,128]{1,0:T(8,128)S(1)} collective-permute-done((f32[64,128]{1,0:T(8,128)S(1)}, f32[64,128]{1,0:T(8,128)S(1)}, u32[]{:S(2)}, u32[]{:S(2)}) %collective-permute-start.3) | collective-permute-done | bytes 32800 | tf_op jit(solution)/shard_map/ppermute | solution.py:28
  18.7 2.6 %collective-permute-start.5 = (f32[64,128]{1,0:T(8,128)S(1)}, f32[64,128]{1,0:T(8,128)S(1)}, u32[]{:S(2)}, u32[]{:S(2)}) collective-permute-start(f32[64,128]{1,0:T(8,128)S(1)} %add_add_fusion.4), channel_id=1, source_target_pairs={{0,16},{4,20},{8,24},{12,28},{16,0},{20,4},{24,8},{28,12},{32,48},... | collective-permute-start | bytes 98312 | tf_op jit(solution)/shard_map/ppermute | solution.py:30
  22.9 2.3 %collective-permute-done.6 = f32[64,128]{1,0:T(8,128)S(1)} collective-permute-done((f32[64,128]{1,0:T(8,128)S(1)}, f32[64,128]{1,0:T(8,128)S(1)}, u32[]{:S(2)}, u32[]{:S(2)}) %collective-permute-start.6) | collective-permute-done | bytes 32800 | tf_op jit(solution)/shard_map/ppermute | solution.py:30
  27.0 3.3 %collective-permute-start.8 = (f32[64,128]{1,0:T(8,128)S(1)}, f32[64,128]{1,0:T(8,128)S(1)}, u32[]{:S(2)}, u32[]{:S(2)}) collective-permute-start(f32[64,128]{1,0:T(8,128)S(1)} %add_add_fusion.3), channel_id=1, source_target_pairs={{0,64},{4,68},{8,72},{12,76},{16,80},{20,84},{24,88},{28,92},{32,9... | collective-permute-start | bytes 98312 | tf_op jit(solution)/shard_map/ppermute | solution.py:30
  32.0 2.3 %collective-permute-done.9 = f32[64,128]{1,0:T(8,128)S(1)} collective-permute-done((f32[64,128]{1,0:T(8,128)S(1)}, f32[64,128]{1,0:T(8,128)S(1)}, u32[]{:S(2)}, u32[]{:S(2)}) %collective-permute-start.9) | collective-permute-done | bytes 32800 | tf_op jit(solution)/shard_map/ppermute | solution.py:30
  34.3 5.7 %collective-permute-start.10 = (f32[64,128]{1,0:T(8,128)S(1)}, f32[64,128]{1,0:T(8,128)S(1)}, u32[]{:S(2)}, u32[]{:S(2)}) collective-permute-start(f32[64,128]{1,0:T(8,128)S(1)} %add_add_fusion.2.mine_ref), channel_id=1, source_target_pairs={{0,4},{4,0},{8,12},{12,8},{16,20},{20,16},{24,28},{28,24},{32,36},... | collective-permute-start | bytes 98312 | tf_op jit(solution)/shard_map/ppermute | solution.py:30
  40.9 16.4 %shard_map.59 = (f32[64,128]{1,0:T(8,128)}, bf16[256,128]{1,0:T(8,128)(2,1)S(1)}) custom-call(s32[1]{0:T(128)} %bitcast.core_ref, f32[64,128]{1,0:T(8,128)S(1)} %add_add_fusion.2.mine_ref, f32[64,128]{1,0:T(8,128)S(1)} %collective-permute-done.10.other_ref, f32[64,128]{1,0:T(8,128)S(1)} %bitcast.31), custom_call_target="tpu_custom_call" | custom-call | tf_op jit(solution)/shard_map/pallas_call | solution.py:168
  57.3 2.3 %shard_map.60 = bf16[128,4,2,16,128]{4,3,2,1,0:T(8,128)(2,1)S(1)} custom-call(bf16[32768,128]{1,0:T(8,128)(2,1)S(1)} %get-tuple-element.16.near_ref, bf16[256,128]{1,0:T(8,128)(2,1)S(1)} %get-tuple-element.17.basis_ref), custom_call_target="tpu_custom_call" | custom-call | tf_op jit(solution)/shard_map/pallas_call | solution.py:197
  59.7 56.7 %all_to_all.5 = bf16[128,4,2,16,128]{4,3,2,1,0:T(8,128)(2,1)S(1)} all-to-all(bf16[128,4,2,16,128]{4,3,2,1,0:T(8,128)(2,1)S(1)} %shard_map.60), channel_id=1, replica_groups=mesh['blk'=32,'pen'=4] {'blk','pen'}, dimensions={0} | all-to-all | bytes 8388608 | tf_op jit(solution)/shard_map/all_to_all | solution.py:295
  116.3 4.1 %shard_map.61 = (f32[256,512]{1,0:T(8,128)S(1)}, f32[256,512]{1,0:T(8,128)S(1)}, bf16[32,512,128]{2,1,0:T(8,128)(2,1)}) custom-call(s32[1]{0:T(128)} %bitcast.core_ref, bf16[512,32,128]{2,1,0:T(8,128)(2,1)S(1)} %bitcast.27), custom_call_target="tpu_custom_call" | custom-call | tf_op jit(solution)/shard_map/pallas_call | solution.py:226
  122.9 2.3 %collective-permute-start.13 = (f32[64,512]{1,0:T(8,128)S(1)}, f32[64,512]{1,0:T(8,128)S(1)}, u32[]{:S(2)}, u32[]{:S(2)}) collective-permute-start(f32[64,512]{1,0:T(8,128)S(1)} %get-tuple-element.26), channel_id=1, source_target_pairs={{0,2},{1,3},{2,0},{3,1},{4,6},{5,7},{6,4},{7,5},{8,10},{9,11},{10,... | collective-permute-start | bytes 393224 | tf_op jit(solution)/shard_map/ppermute | solution.py:28
  127.5 3.7 %collective-permute-done.13 = f32[64,512]{1,0:T(8,128)S(1)} collective-permute-done((f32[64,512]{1,0:T(8,128)S(1)}, f32[64,512]{1,0:T(8,128)S(1)}, u32[]{:S(2)}, u32[]{:S(2)}) %collective-permute-start.13) | collective-permute-done | bytes 131104 | tf_op jit(solution)/shard_map/ppermute | solution.py:28
  131.2 2.5 %collective-permute-done.14 = f32[64,512]{1,0:T(8,128)S(1)} collective-permute-done((f32[64,512]{1,0:T(8,128)S(1)}, f32[64,512]{1,0:T(8,128)S(1)}, u32[]{:S(2)}, u32[]{:S(2)}) %collective-permute-start.14) | collective-permute-done | bytes 131104 | tf_op jit(solution)/shard_map/ppermute | solution.py:28
  135.5 2.4 %collective-permute-start.17 = (f32[64,512]{1,0:T(8,128)S(1)}, f32[64,512]{1,0:T(8,128)S(1)}, u32[]{:S(2)}, u32[]{:S(2)}) collective-permute-start(f32[64,512]{1,0:T(8,128)S(1)} %fusion), channel_id=1, source_target_pairs={{0,24},{4,28},{8,16},{12,20},{16,8},{20,12},{24,0},{28,4},{32,56},... | collective-permute-start | bytes 393224 | tf_op jit(solution)/shard_map/ppermute | solution.py:30
  137.9 3.3 %collective-permute-done.16 = f32[64,512]{1,0:T(8,128)S(1)} collective-permute-done((f32[64,512]{1,0:T(8,128)S(1)}, f32[64,512]{1,0:T(8,128)S(1)}, u32[]{:S(2)}, u32[]{:S(2)}) %collective-permute-start.16) | collective-permute-done | bytes 131104 | tf_op jit(solution)/shard_map/ppermute | solution.py:30
  141.2 2.6 %collective-permute-done.17 = f32[64,512]{1,0:T(8,128)S(1)} collective-permute-done((f32[64,512]{1,0:T(8,128)S(1)}, f32[64,512]{1,0:T(8,128)S(1)}, u32[]{:S(2)}, u32[]{:S(2)}) %collective-permute-start.17) | collective-permute-done | bytes 131104 | tf_op jit(solution)/shard_map/ppermute | solution.py:30
  147.7 4.3 %collective-permute-done.19 = f32[64,512]{1,0:T(8,128)S(1)} collective-permute-done((f32[64,512]{1,0:T(8,128)S(1)}, f32[64,512]{1,0:T(8,128)S(1)}, u32[]{:S(2)}, u32[]{:S(2)}) %collective-permute-start.19) | collective-permute-done | bytes 131104 | tf_op jit(solution)/shard_map/ppermute | solution.py:30
  152.0 2.5 %collective-permute-done.20 = f32[64,512]{1,0:T(8,128)S(1)} collective-permute-done((f32[64,512]{1,0:T(8,128)S(1)}, f32[64,512]{1,0:T(8,128)S(1)}, u32[]{:S(2)}, u32[]{:S(2)}) %collective-permute-start.20) | collective-permute-done | bytes 131104 | tf_op jit(solution)/shard_map/ppermute | solution.py:30
  154.7 2.2 %collective-permute-start.22 = (f32[64,512]{1,0:T(8,128)S(1)}, f32[64,512]{1,0:T(8,128)S(1)}, u32[]{:S(2)}, u32[]{:S(2)}) collective-permute-start(f32[64,512]{1,0:T(8,128)S(1)} %get-tuple-element.24), channel_id=1, source_target_pairs={{0,2},{1,3},{2,0},{3,1},{4,6},{5,7},{6,4},{7,5},{8,10},{9,11},{10,... | collective-permute-start | bytes 393224 | tf_op jit(solution)/shard_map/ppermute | solution.py:28
  158.8 2.9 %collective-permute-done.22 = f32[64,512]{1,0:T(8,128)S(1)} collective-permute-done((f32[64,512]{1,0:T(8,128)S(1)}, f32[64,512]{1,0:T(8,128)S(1)}, u32[]{:S(2)}, u32[]{:S(2)}) %collective-permute-start.22) | collective-permute-done | bytes 131104 | tf_op jit(solution)/shard_map/ppermute | solution.py:28
  161.8 2.9 %collective-permute-done.23 = f32[64,512]{1,0:T(8,128)S(1)} collective-permute-done((f32[64,512]{1,0:T(8,128)S(1)}, f32[64,512]{1,0:T(8,128)S(1)}, u32[]{:S(2)}, u32[]{:S(2)}) %collective-permute-start.23) | collective-permute-done | bytes 131104 | tf_op jit(solution)/shard_map/ppermute | solution.py:28
  167.7 12.6 %shard_map.62 = (f32[32,512]{1,0:T(8,128)}, bf16[4,32,1024]{2,1,0:T(8,128)(2,1)}) custom-call(s32[1]{0:T(128)} %bitcast.core_ref, f32[256,512]{1,0:T(8,128)S(1)} %bitcast.29, f32[256,512]{1,0:T(8,128)S(1)} %collective-permute-done.24.other_ref, f32[32,512]{1,0:T(8,128)S(1)} %bitcast.30, bf16[32,512,128]{2,1,0:T(8,128)(2,1)} %get-tuple-element.20.far_ref), custom_call_target="tpu_custom_call" | custom-call | tf_op jit(solution)/shard_map/pallas_call | solution.py:264
  (49 shorter events, 28.5 us)
Async XLA Ops:
  7.2 2.3 %collective-permute-start = (f32[64,128]{1,0:T(8,128)S(1)}, f32[64,128]{1,0:T(8,128)S(1)}, u32[]{:S(2)}, u32[]{:S(2)}) collective-permute-start(f32[64,128]{1,0:T(8,128)S(1)} %get-tuple-element.14), channel_id=1, source_target_pairs={{0,4},{4,0},{8,12},{12,8},{16,20},{20,16},{24,28},{28,24},{32,36},... | collective-permute-start | bytes 98312 | tf_op jit(solution)/shard_map/ppermute | solution.py:30
  9.5 3.9 %collective-permute-start.1 = (f32[64,128]{1,0:T(8,128)S(1)}, f32[64,128]{1,0:T(8,128)S(1)}, u32[]{:S(2)}, u32[]{:S(2)}) collective-permute-start(f32[64,128]{1,0:T(8,128)S(1)} %add.83), channel_id=1, source_target_pairs={{0,1},{1,0},{2,3},{3,2},{4,5},{5,4},{6,7},{7,6},{8,9},{9,8},{10,11... | collective-permute-start | bytes 98312 | tf_op jit(solution)/shard_map/ppermute | solution.py:28
  10.9 4.3 %collective-permute-start.2 = (f32[64,128]{1,0:T(8,128)S(1)}, f32[64,128]{1,0:T(8,128)S(1)}, u32[]{:S(2)}, u32[]{:S(2)}) collective-permute-start(f32[64,128]{1,0:T(8,128)S(1)} %add.83), channel_id=1, source_target_pairs={{0,2},{1,3},{2,0},{3,1},{4,6},{5,7},{6,4},{7,5},{8,10},{9,11},{10,... | collective-permute-start | bytes 98312 | tf_op jit(solution)/shard_map/ppermute | solution.py:28
  13.3 4.0 %collective-permute-start.3 = (f32[64,128]{1,0:T(8,128)S(1)}, f32[64,128]{1,0:T(8,128)S(1)}, u32[]{:S(2)}, u32[]{:S(2)}) collective-permute-start(f32[64,128]{1,0:T(8,128)S(1)} %add.83), channel_id=1, source_target_pairs={{0,3},{1,2},{2,1},{3,0},{4,7},{5,6},{6,5},{7,4},{8,11},{9,10},{10,... | collective-permute-start | bytes 98312 | tf_op jit(solution)/shard_map/ppermute | solution.py:28
  17.3 4.0 %collective-permute-start.4 = (f32[64,128]{1,0:T(8,128)S(1)}, f32[64,128]{1,0:T(8,128)S(1)}, u32[]{:S(2)}, u32[]{:S(2)}) collective-permute-start(f32[64,128]{1,0:T(8,128)S(1)} %add_add_fusion.4), channel_id=1, source_target_pairs={{0,8},{4,12},{8,0},{12,4},{16,24},{20,28},{24,16},{28,20},{32,40},... | collective-permute-start | bytes 98312 | tf_op jit(solution)/shard_map/ppermute | solution.py:30
  18.7 4.3 %collective-permute-start.5 = (f32[64,128]{1,0:T(8,128)S(1)}, f32[64,128]{1,0:T(8,128)S(1)}, u32[]{:S(2)}, u32[]{:S(2)}) collective-permute-start(f32[64,128]{1,0:T(8,128)S(1)} %add_add_fusion.4), channel_id=1, source_target_pairs={{0,16},{4,20},{8,24},{12,28},{16,0},{20,4},{24,8},{28,12},{32,48},... | collective-permute-start | bytes 98312 | tf_op jit(solution)/shard_map/ppermute | solution.py:30
  21.3 4.0 %collective-permute-start.6 = (f32[64,128]{1,0:T(8,128)S(1)}, f32[64,128]{1,0:T(8,128)S(1)}, u32[]{:S(2)}, u32[]{:S(2)}) collective-permute-start(f32[64,128]{1,0:T(8,128)S(1)} %add_add_fusion.4), channel_id=1, source_target_pairs={{0,24},{4,28},{8,16},{12,20},{16,8},{20,12},{24,0},{28,4},{32,56},... | collective-permute-start | bytes 98312 | tf_op jit(solution)/shard_map/ppermute | solution.py:30
  25.3 5.0 %collective-permute-start.7 = (f32[64,128]{1,0:T(8,128)S(1)}, f32[64,128]{1,0:T(8,128)S(1)}, u32[]{:S(2)}, u32[]{:S(2)}) collective-permute-start(f32[64,128]{1,0:T(8,128)S(1)} %add_add_fusion.3), channel_id=1, source_target_pairs={{0,32},{4,36},{8,40},{12,44},{16,48},{20,52},{24,56},{28,60},{32,0... | collective-permute-start | bytes 98312 | tf_op jit(solution)/shard_map/ppermute | solution.py:30
  27.0 5.0 %collective-permute-start.8 = (f32[64,128]{1,0:T(8,128)S(1)}, f32[64,128]{1,0:T(8,128)S(1)}, u32[]{:S(2)}, u32[]{:S(2)}) collective-permute-start(f32[64,128]{1,0:T(8,128)S(1)} %add_add_fusion.3), channel_id=1, source_target_pairs={{0,64},{4,68},{8,72},{12,76},{16,80},{20,84},{24,88},{28,92},{32,9... | collective-permute-start | bytes 98312 | tf_op jit(solution)/shard_map/ppermute | solution.py:30
  30.3 4.0 %collective-permute-start.9 = (f32[64,128]{1,0:T(8,128)S(1)}, f32[64,128]{1,0:T(8,128)S(1)}, u32[]{:S(2)}, u32[]{:S(2)}) collective-permute-start(f32[64,128]{1,0:T(8,128)S(1)} %add_add_fusion.3), channel_id=1, source_target_pairs={{0,96},{4,100},{8,104},{12,108},{16,112},{20,116},{24,120},{28,124... | collective-permute-start | bytes 98312 | tf_op jit(solution)/shard_map/ppermute | solution.py:30
  34.3 6.6 %collective-permute-start.10 = (f32[64,128]{1,0:T(8,128)S(1)}, f32[64,128]{1,0:T(8,128)S(1)}, u32[]{:S(2)}, u32[]{:S(2)}) collective-permute-start(f32[64,128]{1,0:T(8,128)S(1)} %add_add_fusion.2.mine_ref), channel_id=1, source_target_pairs={{0,4},{4,0},{8,12},{12,8},{16,20},{20,16},{24,28},{28,24},{32,36},... | collective-permute-start | bytes 98312 | tf_op jit(solution)/shard_map/ppermute | solution.py:30
  122.7 4.8 %collective-permute-start.12 = (f32[64,512]{1,0:T(8,128)S(1)}, f32[64,512]{1,0:T(8,128)S(1)}, u32[]{:S(2)}, u32[]{:S(2)}) collective-permute-start(f32[64,512]{1,0:T(8,128)S(1)} %get-tuple-element.27), channel_id=1, source_target_pairs={{0,1},{1,0},{2,3},{3,2},{4,5},{5,4},{6,7},{7,6},{8,9},{9,8},{10,11... | collective-permute-start | bytes 393224 | tf_op jit(solution)/shard_map/ppermute | solution.py:28
  122.9 8.3 %collective-permute-start.13 = (f32[64,512]{1,0:T(8,128)S(1)}, f32[64,512]{1,0:T(8,128)S(1)}, u32[]{:S(2)}, u32[]{:S(2)}) collective-permute-start(f32[64,512]{1,0:T(8,128)S(1)} %get-tuple-element.26), channel_id=1, source_target_pairs={{0,2},{1,3},{2,0},{3,1},{4,6},{5,7},{6,4},{7,5},{8,10},{9,11},{10,... | collective-permute-start | bytes 393224 | tf_op jit(solution)/shard_map/ppermute | solution.py:28
  125.1 8.6 %collective-permute-start.14 = (f32[64,512]{1,0:T(8,128)S(1)}, f32[64,512]{1,0:T(8,128)S(1)}, u32[]{:S(2)}, u32[]{:S(2)}) collective-permute-start(f32[64,512]{1,0:T(8,128)S(1)} %get-tuple-element.25), channel_id=1, source_target_pairs={{0,3},{1,2},{2,1},{3,0},{4,7},{5,6},{6,5},{7,4},{8,11},{9,10},{10,... | collective-permute-start | bytes 393224 | tf_op jit(solution)/shard_map/ppermute | solution.py:28
  133.8 4.2 %collective-permute-start.15 = (f32[64,512]{1,0:T(8,128)S(1)}, f32[64,512]{1,0:T(8,128)S(1)}, u32[]{:S(2)}, u32[]{:S(2)}) collective-permute-start(f32[64,512]{1,0:T(8,128)S(1)} %fusion), channel_id=1, source_target_pairs={{0,8},{4,12},{8,0},{12,4},{16,24},{20,28},{24,16},{28,20},{32,40},... | collective-permute-start | bytes 393224 | tf_op jit(solution)/shard_map/ppermute | solution.py:30
  134.1 7.1 %collective-permute-start.16 = (f32[64,512]{1,0:T(8,128)S(1)}, f32[64,512]{1,0:T(8,128)S(1)}, u32[]{:S(2)}, u32[]{:S(2)}) collective-permute-start(f32[64,512]{1,0:T(8,128)S(1)} %fusion), channel_id=1, source_target_pairs={{0,16},{4,20},{8,24},{12,28},{16,0},{20,4},{24,8},{28,12},{32,48},... | collective-permute-start | bytes 393224 | tf_op jit(solution)/shard_map/ppermute | solution.py:30
  135.5 8.2 %collective-permute-start.17 = (f32[64,512]{1,0:T(8,128)S(1)}, f32[64,512]{1,0:T(8,128)S(1)}, u32[]{:S(2)}, u32[]{:S(2)}) collective-permute-start(f32[64,512]{1,0:T(8,128)S(1)} %fusion), channel_id=1, source_target_pairs={{0,24},{4,28},{8,16},{12,20},{16,8},{20,12},{24,0},{28,4},{32,56},... | collective-permute-start | bytes 393224 | tf_op jit(solution)/shard_map/ppermute | solution.py:30
  143.8 3.9 %collective-permute-start.18 = (f32[64,512]{1,0:T(8,128)S(1)}, f32[64,512]{1,0:T(8,128)S(1)}, u32[]{:S(2)}, u32[]{:S(2)}) collective-permute-start(f32[64,512]{1,0:T(8,128)S(1)} %add_add_fusion.1), channel_id=1, source_target_pairs={{0,32},{4,36},{8,40},{12,44},{16,48},{20,52},{24,56},{28,60},{32,0... | collective-permute-start | bytes 393224 | tf_op jit(solution)/shard_map/ppermute | solution.py:30
  145.0 7.1 %collective-permute-start.19 = (f32[64,512]{1,0:T(8,128)S(1)}, f32[64,512]{1,0:T(8,128)S(1)}, u32[]{:S(2)}, u32[]{:S(2)}) collective-permute-start(f32[64,512]{1,0:T(8,128)S(1)} %add_add_fusion.1), channel_id=1, source_target_pairs={{0,64},{4,68},{8,72},{12,76},{16,80},{20,84},{24,88},{28,92},{32,9... | collective-permute-start | bytes 393224 | tf_op jit(solution)/shard_map/ppermute | solution.py:30
  145.7 8.8 %collective-permute-start.20 = (f32[64,512]{1,0:T(8,128)S(1)}, f32[64,512]{1,0:T(8,128)S(1)}, u32[]{:S(2)}, u32[]{:S(2)}) collective-permute-start(f32[64,512]{1,0:T(8,128)S(1)} %add_add_fusion.1), channel_id=1, source_target_pairs={{0,96},{4,100},{8,104},{12,108},{16,112},{20,116},{24,120},{28,124... | collective-permute-start | bytes 393224 | tf_op jit(solution)/shard_map/ppermute | solution.py:30
  154.6 4.2 %collective-permute-start.21 = (f32[64,512]{1,0:T(8,128)S(1)}, f32[64,512]{1,0:T(8,128)S(1)}, u32[]{:S(2)}, u32[]{:S(2)}) collective-permute-start(f32[64,512]{1,0:T(8,128)S(1)} %get-tuple-element.24), channel_id=1, source_target_pairs={{0,1},{1,0},{2,3},{3,2},{4,5},{5,4},{6,7},{7,6},{8,9},{9,8},{10,11... | collective-permute-start | bytes 393224 | tf_op jit(solution)/shard_map/ppermute | solution.py:28
  154.7 7.0 %collective-permute-start.22 = (f32[64,512]{1,0:T(8,128)S(1)}, f32[64,512]{1,0:T(8,128)S(1)}, u32[]{:S(2)}, u32[]{:S(2)}) collective-permute-start(f32[64,512]{1,0:T(8,128)S(1)} %get-tuple-element.24), channel_id=1, source_target_pairs={{0,2},{1,3},{2,0},{3,1},{4,6},{5,7},{6,4},{7,5},{8,10},{9,11},{10,... | collective-permute-start | bytes 393224 | tf_op jit(solution)/shard_map/ppermute | solution.py:28
  156.9 7.7 %collective-permute-start.23 = (f32[64,512]{1,0:T(8,128)S(1)}, f32[64,512]{1,0:T(8,128)S(1)}, u32[]{:S(2)}, u32[]{:S(2)}) collective-permute-start(f32[64,512]{1,0:T(8,128)S(1)} %get-tuple-element.24), channel_id=1, source_target_pairs={{0,3},{1,2},{2,1},{3,0},{4,7},{5,6},{6,5},{7,4},{8,11},{9,10},{10,... | collective-permute-start | bytes 393224 | tf_op jit(solution)/shard_map/ppermute | solution.py:28
  164.6 3.0 %collective-permute-start.24 = (f32[256,512]{1,0:T(8,128)S(1)}, f32[256,512]{1,0:T(8,128)S(1)}, u32[]{:S(2)}, u32[]{:S(2)}) collective-permute-start(f32[256,512]{1,0:T(8,128)S(1)} %bitcast.28), channel_id=1, source_target_pairs={{0,4},{4,0},{8,12},{12,8},{16,20},{20,16},{24,28},{28,24},{32,36},... | collective-permute-start | bytes 1572872 | tf_op jit(solution)/shard_map/ppermute | solution.py:30
  (3 other events, 93.7 us)

commit v4 on v3

--- a/solution.py
+++ b/solution.py
@@ -70,29 +70,30 @@
 
 def inverse_factor(square):
     size = square.shape[0]
-    width = 2 * size
+    blocks = size // 8
     wide = jnp.concatenate([square, identity(size)], axis=1)
-    rows = [wide[8 * i : 8 * i + 8] for i in range(size // 8)]
+    rows = [wide[8 * i : 8 * i + 8] for i in range(blocks)]
     place = lax.broadcasted_iota(jnp.int32, (8, 1), 0)
-    for block in range(size // 8):
-        held = rows[block]
-        splats = [
-            jnp.broadcast_to(held[:, 8 * block + j : 8 * block + j + 1], (8, width)) for j in range(8)
-        ]
+    for block in range(blocks):
+        columns = slice(8 * block, 8 * block + 8)
+        splats = {
+            i: [jnp.broadcast_to(rows[i][:, columns][:, j : j + 1], wide[:8].shape) for j in range(8)]
+            for i in range(block, blocks)
+        }
+        pivots = splats[block]
+        done = []
         for j in range(8):
-            factor = jnp.where(place > j, splats[j] * (1.0 / splats[j][j : j + 1]), 0.0)
-            held = held - factor * held[j : j + 1]
-            for m in range(j + 1, 8):
-                splats[m] = splats[m] - factor * splats[m][j : j + 1]
-        pivots = jnp.concatenate([splats[j][j : j + 1] for j in range(8)], axis=0)
-        held = held * lax.rsqrt(pivots)
-        rows[block] = held
-        for i in range(block + 1, size // 8):
-            column = held[:, 8 * i : 8 * i + 8].T
-            total = rows[i]
-            for j in range(8):
-                total = total - column[:, j : j + 1] * held[j : j + 1]
-            rows[i] = total
+            root = lax.rsqrt(pivots[j][j : j + 1])
+            scaled = rows[block][j : j + 1] * root
+            factors = {i: splats[i][j] * root for i in splats}
+            factors[block] = jnp.where(place > j, factors[block], 0.0)
+            pivot_row = {m: pivots[m][j : j + 1] * root for m in range(j + 1, 8)}
+            for i in splats:
+                rows[i] = rows[i] - factors[i] * scaled
+                for m in pivot_row:
+                    splats[i][m] = splats[i][m] - factors[i] * pivot_row[m]
+            done.append(scaled)
+        rows[block] = jnp.concatenate(done, axis=0)
     return jnp.concatenate(rows, axis=0)[:, size:]
 
 

time: 181 us -> 169 us (0.934)
  Pallas kernels: 42.1 us -> 30.3 us
    pallas_call x1, Pallas kernels: 16.4 us -> 9.23 us  [time_subspace(): pl.pallas_call(kernel, in_specs=[SMEM, VMEM, VMEM, VMEM], out_specs=[VMEM...]
    pallas_call x1, Pallas kernels: 12.6 us -> 8.04 us  [plane_subspace(): pl.pallas_call(kernel, in_specs=[SMEM, VMEM, VMEM, VMEM, HBM], out_specs=...]
where the time goes in v4:
time: 169 us; the launch traced here: 168 us
  blocking collectives  56.7 us (34%)
  waiting for transfers between devices  42.3 us (25%)
  starting transfers between devices  37.9 us (22%)
  Pallas kernels  30.3 us (18%)
    all_to_all x1, blocking collectives, on_device(): lax.all_to_all(core_time, ('blk', 'pen'), split_axis=0, concat_axis=0, ti...  56.7 us
    ppermute x16, starting transfers between devices, swap(): return lax.ppermute(value, 'blk', [(s, s ^ step) for s in range(self.blk)])  26.1 us
    ppermute x16, waiting for transfers between devices, swap(): return lax.ppermute(value, 'blk', [(s, s ^ step) for s in range(self.blk)])  25.3 us
    ppermute x9, waiting for transfers between devices, swap(): return lax.ppermute(value, 'pen', [(s, s ^ step) for s in range(self.pen)])  17.1 us
    ppermute x9, starting transfers between devices, swap(): return lax.ppermute(value, 'pen', [(s, s ^ step) for s in range(self.pen)])  11.7 us
    pallas_call x1, Pallas kernels, time_subspace(): pl.pallas_call(kernel, in_specs=[SMEM, VMEM, VMEM, VMEM], out_specs=[VMEM...  9.23 us
    pallas_call x1, Pallas kernels, plane_subspace(): pl.pallas_call(kernel, in_specs=[SMEM, VMEM, VMEM, VMEM, HBM], out_specs=...  8.04 us
    pallas_call x1, Pallas kernels, time_gram(): pl.pallas_call(kernel, in_specs=[SMEM, HBM], out_specs=[VMEM, VMEM, VMEM]...  6.55 us
  transfers between devices with their start and end apart: 25, of which 20 were waited for; matrix products, arithmetic and copies ran while one was open for 0% of the time, Pallas kernels for 0%

profile of v4, /device:TPU:1, one launch (start us, length us, event | category | flops | bytes accessed | tf_op | source)
XLA Modules:
  0.0 168.5 jit_solution(3519785436265611589)
XLA Ops:
  0.7 6.5 %shard_map.58 = (f32[64,128]{1,0:T(8,128)S(1)}, f32[64,128]{1,0:T(8,128)S(1)}, bf16[32768,128]{1,0:T(8,128)(2,1)S(1)}) custom-call(s32[1]{0:T(128)} %bitcast.core_ref, bf16[32768,128]{1,0:T(8,128)(2,1)} %bitcast.32), custom_call_target="tpu_custom_call" | custom-call | tf_op jit(solution)/shard_map/pallas_call | solution.py:134
  10.9 2.5 %collective-permute-start.2 = (f32[64,128]{1,0:T(8,128)S(1)}, f32[64,128]{1,0:T(8,128)S(1)}, u32[]{:S(2)}, u32[]{:S(2)}) collective-permute-start(f32[64,128]{1,0:T(8,128)S(1)} %add.83), channel_id=1, source_target_pairs={{0,2},{1,3},{2,0},{3,1},{4,6},{5,7},{6,4},{7,5},{8,10},{9,11},{10,... | collective-permute-start | bytes 98312 | tf_op jit(solution)/shard_map/ppermute | solution.py:28
  15.2 2.1 %collective-permute-done.3 = f32[64,128]{1,0:T(8,128)S(1)} collective-permute-done((f32[64,128]{1,0:T(8,128)S(1)}, f32[64,128]{1,0:T(8,128)S(1)}, u32[]{:S(2)}, u32[]{:S(2)}) %collective-permute-start.3) | collective-permute-done | bytes 32800 | tf_op jit(solution)/shard_map/ppermute | solution.py:28
  18.7 2.6 %collective-permute-start.5 = (f32[64,128]{1,0:T(8,128)S(1)}, f32[64,128]{1,0:T(8,128)S(1)}, u32[]{:S(2)}, u32[]{:S(2)}) collective-permute-start(f32[64,128]{1,0:T(8,128)S(1)} %add_add_fusion.4), channel_id=1, source_target_pairs={{0,16},{4,20},{8,24},{12,28},{16,0},{20,4},{24,8},{28,12},{32,48},... | collective-permute-start | bytes 98312 | tf_op jit(solution)/shard_map/ppermute | solution.py:30
  22.9 2.3 %collective-permute-done.6 = f32[64,128]{1,0:T(8,128)S(1)} collective-permute-done((f32[64,128]{1,0:T(8,128)S(1)}, f32[64,128]{1,0:T(8,128)S(1)}, u32[]{:S(2)}, u32[]{:S(2)}) %collective-permute-start.6) | collective-permute-done | bytes 32800 | tf_op jit(solution)/shard_map/ppermute | solution.py:30
  27.0 3.3 %collective-permute-start.8 = (f32[64,128]{1,0:T(8,128)S(1)}, f32[64,128]{1,0:T(8,128)S(1)}, u32[]{:S(2)}, u32[]{:S(2)}) collective-permute-start(f32[64,128]{1,0:T(8,128)S(1)} %add_add_fusion.3), channel_id=1, source_target_pairs={{0,64},{4,68},{8,72},{12,76},{16,80},{20,84},{24,88},{28,92},{32,9... | collective-permute-start | bytes 98312 | tf_op jit(solution)/shard_map/ppermute | solution.py:30
  32.0 2.3 %collective-permute-done.9 = f32[64,128]{1,0:T(8,128)S(1)} collective-permute-done((f32[64,128]{1,0:T(8,128)S(1)}, f32[64,128]{1,0:T(8,128)S(1)}, u32[]{:S(2)}, u32[]{:S(2)}) %collective-permute-start.9) | collective-permute-done | bytes 32800 | tf_op jit(solution)/shard_map/ppermute | solution.py:30
  34.3 5.7 %collective-permute-start.10 = (f32[64,128]{1,0:T(8,128)S(1)}, f32[64,128]{1,0:T(8,128)S(1)}, u32[]{:S(2)}, u32[]{:S(2)}) collective-permute-start(f32[64,128]{1,0:T(8,128)S(1)} %add_add_fusion.2.mine_ref), channel_id=1, source_target_pairs={{0,4},{4,0},{8,12},{12,8},{16,20},{20,16},{24,28},{28,24},{32,36},... | collective-permute-start | bytes 98312 | tf_op jit(solution)/shard_map/ppermute | solution.py:30
  40.9 9.2 %shard_map.59 = (f32[64,128]{1,0:T(8,128)}, bf16[256,128]{1,0:T(8,128)(2,1)S(1)}) custom-call(s32[1]{0:T(128)} %bitcast.core_ref, f32[64,128]{1,0:T(8,128)S(1)} %add_add_fusion.2.mine_ref, f32[64,128]{1,0:T(8,128)S(1)} %collective-permute-done.10.other_ref, f32[64,128]{1,0:T(8,128)S(1)} %bitcast.31), custom_call_target="tpu_custom_call" | custom-call | tf_op jit(solution)/shard_map/pallas_call | solution.py:169
  50.1 2.3 %shard_map.60 = bf16[128,4,2,16,128]{4,3,2,1,0:T(8,128)(2,1)S(1)} custom-call(bf16[32768,128]{1,0:T(8,128)(2,1)S(1)} %get-tuple-element.16.near_ref, bf16[256,128]{1,0:T(8,128)(2,1)S(1)} %get-tuple-element.17.basis_ref), custom_call_target="tpu_custom_call" | custom-call | tf_op jit(solution)/shard_map/pallas_call | solution.py:198
  52.5 56.7 %all_to_all.5 = bf16[128,4,2,16,128]{4,3,2,1,0:T(8,128)(2,1)S(1)} all-to-all(bf16[128,4,2,16,128]{4,3,2,1,0:T(8,128)(2,1)S(1)} %shard_map.60), channel_id=1, replica_groups=mesh['blk'=32,'pen'=4] {'blk','pen'}, dimensions={0} | all-to-all | bytes 8388608 | tf_op jit(solution)/shard_map/all_to_all | solution.py:296
  109.1 4.1 %shard_map.61 = (f32[256,512]{1,0:T(8,128)S(1)}, f32[256,512]{1,0:T(8,128)S(1)}, bf16[32,512,128]{2,1,0:T(8,128)(2,1)}) custom-call(s32[1]{0:T(128)} %bitcast.core_ref, bf16[512,32,128]{2,1,0:T(8,128)(2,1)S(1)} %bitcast.27), custom_call_target="tpu_custom_call" | custom-call | tf_op jit(solution)/shard_map/pallas_call | solution.py:227
  115.7 2.3 %collective-permute-start.13 = (f32[64,512]{1,0:T(8,128)S(1)}, f32[64,512]{1,0:T(8,128)S(1)}, u32[]{:S(2)}, u32[]{:S(2)}) collective-permute-start(f32[64,512]{1,0:T(8,128)S(1)} %get-tuple-element.26), channel_id=1, source_target_pairs={{0,2},{1,3},{2,0},{3,1},{4,6},{5,7},{6,4},{7,5},{8,10},{9,11},{10,... | collective-permute-start | bytes 393224 | tf_op jit(solution)/shard_map/ppermute | solution.py:28
  120.3 3.7 %collective-permute-done.13 = f32[64,512]{1,0:T(8,128)S(1)} collective-permute-done((f32[64,512]{1,0:T(8,128)S(1)}, f32[64,512]{1,0:T(8,128)S(1)}, u32[]{:S(2)}, u32[]{:S(2)}) %collective-permute-start.13) | collective-permute-done | bytes 131104 | tf_op jit(solution)/shard_map/ppermute | solution.py:28
  124.0 2.5 %collective-permute-done.14 = f32[64,512]{1,0:T(8,128)S(1)} collective-permute-done((f32[64,512]{1,0:T(8,128)S(1)}, f32[64,512]{1,0:T(8,128)S(1)}, u32[]{:S(2)}, u32[]{:S(2)}) %collective-permute-start.14) | collective-permute-done | bytes 131104 | tf_op jit(solution)/shard_map/ppermute | solution.py:28
  128.1 2.4 %collective-permute-start.17 = (f32[64,512]{1,0:T(8,128)S(1)}, f32[64,512]{1,0:T(8,128)S(1)}, u32[]{:S(2)}, u32[]{:S(2)}) collective-permute-start(f32[64,512]{1,0:T(8,128)S(1)} %fusion), channel_id=1, source_target_pairs={{0,24},{4,28},{8,16},{12,20},{16,8},{20,12},{24,0},{28,4},{32,56},... | collective-permute-start | bytes 393224 | tf_op jit(solution)/shard_map/ppermute | solution.py:30
  130.5 3.2 %collective-permute-done.16 = f32[64,512]{1,0:T(8,128)S(1)} collective-permute-done((f32[64,512]{1,0:T(8,128)S(1)}, f32[64,512]{1,0:T(8,128)S(1)}, u32[]{:S(2)}, u32[]{:S(2)}) %collective-permute-start.16) | collective-permute-done | bytes 131104 | tf_op jit(solution)/shard_map/ppermute | solution.py:30
  133.8 2.5 %collective-permute-done.17 = f32[64,512]{1,0:T(8,128)S(1)} collective-permute-done((f32[64,512]{1,0:T(8,128)S(1)}, f32[64,512]{1,0:T(8,128)S(1)}, u32[]{:S(2)}, u32[]{:S(2)}) %collective-permute-start.17) | collective-permute-done | bytes 131104 | tf_op jit(solution)/shard_map/ppermute | solution.py:30
  140.3 4.3 %collective-permute-done.19 = f32[64,512]{1,0:T(8,128)S(1)} collective-permute-done((f32[64,512]{1,0:T(8,128)S(1)}, f32[64,512]{1,0:T(8,128)S(1)}, u32[]{:S(2)}, u32[]{:S(2)}) %collective-permute-start.19) | collective-permute-done | bytes 131104 | tf_op jit(solution)/shard_map/ppermute | solution.py:30
  144.6 2.5 %collective-permute-done.20 = f32[64,512]{1,0:T(8,128)S(1)} collective-permute-done((f32[64,512]{1,0:T(8,128)S(1)}, f32[64,512]{1,0:T(8,128)S(1)}, u32[]{:S(2)}, u32[]{:S(2)}) %collective-permute-start.20) | collective-permute-done | bytes 131104 | tf_op jit(solution)/shard_map/ppermute | solution.py:30
  147.3 2.2 %collective-permute-start.22 = (f32[64,512]{1,0:T(8,128)S(1)}, f32[64,512]{1,0:T(8,128)S(1)}, u32[]{:S(2)}, u32[]{:S(2)}) collective-permute-start(f32[64,512]{1,0:T(8,128)S(1)} %get-tuple-element.24), channel_id=1, source_target_pairs={{0,2},{1,3},{2,0},{3,1},{4,6},{5,7},{6,4},{7,5},{8,10},{9,11},{10,... | collective-permute-start | bytes 393224 | tf_op jit(solution)/shard_map/ppermute | solution.py:28
  151.4 2.9 %collective-permute-done.22 = f32[64,512]{1,0:T(8,128)S(1)} collective-permute-done((f32[64,512]{1,0:T(8,128)S(1)}, f32[64,512]{1,0:T(8,128)S(1)}, u32[]{:S(2)}, u32[]{:S(2)}) %collective-permute-start.22) | collective-permute-done | bytes 131104 | tf_op jit(solution)/shard_map/ppermute | solution.py:28
  154.3 2.9 %collective-permute-done.23 = f32[64,512]{1,0:T(8,128)S(1)} collective-permute-done((f32[64,512]{1,0:T(8,128)S(1)}, f32[64,512]{1,0:T(8,128)S(1)}, u32[]{:S(2)}, u32[]{:S(2)}) %collective-permute-start.23) | collective-permute-done | bytes 131104 | tf_op jit(solution)/shard_map/ppermute | solution.py:28
  160.3 8.0 %shard_map.62 = (f32[32,512]{1,0:T(8,128)}, bf16[4,32,1024]{2,1,0:T(8,128)(2,1)}) custom-call(s32[1]{0:T(128)} %bitcast.core_ref, f32[256,512]{1,0:T(8,128)S(1)} %bitcast.29, f32[256,512]{1,0:T(8,128)S(1)} %collective-permute-done.24.other_ref, f32[32,512]{1,0:T(8,128)S(1)} %bitcast.30, bf16[32,512,128]{2,1,0:T(8,128)(2,1)} %get-tuple-element.20.far_ref), custom_call_target="tpu_custom_call" | custom-call | tf_op jit(solution)/shard_map/pallas_call | solution.py:265
  (49 shorter events, 28.2 us)
Async XLA Ops:
  7.2 2.3 %collective-permute-start = (f32[64,128]{1,0:T(8,128)S(1)}, f32[64,128]{1,0:T(8,128)S(1)}, u32[]{:S(2)}, u32[]{:S(2)}) collective-permute-start(f32[64,128]{1,0:T(8,128)S(1)} %get-tuple-element.14), channel_id=1, source_target_pairs={{0,4},{4,0},{8,12},{12,8},{16,20},{20,16},{24,28},{28,24},{32,36},... | collective-permute-start | bytes 98312 | tf_op jit(solution)/shard_map/ppermute | solution.py:30
  9.5 3.9 %collective-permute-start.1 = (f32[64,128]{1,0:T(8,128)S(1)}, f32[64,128]{1,0:T(8,128)S(1)}, u32[]{:S(2)}, u32[]{:S(2)}) collective-permute-start(f32[64,128]{1,0:T(8,128)S(1)} %add.83), channel_id=1, source_target_pairs={{0,1},{1,0},{2,3},{3,2},{4,5},{5,4},{6,7},{7,6},{8,9},{9,8},{10,11... | collective-permute-start | bytes 98312 | tf_op jit(solution)/shard_map/ppermute | solution.py:28
  10.9 4.3 %collective-permute-start.2 = (f32[64,128]{1,0:T(8,128)S(1)}, f32[64,128]{1,0:T(8,128)S(1)}, u32[]{:S(2)}, u32[]{:S(2)}) collective-permute-start(f32[64,128]{1,0:T(8,128)S(1)} %add.83), channel_id=1, source_target_pairs={{0,2},{1,3},{2,0},{3,1},{4,6},{5,7},{6,4},{7,5},{8,10},{9,11},{10,... | collective-permute-start | bytes 98312 | tf_op jit(solution)/shard_map/ppermute | solution.py:28
  13.3 4.0 %collective-permute-start.3 = (f32[64,128]{1,0:T(8,128)S(1)}, f32[64,128]{1,0:T(8,128)S(1)}, u32[]{:S(2)}, u32[]{:S(2)}) collective-permute-start(f32[64,128]{1,0:T(8,128)S(1)} %add.83), channel_id=1, source_target_pairs={{0,3},{1,2},{2,1},{3,0},{4,7},{5,6},{6,5},{7,4},{8,11},{9,10},{10,... | collective-permute-start | bytes 98312 | tf_op jit(solution)/shard_map/ppermute | solution.py:28
  17.3 4.0 %collective-permute-start.4 = (f32[64,128]{1,0:T(8,128)S(1)}, f32[64,128]{1,0:T(8,128)S(1)}, u32[]{:S(2)}, u32[]{:S(2)}) collective-permute-start(f32[64,128]{1,0:T(8,128)S(1)} %add_add_fusion.4), channel_id=1, source_target_pairs={{0,8},{4,12},{8,0},{12,4},{16,24},{20,28},{24,16},{28,20},{32,40},... | collective-permute-start | bytes 98312 | tf_op jit(solution)/shard_map/ppermute | solution.py:30
  18.7 4.3 %collective-permute-start.5 = (f32[64,128]{1,0:T(8,128)S(1)}, f32[64,128]{1,0:T(8,128)S(1)}, u32[]{:S(2)}, u32[]{:S(2)}) collective-permute-start(f32[64,128]{1,0:T(8,128)S(1)} %add_add_fusion.4), channel_id=1, source_target_pairs={{0,16},{4,20},{8,24},{12,28},{16,0},{20,4},{24,8},{28,12},{32,48},... | collective-permute-start | bytes 98312 | tf_op jit(solution)/shard_map/ppermute | solution.py:30
  21.3 4.0 %collective-permute-start.6 = (f32[64,128]{1,0:T(8,128)S(1)}, f32[64,128]{1,0:T(8,128)S(1)}, u32[]{:S(2)}, u32[]{:S(2)}) collective-permute-start(f32[64,128]{1,0:T(8,128)S(1)} %add_add_fusion.4), channel_id=1, source_target_pairs={{0,24},{4,28},{8,16},{12,20},{16,8},{20,12},{24,0},{28,4},{32,56},... | collective-permute-start | bytes 98312 | tf_op jit(solution)/shard_map/ppermute | solution.py:30
  25.3 5.0 %collective-permute-start.7 = (f32[64,128]{1,0:T(8,128)S(1)}, f32[64,128]{1,0:T(8,128)S(1)}, u32[]{:S(2)}, u32[]{:S(2)}) collective-permute-start(f32[64,128]{1,0:T(8,128)S(1)} %add_add_fusion.3), channel_id=1, source_target_pairs={{0,32},{4,36},{8,40},{12,44},{16,48},{20,52},{24,56},{28,60},{32,0... | collective-permute-start | bytes 98312 | tf_op jit(solution)/shard_map/ppermute | solution.py:30
  27.0 5.0 %collective-permute-start.8 = (f32[64,128]{1,0:T(8,128)S(1)}, f32[64,128]{1,0:T(8,128)S(1)}, u32[]{:S(2)}, u32[]{:S(2)}) collective-permute-start(f32[64,128]{1,0:T(8,128)S(1)} %add_add_fusion.3), channel_id=1, source_target_pairs={{0,64},{4,68},{8,72},{12,76},{16,80},{20,84},{24,88},{28,92},{32,9... | collective-permute-start | bytes 98312 | tf_op jit(solution)/shard_map/ppermute | solution.py:30
  30.3 4.0 %collective-permute-start.9 = (f32[64,128]{1,0:T(8,128)S(1)}, f32[64,128]{1,0:T(8,128)S(1)}, u32[]{:S(2)}, u32[]{:S(2)}) collective-permute-start(f32[64,128]{1,0:T(8,128)S(1)} %add_add_fusion.3), channel_id=1, source_target_pairs={{0,96},{4,100},{8,104},{12,108},{16,112},{20,116},{24,120},{28,124... | collective-permute-start | bytes 98312 | tf_op jit(solution)/shard_map/ppermute | solution.py:30
  34.3 6.6 %collective-permute-start.10 = (f32[64,128]{1,0:T(8,128)S(1)}, f32[64,128]{1,0:T(8,128)S(1)}, u32[]{:S(2)}, u32[]{:S(2)}) collective-permute-start(f32[64,128]{1,0:T(8,128)S(1)} %add_add_fusion.2.mine_ref), channel_id=1, source_target_pairs={{0,4},{4,0},{8,12},{12,8},{16,20},{20,16},{24,28},{28,24},{32,36},... | collective-permute-start | bytes 98312 | tf_op jit(solution)/shard_map/ppermute | solution.py:30
  115.5 4.8 %collective-permute-start.12 = (f32[64,512]{1,0:T(8,128)S(1)}, f32[64,512]{1,0:T(8,128)S(1)}, u32[]{:S(2)}, u32[]{:S(2)}) collective-permute-start(f32[64,512]{1,0:T(8,128)S(1)} %get-tuple-element.27), channel_id=1, source_target_pairs={{0,1},{1,0},{2,3},{3,2},{4,5},{5,4},{6,7},{7,6},{8,9},{9,8},{10,11... | collective-permute-start | bytes 393224 | tf_op jit(solution)/shard_map/ppermute | solution.py:28
  115.7 8.4 %collective-permute-start.13 = (f32[64,512]{1,0:T(8,128)S(1)}, f32[64,512]{1,0:T(8,128)S(1)}, u32[]{:S(2)}, u32[]{:S(2)}) collective-permute-start(f32[64,512]{1,0:T(8,128)S(1)} %get-tuple-element.26), channel_id=1, source_target_pairs={{0,2},{1,3},{2,0},{3,1},{4,6},{5,7},{6,4},{7,5},{8,10},{9,11},{10,... | collective-permute-start | bytes 393224 | tf_op jit(solution)/shard_map/ppermute | solution.py:28
  117.9 8.6 %collective-permute-start.14 = (f32[64,512]{1,0:T(8,128)S(1)}, f32[64,512]{1,0:T(8,128)S(1)}, u32[]{:S(2)}, u32[]{:S(2)}) collective-permute-start(f32[64,512]{1,0:T(8,128)S(1)} %get-tuple-element.25), channel_id=1, source_target_pairs={{0,3},{1,2},{2,1},{3,0},{4,7},{5,6},{6,5},{7,4},{8,11},{9,10},{10,... | collective-permute-start | bytes 393224 | tf_op jit(solution)/shard_map/ppermute | solution.py:28
  126.6 3.9 %collective-permute-start.15 = (f32[64,512]{1,0:T(8,128)S(1)}, f32[64,512]{1,0:T(8,128)S(1)}, u32[]{:S(2)}, u32[]{:S(2)}) collective-permute-start(f32[64,512]{1,0:T(8,128)S(1)} %fusion), channel_id=1, source_target_pairs={{0,8},{4,12},{8,0},{12,4},{16,24},{20,28},{24,16},{28,20},{32,40},... | collective-permute-start | bytes 393224 | tf_op jit(solution)/shard_map/ppermute | solution.py:30
  126.7 7.1 %collective-permute-start.16 = (f32[64,512]{1,0:T(8,128)S(1)}, f32[64,512]{1,0:T(8,128)S(1)}, u32[]{:S(2)}, u32[]{:S(2)}) collective-permute-start(f32[64,512]{1,0:T(8,128)S(1)} %fusion), channel_id=1, source_target_pairs={{0,16},{4,20},{8,24},{12,28},{16,0},{20,4},{24,8},{28,12},{32,48},... | collective-permute-start | bytes 393224 | tf_op jit(solution)/shard_map/ppermute | solution.py:30
  128.1 8.2 %collective-permute-start.17 = (f32[64,512]{1,0:T(8,128)S(1)}, f32[64,512]{1,0:T(8,128)S(1)}, u32[]{:S(2)}, u32[]{:S(2)}) collective-permute-start(f32[64,512]{1,0:T(8,128)S(1)} %fusion), channel_id=1, source_target_pairs={{0,24},{4,28},{8,16},{12,20},{16,8},{20,12},{24,0},{28,4},{32,56},... | collective-permute-start | bytes 393224 | tf_op jit(solution)/shard_map/ppermute | solution.py:30
  136.4 3.9 %collective-permute-start.18 = (f32[64,512]{1,0:T(8,128)S(1)}, f32[64,512]{1,0:T(8,128)S(1)}, u32[]{:S(2)}, u32[]{:S(2)}) collective-permute-start(f32[64,512]{1,0:T(8,128)S(1)} %add_add_fusion.1), channel_id=1, source_target_pairs={{0,32},{4,36},{8,40},{12,44},{16,48},{20,52},{24,56},{28,60},{32,0... | collective-permute-start | bytes 393224 | tf_op jit(solution)/shard_map/ppermute | solution.py:30
  137.5 7.1 %collective-permute-start.19 = (f32[64,512]{1,0:T(8,128)S(1)}, f32[64,512]{1,0:T(8,128)S(1)}, u32[]{:S(2)}, u32[]{:S(2)}) collective-permute-start(f32[64,512]{1,0:T(8,128)S(1)} %add_add_fusion.1), channel_id=1, source_target_pairs={{0,64},{4,68},{8,72},{12,76},{16,80},{20,84},{24,88},{28,92},{32,9... | collective-permute-start | bytes 393224 | tf_op jit(solution)/shard_map/ppermute | solution.py:30
  138.3 8.8 %collective-permute-start.20 = (f32[64,512]{1,0:T(8,128)S(1)}, f32[64,512]{1,0:T(8,128)S(1)}, u32[]{:S(2)}, u32[]{:S(2)}) collective-permute-start(f32[64,512]{1,0:T(8,128)S(1)} %add_add_fusion.1), channel_id=1, source_target_pairs={{0,96},{4,100},{8,104},{12,108},{16,112},{20,116},{24,120},{28,124... | collective-permute-start | bytes 393224 | tf_op jit(solution)/shard_map/ppermute | solution.py:30
  147.2 4.2 %collective-permute-start.21 = (f32[64,512]{1,0:T(8,128)S(1)}, f32[64,512]{1,0:T(8,128)S(1)}, u32[]{:S(2)}, u32[]{:S(2)}) collective-permute-start(f32[64,512]{1,0:T(8,128)S(1)} %get-tuple-element.24), channel_id=1, source_target_pairs={{0,1},{1,0},{2,3},{3,2},{4,5},{5,4},{6,7},{7,6},{8,9},{9,8},{10,11... | collective-permute-start | bytes 393224 | tf_op jit(solution)/shard_map/ppermute | solution.py:28
  147.3 7.1 %collective-permute-start.22 = (f32[64,512]{1,0:T(8,128)S(1)}, f32[64,512]{1,0:T(8,128)S(1)}, u32[]{:S(2)}, u32[]{:S(2)}) collective-permute-start(f32[64,512]{1,0:T(8,128)S(1)} %get-tuple-element.24), channel_id=1, source_target_pairs={{0,2},{1,3},{2,0},{3,1},{4,6},{5,7},{6,4},{7,5},{8,10},{9,11},{10,... | collective-permute-start | bytes 393224 | tf_op jit(solution)/shard_map/ppermute | solution.py:28
  149.5 7.7 %collective-permute-start.23 = (f32[64,512]{1,0:T(8,128)S(1)}, f32[64,512]{1,0:T(8,128)S(1)}, u32[]{:S(2)}, u32[]{:S(2)}) collective-permute-start(f32[64,512]{1,0:T(8,128)S(1)} %get-tuple-element.24), channel_id=1, source_target_pairs={{0,3},{1,2},{2,1},{3,0},{4,7},{5,6},{6,5},{7,4},{8,11},{9,10},{10,... | collective-permute-start | bytes 393224 | tf_op jit(solution)/shard_map/ppermute | solution.py:28
  157.2 3.0 %collective-permute-start.24 = (f32[256,512]{1,0:T(8,128)S(1)}, f32[256,512]{1,0:T(8,128)S(1)}, u32[]{:S(2)}, u32[]{:S(2)}) collective-permute-start(f32[256,512]{1,0:T(8,128)S(1)} %bitcast.28), channel_id=1, source_target_pairs={{0,4},{4,0},{8,12},{12,8},{16,20},{20,16},{24,28},{28,24},{32,36},... | collective-permute-start | bytes 1572872 | tf_op jit(solution)/shard_map/ppermute | solution.py:30
  (3 other events, 93.5 us)

commit v5 on v4

--- a/solution.py
+++ b/solution.py
@@ -16,6 +16,9 @@
 
 
 class Torus:
+    orders = ("xyz", "yzx")
+    steps = (2, 3, 1)
+
     def __init__(self):
         self.blk = lax.axis_size("blk")
         self.pen = lax.axis_size("pen")
@@ -23,28 +26,42 @@
         self.core = index % 2
         self.place = {"x": lax.axis_index("pen"), "y": (index // 2) % 4, "z": index // 8}
 
-    def swap(self, value, axis, step):
-        if axis == "x":
-            return lax.ppermute(value, "pen", [(s, s ^ step) for s in range(self.pen)])
-        step = {"core": step, "y": step * 2, "z": step * 8}[axis]
-        return lax.ppermute(value, "blk", [(s, s ^ step) for s in range(self.blk)])
-
-    def all_sum(self, value, axis):
-        near, across, far = [self.swap(value, axis, step) for step in (1, 2, 3)]
-        return (value + near) + (across + far)
-
-    def scatter_sum(self, value, axis):
+    def partners(self, stage, step):
+        pairs = []
+        for blk in range(self.blk):
+            axis = "core" if stage is None else self.orders[blk % 2][stage]
+            for pen in range(self.pen):
+                to_pen = pen ^ step if axis == "x" else pen
+                to_blk = blk ^ (step * {"core": 1, "x": 0, "y": 2, "z": 8}[axis])
+                pairs.append((blk * self.pen + pen, to_blk * self.pen + to_pen))
+        return pairs
+
+    def swap(self, value, stage, step):
+        return lax.ppermute(value, ("blk", "pen"), self.partners(stage, step))
+
+    def swap_cores(self, value):
+        return self.swap(value, None, 1)
+
+    def stage_place(self, stage):
+        first, second = [self.place[order[stage]] for order in self.orders]
+        return jnp.where(self.core == 0, first, second)
+
+    def all_sum(self, value, stage):
+        got = {step: self.swap(value, stage, step) for step in self.steps}
+        return (value + got[1]) + (got[2] + got[3])
+
+    def scatter_sum(self, value, stage):
         pieces = value.reshape((4, value.shape[0] // 4) + value.shape[1:])
-        place = self.place[axis]
+        place = self.stage_place(stage)
         take = lambda step: lax.dynamic_index_in_dim(pieces, place ^ step, 0, False)
-        near, across, far = [self.swap(take(step), axis, step) for step in (1, 2, 3)]
-        return (take(0) + near) + (across + far)
-
-    def gather(self, value, axis):
-        place = self.place[axis]
+        got = {step: self.swap(take(step), stage, step) for step in self.steps}
+        return (take(0) + got[1]) + (got[2] + got[3])
+
+    def gather(self, value, stage):
+        place = self.stage_place(stage)
         result = jnp.zeros((4,) + value.shape, value.dtype)
-        for step in range(4):
-            piece = value if step == 0 else self.swap(value, axis, step)
+        for step in (0,) + self.steps:
+            piece = value if step == 0 else self.swap(value, stage, step)
             result = lax.dynamic_update_index_in_dim(result, piece, place ^ step, 0)
         return result.reshape((4 * value.shape[0],) + value.shape[1:])
 
@@ -284,26 +301,26 @@
     core = torus.core.reshape(1)
 
     mine, other, near = time_gram(core, snapshots)
-    total = mine + torus.swap(other, "core", 1)
-    for axis in "xyz":
-        total = torus.all_sum(total, axis)
+    total = mine + torus.swap_cores(other)
+    for stage in range(3):
+        total = torus.all_sum(total, stage)
     scale_time = 1.0 / float(variables * planes * cells * devices_all)
     time_basis, pair_basis = time_subspace(
-        core, total, torus.swap(total, "core", 1), start_time.T, scale_time
+        core, total, torus.swap_cores(total), start_time.T, scale_time
     )
 
     core_time = truncate_time(snapshots.shape, near, pair_basis, devices_all)
     pencils = lax.all_to_all(core_time, ("blk", "pen"), split_axis=0, concat_axis=0, tiled=True)
     mine, other, groups = plane_gram(core, pencils.reshape(devices_all * planes, -1, 2 * rank))
 
-    total = mine + torus.swap(other, "core", 1)
-    total = torus.scatter_sum(total, "x")
-    total = torus.all_sum(total, "y")
-    total = torus.all_sum(total, "z")
-    total = torus.gather(total, "x")
+    total = mine + torus.swap_cores(other)
+    total = torus.scatter_sum(total, 0)
+    for stage in (1, 2):
+        total = torus.all_sum(total, stage)
+    total = torus.gather(total, 0)
     scale_plane = 1.0 / float(variables * cells * rank)
     plane_basis, core_tensor = plane_subspace(
-        core, total, torus.swap(total, "core", 1), start_plane.T, groups, scale_plane, half
+        core, total, torus.swap_cores(total), start_plane.T, groups, scale_plane, half
     )
     return (time_basis.T, plane_basis.T, core_tensor)
 

time: 169 us -> 160 us (0.947)
  waiting for transfers between devices: 42.3 us -> 30.9 us
  starting transfers between devices: 37.9 us -> 40.9 us
    ppermute x25, waiting for transfers between devices: 42.3 us -> 30.9 us  [swap(): return lax.ppermute(value, ('blk', 'pen'), self.partners(stage, step))]
    ppermute x25, starting transfers between devices: 37.9 us -> 40.9 us  [swap(): return lax.ppermute(value, ('blk', 'pen'), self.partners(stage, step))]
  transfers between devices with their start and end apart: 25 -> 25, of which waited for: 20 -> 19; matrix products, arithmetic and copies ran while one was open for 0% -> 0% of each run, Pallas kernels for 0% -> 0%
where the time goes in v5:
time: 160 us
  blocking collectives  56.7 us (35%)
  starting transfers between devices  40.9 us (26%)
  waiting for transfers between devices  30.9 us (19%)
  Pallas kernels  30.3 us (19%)
    all_to_all x1, blocking collectives, on_device(): lax.all_to_all(core_time, ('blk', 'pen'), split_axis=0, concat_axis=0, ti...  56.7 us
    ppermute x25, starting transfers between devices, swap(): return lax.ppermute(value, ('blk', 'pen'), self.partners(stage, step))  40.9 us
    ppermute x25, waiting for transfers between devices, swap(): return lax.ppermute(value, ('blk', 'pen'), self.partners(stage, step))  30.9 us
    pallas_call x1, Pallas kernels, time_subspace(): pl.pallas_call(kernel, in_specs=[SMEM, VMEM, VMEM, VMEM], out_specs=[VMEM...  9.23 us
    pallas_call x1, Pallas kernels, plane_subspace(): pl.pallas_call(kernel, in_specs=[SMEM, VMEM, VMEM, VMEM, HBM], out_specs=...  8.04 us
    pallas_call x1, Pallas kernels, time_gram(): pl.pallas_call(kernel, in_specs=[SMEM, HBM], out_specs=[VMEM, VMEM, VMEM]...  6.55 us
    pallas_call x1, Pallas kernels, plane_gram(): pl.pallas_call(kernel, in_specs=[SMEM, VMEM], out_specs=[VMEM, VMEM, HBM]...  4.13 us
  transfers between devices with their start and end apart: 25, of which 19 were waited for; matrix products, arithmetic and copies ran while one was open for 0% of the time, Pallas kernels for 0%

profile of v5, /device:TPU:1, one launch (start us, length us, event | category | flops | bytes accessed | tf_op | source)
XLA Modules:
  0.0 160.1 jit_solution(14362934374183996006)
XLA Ops:
  0.7 6.5 %shard_map.58 = (f32[64,128]{1,0:T(8,128)S(1)}, f32[64,128]{1,0:T(8,128)S(1)}, bf16[32768,128]{1,0:T(8,128)(2,1)S(1)}) custom-call(s32[1]{0:T(128)} %bitcast.core_ref, bf16[32768,128]{1,0:T(8,128)(2,1)} %bitcast.32), custom_call_target="tpu_custom_call" | custom-call | tf_op jit(solution)/shard_map/pallas_call | solution.py:151
  10.9 2.6 %collective-permute-start.2 = (f32[64,128]{1,0:T(8,128)S(1)}, f32[64,128]{1,0:T(8,128)S(1)}, u32[]{:S(2)}, u32[]{:S(2)}) collective-permute-start(f32[64,128]{1,0:T(8,128)S(1)} %add.87), channel_id=1, source_target_pairs={{0,2},{1,3},{2,0},{3,1},{4,20},{5,21},{6,22},{7,23},{8,10},{9,11},... | collective-permute-start | bytes 98312 | tf_op jit(solution)/shard_map/ppermute | solution.py:40
  15.2 2.3 %collective-permute-done.3 = f32[64,128]{1,0:T(8,128)S(1)} collective-permute-done((f32[64,128]{1,0:T(8,128)S(1)}, f32[64,128]{1,0:T(8,128)S(1)}, u32[]{:S(2)}, u32[]{:S(2)}) %collective-permute-start.3) | collective-permute-done | bytes 32800 | tf_op jit(solution)/shard_map/ppermute | solution.py:40
  17.6 1.7 %collective-permute-start.4 = (f32[64,128]{1,0:T(8,128)S(1)}, f32[64,128]{1,0:T(8,128)S(1)}, u32[]{:S(2)}, u32[]{:S(2)}) collective-permute-start(f32[64,128]{1,0:T(8,128)S(1)} %add_add_fusion.4), channel_id=1, source_target_pairs={{0,8},{1,9},{2,10},{3,11},{4,36},{5,37},{6,38},{7,39},{8,0},{9,1},... | collective-permute-start | bytes 98312 | tf_op jit(solution)/shard_map/ppermute | solution.py:40
  19.3 3.3 %collective-permute-start.5 = (f32[64,128]{1,0:T(8,128)S(1)}, f32[64,128]{1,0:T(8,128)S(1)}, u32[]{:S(2)}, u32[]{:S(2)}) collective-permute-start(f32[64,128]{1,0:T(8,128)S(1)} %add_add_fusion.4), channel_id=1, source_target_pairs={{0,16},{1,17},{2,18},{3,19},{4,68},{5,69},{6,70},{7,71},{8,24},{9,... | collective-permute-start | bytes 98312 | tf_op jit(solution)/shard_map/ppermute | solution.py:40
  24.2 2.3 %collective-permute-done.6 = f32[64,128]{1,0:T(8,128)S(1)} collective-permute-done((f32[64,128]{1,0:T(8,128)S(1)}, f32[64,128]{1,0:T(8,128)S(1)}, u32[]{:S(2)}, u32[]{:S(2)}) %collective-permute-start.6) | collective-permute-done | bytes 32800 | tf_op jit(solution)/shard_map/ppermute | solution.py:40
  27.9 2.5 %collective-permute-start.8 = (f32[64,128]{1,0:T(8,128)S(1)}, f32[64,128]{1,0:T(8,128)S(1)}, u32[]{:S(2)}, u32[]{:S(2)}) collective-permute-start(f32[64,128]{1,0:T(8,128)S(1)} %add_add_fusion.3), channel_id=1, source_target_pairs={{0,64},{1,65},{2,66},{3,67},{4,6},{5,7},{6,4},{7,5},{8,72},{9,73},... | collective-permute-start | bytes 98312 | tf_op jit(solution)/shard_map/ppermute | solution.py:40
  32.1 2.2 %collective-permute-done.9 = f32[64,128]{1,0:T(8,128)S(1)} collective-permute-done((f32[64,128]{1,0:T(8,128)S(1)}, f32[64,128]{1,0:T(8,128)S(1)}, u32[]{:S(2)}, u32[]{:S(2)}) %collective-permute-start.9) | collective-permute-done | bytes 32800 | tf_op jit(solution)/shard_map/ppermute | solution.py:40
  34.3 5.7 %collective-permute-start.10 = (f32[64,128]{1,0:T(8,128)S(1)}, f32[64,128]{1,0:T(8,128)S(1)}, u32[]{:S(2)}, u32[]{:S(2)}) collective-permute-start(f32[64,128]{1,0:T(8,128)S(1)} %add_add_fusion.2.mine_ref), channel_id=1, source_target_pairs={{0,4},{1,5},{2,6},{3,7},{4,0},{5,1},{6,2},{7,3},{8,12},{9,13},{10,... | collective-permute-start | bytes 98312 | tf_op jit(solution)/shard_map/ppermute | solution.py:40
  40.9 9.2 %shard_map.59 = (f32[64,128]{1,0:T(8,128)}, bf16[256,128]{1,0:T(8,128)(2,1)S(1)}) custom-call(s32[1]{0:T(128)} %bitcast.core_ref, f32[64,128]{1,0:T(8,128)S(1)} %add_add_fusion.2.mine_ref, f32[64,128]{1,0:T(8,128)S(1)} %collective-permute-done.10.other_ref, f32[64,128]{1,0:T(8,128)S(1)} %bitcast.31), custom_call_target="tpu_custom_call" | custom-call | tf_op jit(solution)/shard_map/pallas_call | solution.py:186
  50.1 2.3 %shard_map.60 = bf16[128,4,2,16,128]{4,3,2,1,0:T(8,128)(2,1)S(1)} custom-call(bf16[32768,128]{1,0:T(8,128)(2,1)S(1)} %get-tuple-element.16.near_ref, bf16[256,128]{1,0:T(8,128)(2,1)S(1)} %get-tuple-element.17.basis_ref), custom_call_target="tpu_custom_call" | custom-call | tf_op jit(solution)/shard_map/pallas_call | solution.py:215
  52.5 56.7 %all_to_all.5 = bf16[128,4,2,16,128]{4,3,2,1,0:T(8,128)(2,1)S(1)} all-to-all(bf16[128,4,2,16,128]{4,3,2,1,0:T(8,128)(2,1)S(1)} %shard_map.60), channel_id=1, replica_groups=mesh['blk'=32,'pen'=4] {'blk','pen'}, dimensions={0} | all-to-all | bytes 8388608 | tf_op jit(solution)/shard_map/all_to_all | solution.py:313
  109.1 4.1 %shard_map.61 = (f32[256,512]{1,0:T(8,128)S(1)}, f32[256,512]{1,0:T(8,128)S(1)}, bf16[32,512,128]{2,1,0:T(8,128)(2,1)}) custom-call(s32[1]{0:T(128)} %bitcast.core_ref, bf16[512,32,128]{2,1,0:T(8,128)(2,1)S(1)} %bitcast.27), custom_call_target="tpu_custom_call" | custom-call | tf_op jit(solution)/shard_map/pallas_call | solution.py:244
  115.7 1.7 %collective-permute-start.13 = (f32[64,512]{1,0:T(8,128)S(1)}, f32[64,512]{1,0:T(8,128)S(1)}, u32[]{:S(2)}, u32[]{:S(2)}) collective-permute-start(f32[64,512]{1,0:T(8,128)S(1)} %get-tuple-element.26), channel_id=1, source_target_pairs={{0,2},{1,3},{2,0},{3,1},{4,20},{5,21},{6,22},{7,23},{8,10},{9,11},... | collective-permute-start | bytes 393224 | tf_op jit(solution)/shard_map/ppermute | solution.py:40
  117.4 2.1 %collective-permute-start.14 = (f32[64,512]{1,0:T(8,128)S(1)}, f32[64,512]{1,0:T(8,128)S(1)}, u32[]{:S(2)}, u32[]{:S(2)}) collective-permute-start(f32[64,512]{1,0:T(8,128)S(1)} %get-tuple-element.25), channel_id=1, source_target_pairs={{0,3},{1,2},{2,1},{3,0},{4,28},{5,29},{6,30},{7,31},{8,11},{9,10},... | collective-permute-start | bytes 393224 | tf_op jit(solution)/shard_map/ppermute | solution.py:40
  119.7 1.7 %collective-permute-done.13 = f32[64,512]{1,0:T(8,128)S(1)} collective-permute-done((f32[64,512]{1,0:T(8,128)S(1)}, f32[64,512]{1,0:T(8,128)S(1)}, u32[]{:S(2)}, u32[]{:S(2)}) %collective-permute-start.13) | collective-permute-done | bytes 131104 | tf_op jit(solution)/shard_map/ppermute | solution.py:40
  124.6 2.2 %collective-permute-start.17 = (f32[64,512]{1,0:T(8,128)S(1)}, f32[64,512]{1,0:T(8,128)S(1)}, u32[]{:S(2)}, u32[]{:S(2)}) collective-permute-start(f32[64,512]{1,0:T(8,128)S(1)} %fusion), channel_id=1, source_target_pairs={{0,24},{1,25},{2,26},{3,27},{4,100},{5,101},{6,102},{7,103},{8,16}... | collective-permute-start | bytes 393224 | tf_op jit(solution)/shard_map/ppermute | solution.py:40
  126.8 1.9 %collective-permute-done.16 = f32[64,512]{1,0:T(8,128)S(1)} collective-permute-done((f32[64,512]{1,0:T(8,128)S(1)}, f32[64,512]{1,0:T(8,128)S(1)}, u32[]{:S(2)}, u32[]{:S(2)}) %collective-permute-start.16) | collective-permute-done | bytes 131104 | tf_op jit(solution)/shard_map/ppermute | solution.py:40
  130.6 1.9 %collective-permute-start.19 = (f32[64,512]{1,0:T(8,128)S(1)}, f32[64,512]{1,0:T(8,128)S(1)}, u32[]{:S(2)}, u32[]{:S(2)}) collective-permute-start(f32[64,512]{1,0:T(8,128)S(1)} %add_add_fusion.1), channel_id=1, source_target_pairs={{0,64},{1,65},{2,66},{3,67},{4,6},{5,7},{6,4},{7,5},{8,72},{9,73},... | collective-permute-start | bytes 393224 | tf_op jit(solution)/shard_map/ppermute | solution.py:40
  132.6 1.8 %collective-permute-start.20 = (f32[64,512]{1,0:T(8,128)S(1)}, f32[64,512]{1,0:T(8,128)S(1)}, u32[]{:S(2)}, u32[]{:S(2)}) collective-permute-start(f32[64,512]{1,0:T(8,128)S(1)} %add_add_fusion.1), channel_id=1, source_target_pairs={{0,96},{1,97},{2,98},{3,99},{4,7},{5,6},{6,5},{7,4},{8,104},{9,105... | collective-permute-start | bytes 393224 | tf_op jit(solution)/shard_map/ppermute | solution.py:40
  134.4 2.0 %collective-permute-done.19 = f32[64,512]{1,0:T(8,128)S(1)} collective-permute-done((f32[64,512]{1,0:T(8,128)S(1)}, f32[64,512]{1,0:T(8,128)S(1)}, u32[]{:S(2)}, u32[]{:S(2)}) %collective-permute-start.19) | collective-permute-done | bytes 131104 | tf_op jit(solution)/shard_map/ppermute | solution.py:40
  140.6 2.7 %collective-permute-done.21 = f32[64,512]{1,0:T(8,128)S(1)} collective-permute-done((f32[64,512]{1,0:T(8,128)S(1)}, f32[64,512]{1,0:T(8,128)S(1)}, u32[]{:S(2)}, u32[]{:S(2)}) %collective-permute-start.21) | collective-permute-done | bytes 131104 | tf_op jit(solution)/shard_map/ppermute | solution.py:40
  144.7 5.6 %collective-permute-start.24 = (f32[256,512]{1,0:T(8,128)S(1)}, f32[256,512]{1,0:T(8,128)S(1)}, u32[]{:S(2)}, u32[]{:S(2)}) collective-permute-start(f32[256,512]{1,0:T(8,128)S(1)} %bitcast.28), channel_id=1, source_target_pairs={{0,4},{1,5},{2,6},{3,7},{4,0},{5,1},{6,2},{7,3},{8,12},{9,13},{10,... | collective-permute-start | bytes 1572872 | tf_op jit(solution)/shard_map/ppermute | solution.py:40
  151.9 8.0 %shard_map.62 = (f32[32,512]{1,0:T(8,128)}, bf16[4,32,1024]{2,1,0:T(8,128)(2,1)}) custom-call(s32[1]{0:T(128)} %bitcast.core_ref, f32[256,512]{1,0:T(8,128)S(1)} %bitcast.29, f32[256,512]{1,0:T(8,128)S(1)} %collective-permute-done.24.other_ref, f32[32,512]{1,0:T(8,128)S(1)} %bitcast.30, bf16[32,512,128]{2,1,0:T(8,128)(2,1)} %get-tuple-element.20.far_ref), custom_call_target="tpu_custom_call" | custom-call | tf_op jit(solution)/shard_map/pallas_call | solution.py:282
  (49 shorter events, 25.9 us)
Async XLA Ops:
  7.2 2.3 %collective-permute-start = (f32[64,128]{1,0:T(8,128)S(1)}, f32[64,128]{1,0:T(8,128)S(1)}, u32[]{:S(2)}, u32[]{:S(2)}) collective-permute-start(f32[64,128]{1,0:T(8,128)S(1)} %get-tuple-element.14), channel_id=1, source_target_pairs={{0,4},{1,5},{2,6},{3,7},{4,0},{5,1},{6,2},{7,3},{8,12},{9,13},{10,... | collective-permute-start | bytes 98312 | tf_op jit(solution)/shard_map/ppermute | solution.py:40
  9.5 4.0 %collective-permute-start.1 = (f32[64,128]{1,0:T(8,128)S(1)}, f32[64,128]{1,0:T(8,128)S(1)}, u32[]{:S(2)}, u32[]{:S(2)}) collective-permute-start(f32[64,128]{1,0:T(8,128)S(1)} %add.87), channel_id=1, source_target_pairs={{0,1},{1,0},{2,3},{3,2},{4,12},{5,13},{6,14},{7,15},{8,9},{9,8},{1... | collective-permute-start | bytes 98312 | tf_op jit(solution)/shard_map/ppermute | solution.py:40
  10.9 4.3 %collective-permute-start.2 = (f32[64,128]{1,0:T(8,128)S(1)}, f32[64,128]{1,0:T(8,128)S(1)}, u32[]{:S(2)}, u32[]{:S(2)}) collective-permute-start(f32[64,128]{1,0:T(8,128)S(1)} %add.87), channel_id=1, source_target_pairs={{0,2},{1,3},{2,0},{3,1},{4,20},{5,21},{6,22},{7,23},{8,10},{9,11},... | collective-permute-start | bytes 98312 | tf_op jit(solution)/shard_map/ppermute | solution.py:40
  13.6 4.0 %collective-permute-start.3 = (f32[64,128]{1,0:T(8,128)S(1)}, f32[64,128]{1,0:T(8,128)S(1)}, u32[]{:S(2)}, u32[]{:S(2)}) collective-permute-start(f32[64,128]{1,0:T(8,128)S(1)} %add.87), channel_id=1, source_target_pairs={{0,3},{1,2},{2,1},{3,0},{4,28},{5,29},{6,30},{7,31},{8,11},{9,10},... | collective-permute-start | bytes 98312 | tf_op jit(solution)/shard_map/ppermute | solution.py:40
  17.6 5.0 %collective-permute-start.4 = (f32[64,128]{1,0:T(8,128)S(1)}, f32[64,128]{1,0:T(8,128)S(1)}, u32[]{:S(2)}, u32[]{:S(2)}) collective-permute-start(f32[64,128]{1,0:T(8,128)S(1)} %add_add_fusion.4), channel_id=1, source_target_pairs={{0,8},{1,9},{2,10},{3,11},{4,36},{5,37},{6,38},{7,39},{8,0},{9,1},... | collective-permute-start | bytes 98312 | tf_op jit(solution)/shard_map/ppermute | solution.py:40
  19.3 5.0 %collective-permute-start.5 = (f32[64,128]{1,0:T(8,128)S(1)}, f32[64,128]{1,0:T(8,128)S(1)}, u32[]{:S(2)}, u32[]{:S(2)}) collective-permute-start(f32[64,128]{1,0:T(8,128)S(1)} %add_add_fusion.4), channel_id=1, source_target_pairs={{0,16},{1,17},{2,18},{3,19},{4,68},{5,69},{6,70},{7,71},{8,24},{9,... | collective-permute-start | bytes 98312 | tf_op jit(solution)/shard_map/ppermute | solution.py:40
  22.6 4.0 %collective-permute-start.6 = (f32[64,128]{1,0:T(8,128)S(1)}, f32[64,128]{1,0:T(8,128)S(1)}, u32[]{:S(2)}, u32[]{:S(2)}) collective-permute-start(f32[64,128]{1,0:T(8,128)S(1)} %add_add_fusion.4), channel_id=1, source_target_pairs={{0,24},{1,25},{2,26},{3,27},{4,100},{5,101},{6,102},{7,103},{8,16}... | collective-permute-start | bytes 98312 | tf_op jit(solution)/shard_map/ppermute | solution.py:40
  26.6 3.9 %collective-permute-start.7 = (f32[64,128]{1,0:T(8,128)S(1)}, f32[64,128]{1,0:T(8,128)S(1)}, u32[]{:S(2)}, u32[]{:S(2)}) collective-permute-start(f32[64,128]{1,0:T(8,128)S(1)} %add_add_fusion.3), channel_id=1, source_target_pairs={{0,32},{1,33},{2,34},{3,35},{4,5},{5,4},{6,7},{7,6},{8,40},{9,41},... | collective-permute-start | bytes 98312 | tf_op jit(solution)/shard_map/ppermute | solution.py:40
  27.9 4.3 %collective-permute-start.8 = (f32[64,128]{1,0:T(8,128)S(1)}, f32[64,128]{1,0:T(8,128)S(1)}, u32[]{:S(2)}, u32[]{:S(2)}) collective-permute-start(f32[64,128]{1,0:T(8,128)S(1)} %add_add_fusion.3), channel_id=1, source_target_pairs={{0,64},{1,65},{2,66},{3,67},{4,6},{5,7},{6,4},{7,5},{8,72},{9,73},... | collective-permute-start | bytes 98312 | tf_op jit(solution)/shard_map/ppermute | solution.py:40
  30.3 4.0 %collective-permute-start.9 = (f32[64,128]{1,0:T(8,128)S(1)}, f32[64,128]{1,0:T(8,128)S(1)}, u32[]{:S(2)}, u32[]{:S(2)}) collective-permute-start(f32[64,128]{1,0:T(8,128)S(1)} %add_add_fusion.3), channel_id=1, source_target_pairs={{0,96},{1,97},{2,98},{3,99},{4,7},{5,6},{6,5},{7,4},{8,104},{9,105... | collective-permute-start | bytes 98312 | tf_op jit(solution)/shard_map/ppermute | solution.py:40
  34.3 6.6 %collective-permute-start.10 = (f32[64,128]{1,0:T(8,128)S(1)}, f32[64,128]{1,0:T(8,128)S(1)}, u32[]{:S(2)}, u32[]{:S(2)}) collective-permute-start(f32[64,128]{1,0:T(8,128)S(1)} %add_add_fusion.2.mine_ref), channel_id=1, source_target_pairs={{0,4},{1,5},{2,6},{3,7},{4,0},{5,1},{6,2},{7,3},{8,12},{9,13},{10,... | collective-permute-start | bytes 98312 | tf_op jit(solution)/shard_map/ppermute | solution.py:40
  115.5 4.2 %collective-permute-start.12 = (f32[64,512]{1,0:T(8,128)S(1)}, f32[64,512]{1,0:T(8,128)S(1)}, u32[]{:S(2)}, u32[]{:S(2)}) collective-permute-start(f32[64,512]{1,0:T(8,128)S(1)} %get-tuple-element.27), channel_id=1, source_target_pairs={{0,1},{1,0},{2,3},{3,2},{4,12},{5,13},{6,14},{7,15},{8,9},{9,8},{1... | collective-permute-start | bytes 393224 | tf_op jit(solution)/shard_map/ppermute | solution.py:40
  115.7 5.7 %collective-permute-start.13 = (f32[64,512]{1,0:T(8,128)S(1)}, f32[64,512]{1,0:T(8,128)S(1)}, u32[]{:S(2)}, u32[]{:S(2)}) collective-permute-start(f32[64,512]{1,0:T(8,128)S(1)} %get-tuple-element.26), channel_id=1, source_target_pairs={{0,2},{1,3},{2,0},{3,1},{4,20},{5,21},{6,22},{7,23},{8,10},{9,11},... | collective-permute-start | bytes 393224 | tf_op jit(solution)/shard_map/ppermute | solution.py:40
  117.4 5.4 %collective-permute-start.14 = (f32[64,512]{1,0:T(8,128)S(1)}, f32[64,512]{1,0:T(8,128)S(1)}, u32[]{:S(2)}, u32[]{:S(2)}) collective-permute-start(f32[64,512]{1,0:T(8,128)S(1)} %get-tuple-element.25), channel_id=1, source_target_pairs={{0,3},{1,2},{2,1},{3,0},{4,28},{5,29},{6,30},{7,31},{8,11},{9,10},... | collective-permute-start | bytes 393224 | tf_op jit(solution)/shard_map/ppermute | solution.py:40
  122.9 3.9 %collective-permute-start.15 = (f32[64,512]{1,0:T(8,128)S(1)}, f32[64,512]{1,0:T(8,128)S(1)}, u32[]{:S(2)}, u32[]{:S(2)}) collective-permute-start(f32[64,512]{1,0:T(8,128)S(1)} %fusion), channel_id=1, source_target_pairs={{0,8},{1,9},{2,10},{3,11},{4,36},{5,37},{6,38},{7,39},{8,0},{9,1},... | collective-permute-start | bytes 393224 | tf_op jit(solution)/shard_map/ppermute | solution.py:40
  123.4 5.4 %collective-permute-start.16 = (f32[64,512]{1,0:T(8,128)S(1)}, f32[64,512]{1,0:T(8,128)S(1)}, u32[]{:S(2)}, u32[]{:S(2)}) collective-permute-start(f32[64,512]{1,0:T(8,128)S(1)} %fusion), channel_id=1, source_target_pairs={{0,16},{1,17},{2,18},{3,19},{4,68},{5,69},{6,70},{7,71},{8,24},{9,... | collective-permute-start | bytes 393224 | tf_op jit(solution)/shard_map/ppermute | solution.py:40
  124.6 5.8 %collective-permute-start.17 = (f32[64,512]{1,0:T(8,128)S(1)}, f32[64,512]{1,0:T(8,128)S(1)}, u32[]{:S(2)}, u32[]{:S(2)}) collective-permute-start(f32[64,512]{1,0:T(8,128)S(1)} %fusion), channel_id=1, source_target_pairs={{0,24},{1,25},{2,26},{3,27},{4,100},{5,101},{6,102},{7,103},{8,16}... | collective-permute-start | bytes 393224 | tf_op jit(solution)/shard_map/ppermute | solution.py:40
  130.4 3.9 %collective-permute-start.18 = (f32[64,512]{1,0:T(8,128)S(1)}, f32[64,512]{1,0:T(8,128)S(1)}, u32[]{:S(2)}, u32[]{:S(2)}) collective-permute-start(f32[64,512]{1,0:T(8,128)S(1)} %add_add_fusion.1), channel_id=1, source_target_pairs={{0,32},{1,33},{2,34},{3,35},{4,5},{5,4},{6,7},{7,6},{8,40},{9,41},... | collective-permute-start | bytes 393224 | tf_op jit(solution)/shard_map/ppermute | solution.py:40
  130.6 5.7 %collective-permute-start.19 = (f32[64,512]{1,0:T(8,128)S(1)}, f32[64,512]{1,0:T(8,128)S(1)}, u32[]{:S(2)}, u32[]{:S(2)}) collective-permute-start(f32[64,512]{1,0:T(8,128)S(1)} %add_add_fusion.1), channel_id=1, source_target_pairs={{0,64},{1,65},{2,66},{3,67},{4,6},{5,7},{6,4},{7,5},{8,72},{9,73},... | collective-permute-start | bytes 393224 | tf_op jit(solution)/shard_map/ppermute | solution.py:40
  132.6 5.2 %collective-permute-start.20 = (f32[64,512]{1,0:T(8,128)S(1)}, f32[64,512]{1,0:T(8,128)S(1)}, u32[]{:S(2)}, u32[]{:S(2)}) collective-permute-start(f32[64,512]{1,0:T(8,128)S(1)} %add_add_fusion.1), channel_id=1, source_target_pairs={{0,96},{1,97},{2,98},{3,99},{4,7},{5,6},{6,5},{7,4},{8,104},{9,105... | collective-permute-start | bytes 393224 | tf_op jit(solution)/shard_map/ppermute | solution.py:40
  137.8 5.4 %collective-permute-start.21 = (f32[64,512]{1,0:T(8,128)S(1)}, f32[64,512]{1,0:T(8,128)S(1)}, u32[]{:S(2)}, u32[]{:S(2)}) collective-permute-start(f32[64,512]{1,0:T(8,128)S(1)} %get-tuple-element.24), channel_id=1, source_target_pairs={{0,2},{1,3},{2,0},{3,1},{4,20},{5,21},{6,22},{7,23},{8,10},{9,11},... | collective-permute-start | bytes 393224 | tf_op jit(solution)/shard_map/ppermute | solution.py:40
  139.2 5.4 %collective-permute-start.22 = (f32[64,512]{1,0:T(8,128)S(1)}, f32[64,512]{1,0:T(8,128)S(1)}, u32[]{:S(2)}, u32[]{:S(2)}) collective-permute-start(f32[64,512]{1,0:T(8,128)S(1)} %get-tuple-element.24), channel_id=1, source_target_pairs={{0,3},{1,2},{2,1},{3,0},{4,28},{5,29},{6,30},{7,31},{8,11},{9,10},... | collective-permute-start | bytes 393224 | tf_op jit(solution)/shard_map/ppermute | solution.py:40
  140.3 4.4 %collective-permute-start.23 = (f32[64,512]{1,0:T(8,128)S(1)}, f32[64,512]{1,0:T(8,128)S(1)}, u32[]{:S(2)}, u32[]{:S(2)}) collective-permute-start(f32[64,512]{1,0:T(8,128)S(1)} %get-tuple-element.24), channel_id=1, source_target_pairs={{0,1},{1,0},{2,3},{3,2},{4,12},{5,13},{6,14},{7,15},{8,9},{9,8},{1... | collective-permute-start | bytes 393224 | tf_op jit(solution)/shard_map/ppermute | solution.py:40
  144.7 7.2 %collective-permute-start.24 = (f32[256,512]{1,0:T(8,128)S(1)}, f32[256,512]{1,0:T(8,128)S(1)}, u32[]{:S(2)}, u32[]{:S(2)}) collective-permute-start(f32[256,512]{1,0:T(8,128)S(1)} %bitcast.28), channel_id=1, source_target_pairs={{0,4},{1,5},{2,6},{3,7},{4,0},{5,1},{6,2},{7,3},{8,12},{9,13},{10,... | collective-permute-start | bytes 1572872 | tf_op jit(solution)/shard_map/ppermute | solution.py:40
  (3 other events, 85.1 us)

commit v6 on v5

--- a/solution.py
+++ b/solution.py
@@ -9,6 +9,7 @@
 ITX = 3
 
 F32, BF16 = jnp.float32, jnp.bfloat16
+PIVOT_FLOOR = 1e-5
 HIGHEST = lax.Precision.HIGHEST
 VMEM = pl.BlockSpec(memory_space=pltpu.VMEM)
 SMEM = pl.BlockSpec(memory_space=pltpu.SMEM)
@@ -114,12 +115,43 @@
     return jnp.concatenate(rows, axis=0)[:, size:]
 
 
-def subspace(gram, flat, sweeps):
+def orthonormal_round(flat):
+    square = product(flat, flat, 1, 1)
+    inverse = inverse_factor(square)
+    same = identity(square.shape[0])
+    lead = jnp.sum(inverse * same, axis=1, keepdims=True)
+    diagonal = jnp.sum(square * same, axis=1, keepdims=True)
+    weak = jnp.where(lead * lead * diagonal * PIVOT_FLOOR < 1.0, 0.0, 1.0)
+    return product(inverse, flat, 1, 0), jnp.sum(weak)
+
+
+def separate_sweeps(gram, start, sweeps):
+    flat = start
     for sweep in range(sweeps):
-        flat = product(flat, gram, 1, 0)
-        for repeat in range(2 if sweep == sweeps - 1 else 1):
-            flat = product(inverse_factor(product(flat, flat, 1, 1)), flat, 1, 0)
-    return flat
+        flat = orthonormal_round(product(flat, gram, 1, 0))[0]
+    return orthonormal_round(flat)[0]
+
+
+def joined_sweeps(gram_ref, start, sweeps, flat_ref):
+    gram = gram_ref[...]
+    flat = start
+    for sweep in range(sweeps - 2):
+        flat = orthonormal_round(product(flat, gram, 1, 0))[0]
+    flat = product(product(flat, gram, 1, 0), gram, 1, 0)
+    flat, weak = orthonormal_round(flat)
+    flat_ref[...] = orthonormal_round(flat)[0]
+
+    @pl.when(weak > 0.0)
+    def _():
+        flat_ref[...] = start
+
+        @pl.loop(0, sweeps + 1)
+        def _(index):
+            @pl.when(index < sweeps)
+            def _():
+                flat_ref[...] = product(flat_ref[...], gram_ref[...], 1, 0)
+
+            flat_ref[...] = orthonormal_round(flat_ref[...])[0]
 
 
 def time_gram(core, snapshots):
@@ -174,11 +206,10 @@
 def time_subspace(core, mine, other, start, scale):
     rank, window = start.shape
 
-    def kernel(core_ref, mine_ref, other_ref, start_ref, basis_ref, pair_ref):
-        gram = join_halves(core_ref, mine_ref, other_ref, scale)
-        flat = subspace(gram, start_ref[...], ITT)
-        basis_ref[...] = flat
-        narrow = flat.T.astype(BF16)
+    def kernel(core_ref, mine_ref, other_ref, start_ref, basis_ref, pair_ref, held_ref):
+        held_ref[...] = join_halves(core_ref, mine_ref, other_ref, scale)
+        joined_sweeps(held_ref, start_ref[...], ITT, basis_ref)
+        narrow = basis_ref[...].T.astype(BF16)
         zero = jnp.zeros_like(narrow)
         pair_ref[:window] = jnp.concatenate([narrow, zero], axis=1)
         pair_ref[window:] = jnp.concatenate([zero, narrow], axis=1)
@@ -191,6 +222,7 @@
             jax.ShapeDtypeStruct((rank, window), F32),
             jax.ShapeDtypeStruct((2 * window, 2 * rank), BF16),
         ],
+        scratch_shapes=[pltpu.VMEM((window, window), F32)],
         compiler_params=limit(6),
     )(core, mine, other, start)
 
@@ -264,7 +296,7 @@
         fetch = pltpu.make_async_copy(far_ref, group_ref, arrived)
         fetch.start()
         gram = join_halves(core_ref, mine_ref, other_ref, scale)
-        flat = subspace(gram, start_ref[...], ITX)
+        flat = separate_sweeps(gram, start_ref[...], ITX)
         basis_ref[...] = flat
         narrow = flat.astype(BF16)
         fetch.wait()

time: 160 us -> 167 us (1.044)
  Pallas kernels: 30.3 us -> 36.9 us
    pallas_call x1, Pallas kernels: 9.23 us -> 15.9 us  [time_subspace(): pl.pallas_call(kernel, in_specs=[SMEM, VMEM, VMEM, VMEM], out_specs=[VMEM...]
where the time goes in v6:
time: 167 us
  blocking collectives  56.7 us (34%)
  starting transfers between devices  41 us (25%)
  Pallas kernels  36.9 us (22%)
  waiting for transfers between devices  30.9 us (19%)
    all_to_all x1, blocking collectives, on_device(): lax.all_to_all(core_time, ('blk', 'pen'), split_axis=0, concat_axis=0, ti...  56.7 us
    ppermute x25, starting transfers between devices, swap(): return lax.ppermute(value, ('blk', 'pen'), self.partners(stage, step))  41 us
    ppermute x25, waiting for transfers between devices, swap(): return lax.ppermute(value, ('blk', 'pen'), self.partners(stage, step))  30.9 us
    pallas_call x1, Pallas kernels, time_subspace(): pl.pallas_call(kernel, in_specs=[SMEM, VMEM, VMEM, VMEM], out_specs=[VMEM...  15.9 us
    pallas_call x1, Pallas kernels, plane_subspace(): pl.pallas_call(kernel, in_specs=[SMEM, VMEM, VMEM, VMEM, HBM], out_specs=...  8.04 us
    pallas_call x1, Pallas kernels, time_gram(): pl.pallas_call(kernel, in_specs=[SMEM, HBM], out_specs=[VMEM, VMEM, VMEM]...  6.55 us
    pallas_call x1, Pallas kernels, plane_gram(): pl.pallas_call(kernel, in_specs=[SMEM, VMEM], out_specs=[VMEM, VMEM, HBM]...  4.12 us
  transfers between devices with their start and end apart: 25, of which 19 were waited for; matrix products, arithmetic and copies ran while one was open for 0% of the time, Pallas kernels for 0%

profile of v6, /device:TPU:1, one launch (start us, length us, event | category | flops | bytes accessed | tf_op | source)
XLA Modules:
  0.0 166.7 jit_solution(6709432703750222495)
XLA Ops:
  0.7 6.5 %shard_map.58 = (f32[64,128]{1,0:T(8,128)S(1)}, f32[64,128]{1,0:T(8,128)S(1)}, bf16[32768,128]{1,0:T(8,128)(2,1)S(1)}) custom-call(s32[1]{0:T(128)} %bitcast.core_ref, bf16[32768,128]{1,0:T(8,128)(2,1)} %bitcast.32), custom_call_target="tpu_custom_call" | custom-call | tf_op jit(solution)/shard_map/pallas_call | solution.py:183
  10.9 2.6 %collective-permute-start.2 = (f32[64,128]{1,0:T(8,128)S(1)}, f32[64,128]{1,0:T(8,128)S(1)}, u32[]{:S(2)}, u32[]{:S(2)}) collective-permute-start(f32[64,128]{1,0:T(8,128)S(1)} %add.87), channel_id=1, source_target_pairs={{0,2},{1,3},{2,0},{3,1},{4,20},{5,21},{6,22},{7,23},{8,10},{9,11},... | collective-permute-start | bytes 98312 | tf_op jit(solution)/shard_map/ppermute | solution.py:41
  15.2 2.3 %collective-permute-done.3 = f32[64,128]{1,0:T(8,128)S(1)} collective-permute-done((f32[64,128]{1,0:T(8,128)S(1)}, f32[64,128]{1,0:T(8,128)S(1)}, u32[]{:S(2)}, u32[]{:S(2)}) %collective-permute-start.3) | collective-permute-done | bytes 32800 | tf_op jit(solution)/shard_map/ppermute | solution.py:41
  17.6 1.7 %collective-permute-start.4 = (f32[64,128]{1,0:T(8,128)S(1)}, f32[64,128]{1,0:T(8,128)S(1)}, u32[]{:S(2)}, u32[]{:S(2)}) collective-permute-start(f32[64,128]{1,0:T(8,128)S(1)} %add_add_fusion.4), channel_id=1, source_target_pairs={{0,8},{1,9},{2,10},{3,11},{4,36},{5,37},{6,38},{7,39},{8,0},{9,1},... | collective-permute-start | bytes 98312 | tf_op jit(solution)/shard_map/ppermute | solution.py:41
  19.3 3.3 %collective-permute-start.5 = (f32[64,128]{1,0:T(8,128)S(1)}, f32[64,128]{1,0:T(8,128)S(1)}, u32[]{:S(2)}, u32[]{:S(2)}) collective-permute-start(f32[64,128]{1,0:T(8,128)S(1)} %add_add_fusion.4), channel_id=1, source_target_pairs={{0,16},{1,17},{2,18},{3,19},{4,68},{5,69},{6,70},{7,71},{8,24},{9,... | collective-permute-start | bytes 98312 | tf_op jit(solution)/shard_map/ppermute | solution.py:41
  24.2 2.3 %collective-permute-done.6 = f32[64,128]{1,0:T(8,128)S(1)} collective-permute-done((f32[64,128]{1,0:T(8,128)S(1)}, f32[64,128]{1,0:T(8,128)S(1)}, u32[]{:S(2)}, u32[]{:S(2)}) %collective-permute-start.6) | collective-permute-done | bytes 32800 | tf_op jit(solution)/shard_map/ppermute | solution.py:41
  27.9 2.5 %collective-permute-start.8 = (f32[64,128]{1,0:T(8,128)S(1)}, f32[64,128]{1,0:T(8,128)S(1)}, u32[]{:S(2)}, u32[]{:S(2)}) collective-permute-start(f32[64,128]{1,0:T(8,128)S(1)} %add_add_fusion.3), channel_id=1, source_target_pairs={{0,64},{1,65},{2,66},{3,67},{4,6},{5,7},{6,4},{7,5},{8,72},{9,73},... | collective-permute-start | bytes 98312 | tf_op jit(solution)/shard_map/ppermute | solution.py:41
  32.1 2.2 %collective-permute-done.9 = f32[64,128]{1,0:T(8,128)S(1)} collective-permute-done((f32[64,128]{1,0:T(8,128)S(1)}, f32[64,128]{1,0:T(8,128)S(1)}, u32[]{:S(2)}, u32[]{:S(2)}) %collective-permute-start.9) | collective-permute-done | bytes 32800 | tf_op jit(solution)/shard_map/ppermute | solution.py:41
  34.3 5.6 %collective-permute-start.10 = (f32[64,128]{1,0:T(8,128)S(1)}, f32[64,128]{1,0:T(8,128)S(1)}, u32[]{:S(2)}, u32[]{:S(2)}) collective-permute-start(f32[64,128]{1,0:T(8,128)S(1)} %add_add_fusion.2.mine_ref), channel_id=1, source_target_pairs={{0,4},{1,5},{2,6},{3,7},{4,0},{5,1},{6,2},{7,3},{8,12},{9,13},{10,... | collective-permute-start | bytes 98312 | tf_op jit(solution)/shard_map/ppermute | solution.py:41
  40.7 15.9 %shard_map.59 = (f32[64,128]{1,0:T(8,128)}, bf16[256,128]{1,0:T(8,128)(2,1)S(1)}) custom-call(s32[1]{0:T(128)} %bitcast.core_ref, f32[64,128]{1,0:T(8,128)S(1)} %add_add_fusion.2.mine_ref, f32[64,128]{1,0:T(8,128)S(1)} %collective-permute-done.10.other_ref, f32[64,128]{1,0:T(8,128)S(1)} %bitcast.31), custom_call_target="tpu_custom_call" | custom-call | tf_op jit(solution)/shard_map/pallas_call | solution.py:217
  56.6 2.3 %shard_map.60 = bf16[128,4,2,16,128]{4,3,2,1,0:T(8,128)(2,1)S(1)} custom-call(bf16[32768,128]{1,0:T(8,128)(2,1)S(1)} %get-tuple-element.16.near_ref, bf16[256,128]{1,0:T(8,128)(2,1)S(1)} %get-tuple-element.17.basis_ref), custom_call_target="tpu_custom_call" | custom-call | tf_op jit(solution)/shard_map/pallas_call | solution.py:247
  58.9 56.7 %all_to_all.5 = bf16[128,4,2,16,128]{4,3,2,1,0:T(8,128)(2,1)S(1)} all-to-all(bf16[128,4,2,16,128]{4,3,2,1,0:T(8,128)(2,1)S(1)} %shard_map.60), channel_id=1, replica_groups=mesh['blk'=32,'pen'=4] {'blk','pen'}, dimensions={0} | all-to-all | bytes 8388608 | tf_op jit(solution)/shard_map/all_to_all | solution.py:345
  115.6 4.1 %shard_map.61 = (f32[256,512]{1,0:T(8,128)S(1)}, f32[256,512]{1,0:T(8,128)S(1)}, bf16[32,512,128]{2,1,0:T(8,128)(2,1)}) custom-call(s32[1]{0:T(128)} %bitcast.core_ref, bf16[512,32,128]{2,1,0:T(8,128)(2,1)S(1)} %bitcast.27), custom_call_target="tpu_custom_call" | custom-call | tf_op jit(solution)/shard_map/pallas_call | solution.py:276
  122.1 1.7 %collective-permute-start.13 = (f32[64,512]{1,0:T(8,128)S(1)}, f32[64,512]{1,0:T(8,128)S(1)}, u32[]{:S(2)}, u32[]{:S(2)}) collective-permute-start(f32[64,512]{1,0:T(8,128)S(1)} %get-tuple-element.26), channel_id=1, source_target_pairs={{0,2},{1,3},{2,0},{3,1},{4,20},{5,21},{6,22},{7,23},{8,10},{9,11},... | collective-permute-start | bytes 393224 | tf_op jit(solution)/shard_map/ppermute | solution.py:41
  123.8 2.1 %collective-permute-start.14 = (f32[64,512]{1,0:T(8,128)S(1)}, f32[64,512]{1,0:T(8,128)S(1)}, u32[]{:S(2)}, u32[]{:S(2)}) collective-permute-start(f32[64,512]{1,0:T(8,128)S(1)} %get-tuple-element.25), channel_id=1, source_target_pairs={{0,3},{1,2},{2,1},{3,0},{4,28},{5,29},{6,30},{7,31},{8,11},{9,10},... | collective-permute-start | bytes 393224 | tf_op jit(solution)/shard_map/ppermute | solution.py:41
  126.1 1.7 %collective-permute-done.13 = f32[64,512]{1,0:T(8,128)S(1)} collective-permute-done((f32[64,512]{1,0:T(8,128)S(1)}, f32[64,512]{1,0:T(8,128)S(1)}, u32[]{:S(2)}, u32[]{:S(2)}) %collective-permute-start.13) | collective-permute-done | bytes 131104 | tf_op jit(solution)/shard_map/ppermute | solution.py:41
  131.1 2.2 %collective-permute-start.17 = (f32[64,512]{1,0:T(8,128)S(1)}, f32[64,512]{1,0:T(8,128)S(1)}, u32[]{:S(2)}, u32[]{:S(2)}) collective-permute-start(f32[64,512]{1,0:T(8,128)S(1)} %fusion), channel_id=1, source_target_pairs={{0,24},{1,25},{2,26},{3,27},{4,100},{5,101},{6,102},{7,103},{8,16}... | collective-permute-start | bytes 393224 | tf_op jit(solution)/shard_map/ppermute | solution.py:41
  133.2 1.9 %collective-permute-done.16 = f32[64,512]{1,0:T(8,128)S(1)} collective-permute-done((f32[64,512]{1,0:T(8,128)S(1)}, f32[64,512]{1,0:T(8,128)S(1)}, u32[]{:S(2)}, u32[]{:S(2)}) %collective-permute-start.16) | collective-permute-done | bytes 131104 | tf_op jit(solution)/shard_map/ppermute | solution.py:41
  137.1 1.9 %collective-permute-start.19 = (f32[64,512]{1,0:T(8,128)S(1)}, f32[64,512]{1,0:T(8,128)S(1)}, u32[]{:S(2)}, u32[]{:S(2)}) collective-permute-start(f32[64,512]{1,0:T(8,128)S(1)} %add_add_fusion.1), channel_id=1, source_target_pairs={{0,64},{1,65},{2,66},{3,67},{4,6},{5,7},{6,4},{7,5},{8,72},{9,73},... | collective-permute-start | bytes 393224 | tf_op jit(solution)/shard_map/ppermute | solution.py:41
  139.0 1.8 %collective-permute-start.20 = (f32[64,512]{1,0:T(8,128)S(1)}, f32[64,512]{1,0:T(8,128)S(1)}, u32[]{:S(2)}, u32[]{:S(2)}) collective-permute-start(f32[64,512]{1,0:T(8,128)S(1)} %add_add_fusion.1), channel_id=1, source_target_pairs={{0,96},{1,97},{2,98},{3,99},{4,7},{5,6},{6,5},{7,4},{8,104},{9,105... | collective-permute-start | bytes 393224 | tf_op jit(solution)/shard_map/ppermute | solution.py:41
  140.8 2.0 %collective-permute-done.19 = f32[64,512]{1,0:T(8,128)S(1)} collective-permute-done((f32[64,512]{1,0:T(8,128)S(1)}, f32[64,512]{1,0:T(8,128)S(1)}, u32[]{:S(2)}, u32[]{:S(2)}) %collective-permute-start.19) | collective-permute-done | bytes 131104 | tf_op jit(solution)/shard_map/ppermute | solution.py:41
  147.0 2.7 %collective-permute-done.21 = f32[64,512]{1,0:T(8,128)S(1)} collective-permute-done((f32[64,512]{1,0:T(8,128)S(1)}, f32[64,512]{1,0:T(8,128)S(1)}, u32[]{:S(2)}, u32[]{:S(2)}) %collective-permute-start.21) | collective-permute-done | bytes 131104 | tf_op jit(solution)/shard_map/ppermute | solution.py:41
  151.1 5.8 %collective-permute-start.24 = (f32[256,512]{1,0:T(8,128)S(1)}, f32[256,512]{1,0:T(8,128)S(1)}, u32[]{:S(2)}, u32[]{:S(2)}) collective-permute-start(f32[256,512]{1,0:T(8,128)S(1)} %bitcast.28), channel_id=1, source_target_pairs={{0,4},{1,5},{2,6},{3,7},{4,0},{5,1},{6,2},{7,3},{8,12},{9,13},{10,... | collective-permute-start | bytes 1572872 | tf_op jit(solution)/shard_map/ppermute | solution.py:41
  158.5 8.0 %shard_map.62 = (f32[32,512]{1,0:T(8,128)}, bf16[4,32,1024]{2,1,0:T(8,128)(2,1)}) custom-call(s32[1]{0:T(128)} %bitcast.core_ref, f32[256,512]{1,0:T(8,128)S(1)} %bitcast.29, f32[256,512]{1,0:T(8,128)S(1)} %collective-permute-done.24.other_ref, f32[32,512]{1,0:T(8,128)S(1)} %bitcast.30, bf16[32,512,128]{2,1,0:T(8,128)(2,1)} %get-tuple-element.20.far_ref), custom_call_target="tpu_custom_call" | custom-call | tf_op jit(solution)/shard_map/pallas_call | solution.py:314
  (49 shorter events, 25.9 us)
Async XLA Ops:
  7.2 2.3 %collective-permute-start = (f32[64,128]{1,0:T(8,128)S(1)}, f32[64,128]{1,0:T(8,128)S(1)}, u32[]{:S(2)}, u32[]{:S(2)}) collective-permute-start(f32[64,128]{1,0:T(8,128)S(1)} %get-tuple-element.14), channel_id=1, source_target_pairs={{0,4},{1,5},{2,6},{3,7},{4,0},{5,1},{6,2},{7,3},{8,12},{9,13},{10,... | collective-permute-start | bytes 98312 | tf_op jit(solution)/shard_map/ppermute | solution.py:41
  9.5 4.0 %collective-permute-start.1 = (f32[64,128]{1,0:T(8,128)S(1)}, f32[64,128]{1,0:T(8,128)S(1)}, u32[]{:S(2)}, u32[]{:S(2)}) collective-permute-start(f32[64,128]{1,0:T(8,128)S(1)} %add.87), channel_id=1, source_target_pairs={{0,1},{1,0},{2,3},{3,2},{4,12},{5,13},{6,14},{7,15},{8,9},{9,8},{1... | collective-permute-start | bytes 98312 | tf_op jit(solution)/shard_map/ppermute | solution.py:41
  10.9 4.3 %collective-permute-start.2 = (f32[64,128]{1,0:T(8,128)S(1)}, f32[64,128]{1,0:T(8,128)S(1)}, u32[]{:S(2)}, u32[]{:S(2)}) collective-permute-start(f32[64,128]{1,0:T(8,128)S(1)} %add.87), channel_id=1, source_target_pairs={{0,2},{1,3},{2,0},{3,1},{4,20},{5,21},{6,22},{7,23},{8,10},{9,11},... | collective-permute-start | bytes 98312 | tf_op jit(solution)/shard_map/ppermute | solution.py:41
  13.6 4.0 %collective-permute-start.3 = (f32[64,128]{1,0:T(8,128)S(1)}, f32[64,128]{1,0:T(8,128)S(1)}, u32[]{:S(2)}, u32[]{:S(2)}) collective-permute-start(f32[64,128]{1,0:T(8,128)S(1)} %add.87), channel_id=1, source_target_pairs={{0,3},{1,2},{2,1},{3,0},{4,28},{5,29},{6,30},{7,31},{8,11},{9,10},... | collective-permute-start | bytes 98312 | tf_op jit(solution)/shard_map/ppermute | solution.py:41
  17.6 5.0 %collective-permute-start.4 = (f32[64,128]{1,0:T(8,128)S(1)}, f32[64,128]{1,0:T(8,128)S(1)}, u32[]{:S(2)}, u32[]{:S(2)}) collective-permute-start(f32[64,128]{1,0:T(8,128)S(1)} %add_add_fusion.4), channel_id=1, source_target_pairs={{0,8},{1,9},{2,10},{3,11},{4,36},{5,37},{6,38},{7,39},{8,0},{9,1},... | collective-permute-start | bytes 98312 | tf_op jit(solution)/shard_map/ppermute | solution.py:41
  19.3 5.0 %collective-permute-start.5 = (f32[64,128]{1,0:T(8,128)S(1)}, f32[64,128]{1,0:T(8,128)S(1)}, u32[]{:S(2)}, u32[]{:S(2)}) collective-permute-start(f32[64,128]{1,0:T(8,128)S(1)} %add_add_fusion.4), channel_id=1, source_target_pairs={{0,16},{1,17},{2,18},{3,19},{4,68},{5,69},{6,70},{7,71},{8,24},{9,... | collective-permute-start | bytes 98312 | tf_op jit(solution)/shard_map/ppermute | solution.py:41
  22.6 4.0 %collective-permute-start.6 = (f32[64,128]{1,0:T(8,128)S(1)}, f32[64,128]{1,0:T(8,128)S(1)}, u32[]{:S(2)}, u32[]{:S(2)}) collective-permute-start(f32[64,128]{1,0:T(8,128)S(1)} %add_add_fusion.4), channel_id=1, source_target_pairs={{0,24},{1,25},{2,26},{3,27},{4,100},{5,101},{6,102},{7,103},{8,16}... | collective-permute-start | bytes 98312 | tf_op jit(solution)/shard_map/ppermute | solution.py:41
  26.6 3.9 %collective-permute-start.7 = (f32[64,128]{1,0:T(8,128)S(1)}, f32[64,128]{1,0:T(8,128)S(1)}, u32[]{:S(2)}, u32[]{:S(2)}) collective-permute-start(f32[64,128]{1,0:T(8,128)S(1)} %add_add_fusion.3), channel_id=1, source_target_pairs={{0,32},{1,33},{2,34},{3,35},{4,5},{5,4},{6,7},{7,6},{8,40},{9,41},... | collective-permute-start | bytes 98312 | tf_op jit(solution)/shard_map/ppermute | solution.py:41
  27.9 4.3 %collective-permute-start.8 = (f32[64,128]{1,0:T(8,128)S(1)}, f32[64,128]{1,0:T(8,128)S(1)}, u32[]{:S(2)}, u32[]{:S(2)}) collective-permute-start(f32[64,128]{1,0:T(8,128)S(1)} %add_add_fusion.3), channel_id=1, source_target_pairs={{0,64},{1,65},{2,66},{3,67},{4,6},{5,7},{6,4},{7,5},{8,72},{9,73},... | collective-permute-start | bytes 98312 | tf_op jit(solution)/shard_map/ppermute | solution.py:41
  30.3 4.0 %collective-permute-start.9 = (f32[64,128]{1,0:T(8,128)S(1)}, f32[64,128]{1,0:T(8,128)S(1)}, u32[]{:S(2)}, u32[]{:S(2)}) collective-permute-start(f32[64,128]{1,0:T(8,128)S(1)} %add_add_fusion.3), channel_id=1, source_target_pairs={{0,96},{1,97},{2,98},{3,99},{4,7},{5,6},{6,5},{7,4},{8,104},{9,105... | collective-permute-start | bytes 98312 | tf_op jit(solution)/shard_map/ppermute | solution.py:41
  34.3 6.4 %collective-permute-start.10 = (f32[64,128]{1,0:T(8,128)S(1)}, f32[64,128]{1,0:T(8,128)S(1)}, u32[]{:S(2)}, u32[]{:S(2)}) collective-permute-start(f32[64,128]{1,0:T(8,128)S(1)} %add_add_fusion.2.mine_ref), channel_id=1, source_target_pairs={{0,4},{1,5},{2,6},{3,7},{4,0},{5,1},{6,2},{7,3},{8,12},{9,13},{10,... | collective-permute-start | bytes 98312 | tf_op jit(solution)/shard_map/ppermute | solution.py:41
  121.9 4.2 %collective-permute-start.12 = (f32[64,512]{1,0:T(8,128)S(1)}, f32[64,512]{1,0:T(8,128)S(1)}, u32[]{:S(2)}, u32[]{:S(2)}) collective-permute-start(f32[64,512]{1,0:T(8,128)S(1)} %get-tuple-element.27), channel_id=1, source_target_pairs={{0,1},{1,0},{2,3},{3,2},{4,12},{5,13},{6,14},{7,15},{8,9},{9,8},{1... | collective-permute-start | bytes 393224 | tf_op jit(solution)/shard_map/ppermute | solution.py:41
  122.1 5.8 %collective-permute-start.13 = (f32[64,512]{1,0:T(8,128)S(1)}, f32[64,512]{1,0:T(8,128)S(1)}, u32[]{:S(2)}, u32[]{:S(2)}) collective-permute-start(f32[64,512]{1,0:T(8,128)S(1)} %get-tuple-element.26), channel_id=1, source_target_pairs={{0,2},{1,3},{2,0},{3,1},{4,20},{5,21},{6,22},{7,23},{8,10},{9,11},... | collective-permute-start | bytes 393224 | tf_op jit(solution)/shard_map/ppermute | solution.py:41
  123.8 5.5 %collective-permute-start.14 = (f32[64,512]{1,0:T(8,128)S(1)}, f32[64,512]{1,0:T(8,128)S(1)}, u32[]{:S(2)}, u32[]{:S(2)}) collective-permute-start(f32[64,512]{1,0:T(8,128)S(1)} %get-tuple-element.25), channel_id=1, source_target_pairs={{0,3},{1,2},{2,1},{3,0},{4,28},{5,29},{6,30},{7,31},{8,11},{9,10},... | collective-permute-start | bytes 393224 | tf_op jit(solution)/shard_map/ppermute | solution.py:41
  129.3 3.9 %collective-permute-start.15 = (f32[64,512]{1,0:T(8,128)S(1)}, f32[64,512]{1,0:T(8,128)S(1)}, u32[]{:S(2)}, u32[]{:S(2)}) collective-permute-start(f32[64,512]{1,0:T(8,128)S(1)} %fusion), channel_id=1, source_target_pairs={{0,8},{1,9},{2,10},{3,11},{4,36},{5,37},{6,38},{7,39},{8,0},{9,1},... | collective-permute-start | bytes 393224 | tf_op jit(solution)/shard_map/ppermute | solution.py:41
  129.8 5.4 %collective-permute-start.16 = (f32[64,512]{1,0:T(8,128)S(1)}, f32[64,512]{1,0:T(8,128)S(1)}, u32[]{:S(2)}, u32[]{:S(2)}) collective-permute-start(f32[64,512]{1,0:T(8,128)S(1)} %fusion), channel_id=1, source_target_pairs={{0,16},{1,17},{2,18},{3,19},{4,68},{5,69},{6,70},{7,71},{8,24},{9,... | collective-permute-start | bytes 393224 | tf_op jit(solution)/shard_map/ppermute | solution.py:41
  131.1 5.8 %collective-permute-start.17 = (f32[64,512]{1,0:T(8,128)S(1)}, f32[64,512]{1,0:T(8,128)S(1)}, u32[]{:S(2)}, u32[]{:S(2)}) collective-permute-start(f32[64,512]{1,0:T(8,128)S(1)} %fusion), channel_id=1, source_target_pairs={{0,24},{1,25},{2,26},{3,27},{4,100},{5,101},{6,102},{7,103},{8,16}... | collective-permute-start | bytes 393224 | tf_op jit(solution)/shard_map/ppermute | solution.py:41
  136.9 3.9 %collective-permute-start.18 = (f32[64,512]{1,0:T(8,128)S(1)}, f32[64,512]{1,0:T(8,128)S(1)}, u32[]{:S(2)}, u32[]{:S(2)}) collective-permute-start(f32[64,512]{1,0:T(8,128)S(1)} %add_add_fusion.1), channel_id=1, source_target_pairs={{0,32},{1,33},{2,34},{3,35},{4,5},{5,4},{6,7},{7,6},{8,40},{9,41},... | collective-permute-start | bytes 393224 | tf_op jit(solution)/shard_map/ppermute | solution.py:41
  137.1 5.7 %collective-permute-start.19 = (f32[64,512]{1,0:T(8,128)S(1)}, f32[64,512]{1,0:T(8,128)S(1)}, u32[]{:S(2)}, u32[]{:S(2)}) collective-permute-start(f32[64,512]{1,0:T(8,128)S(1)} %add_add_fusion.1), channel_id=1, source_target_pairs={{0,64},{1,65},{2,66},{3,67},{4,6},{5,7},{6,4},{7,5},{8,72},{9,73},... | collective-permute-start | bytes 393224 | tf_op jit(solution)/shard_map/ppermute | solution.py:41
  139.0 5.2 %collective-permute-start.20 = (f32[64,512]{1,0:T(8,128)S(1)}, f32[64,512]{1,0:T(8,128)S(1)}, u32[]{:S(2)}, u32[]{:S(2)}) collective-permute-start(f32[64,512]{1,0:T(8,128)S(1)} %add_add_fusion.1), channel_id=1, source_target_pairs={{0,96},{1,97},{2,98},{3,99},{4,7},{5,6},{6,5},{7,4},{8,104},{9,105... | collective-permute-start | bytes 393224 | tf_op jit(solution)/shard_map/ppermute | solution.py:41
  144.3 5.4 %collective-permute-start.21 = (f32[64,512]{1,0:T(8,128)S(1)}, f32[64,512]{1,0:T(8,128)S(1)}, u32[]{:S(2)}, u32[]{:S(2)}) collective-permute-start(f32[64,512]{1,0:T(8,128)S(1)} %get-tuple-element.24), channel_id=1, source_target_pairs={{0,2},{1,3},{2,0},{3,1},{4,20},{5,21},{6,22},{7,23},{8,10},{9,11},... | collective-permute-start | bytes 393224 | tf_op jit(solution)/shard_map/ppermute | solution.py:41
  145.7 5.4 %collective-permute-start.22 = (f32[64,512]{1,0:T(8,128)S(1)}, f32[64,512]{1,0:T(8,128)S(1)}, u32[]{:S(2)}, u32[]{:S(2)}) collective-permute-start(f32[64,512]{1,0:T(8,128)S(1)} %get-tuple-element.24), channel_id=1, source_target_pairs={{0,3},{1,2},{2,1},{3,0},{4,28},{5,29},{6,30},{7,31},{8,11},{9,10},... | collective-permute-start | bytes 393224 | tf_op jit(solution)/shard_map/ppermute | solution.py:41
  146.7 4.4 %collective-permute-start.23 = (f32[64,512]{1,0:T(8,128)S(1)}, f32[64,512]{1,0:T(8,128)S(1)}, u32[]{:S(2)}, u32[]{:S(2)}) collective-permute-start(f32[64,512]{1,0:T(8,128)S(1)} %get-tuple-element.24), channel_id=1, source_target_pairs={{0,1},{1,0},{2,3},{3,2},{4,12},{5,13},{6,14},{7,15},{8,9},{9,8},{1... | collective-permute-start | bytes 393224 | tf_op jit(solution)/shard_map/ppermute | solution.py:41
  151.1 7.4 %collective-permute-start.24 = (f32[256,512]{1,0:T(8,128)S(1)}, f32[256,512]{1,0:T(8,128)S(1)}, u32[]{:S(2)}, u32[]{:S(2)}) collective-permute-start(f32[256,512]{1,0:T(8,128)S(1)} %bitcast.28), channel_id=1, source_target_pairs={{0,4},{1,5},{2,6},{3,7},{4,0},{5,1},{6,2},{7,3},{8,12},{9,13},{10,... | collective-permute-start | bytes 1572872 | tf_op jit(solution)/shard_map/ppermute | solution.py:41
  (3 other events, 85.1 us)

commit v7 on v6

--- a/solution.py
+++ b/solution.py
@@ -125,13 +125,6 @@
     return product(inverse, flat, 1, 0), jnp.sum(weak)
 
 
-def separate_sweeps(gram, start, sweeps):
-    flat = start
-    for sweep in range(sweeps):
-        flat = orthonormal_round(product(flat, gram, 1, 0))[0]
-    return orthonormal_round(flat)[0]
-
-
 def joined_sweeps(gram_ref, start, sweeps, flat_ref):
     gram = gram_ref[...]
     flat = start
@@ -292,13 +285,12 @@
     own = count // half
     ranks = lanes // 2
 
-    def kernel(core_ref, mine_ref, other_ref, start_ref, far_ref, basis_ref, out_ref, group_ref, arrived):
+    def kernel(core_ref, mine_ref, other_ref, start_ref, far_ref, basis_ref, out_ref, group_ref, arrived, held_ref):
         fetch = pltpu.make_async_copy(far_ref, group_ref, arrived)
         fetch.start()
-        gram = join_halves(core_ref, mine_ref, other_ref, scale)
-        flat = separate_sweeps(gram, start_ref[...], ITX)
-        basis_ref[...] = flat
-        narrow = flat.astype(BF16)
+        held_ref[...] = join_halves(core_ref, mine_ref, other_ref, scale)
+        joined_sweeps(held_ref, start_ref[...], ITX, basis_ref)
+        narrow = basis_ref[...].astype(BF16)
         fetch.wait()
         first = lax.broadcasted_iota(jnp.int32, (rank, lanes), 1) < ranks
         for v in range(half):
@@ -319,7 +311,11 @@
             jax.ShapeDtypeStruct((rank, planes), F32),
             jax.ShapeDtypeStruct((2 * half, rank, own * ranks), BF16),
         ],
-        scratch_shapes=[pltpu.VMEM(groups.shape, BF16), pltpu.SemaphoreType.DMA],
+        scratch_shapes=[
+            pltpu.VMEM(groups.shape, BF16),
+            pltpu.SemaphoreType.DMA,
+            pltpu.VMEM((planes, planes), F32),
+        ],
         compiler_params=limit(16),
     )(core, mine, other, start, pltpu.with_memory_space_constraint(groups, pltpu.HBM))
 

time: 167 us -> 173 us (1.036)
  Pallas kernels: 36.9 us -> 42.6 us
    pallas_call x1, Pallas kernels: 8.04 us -> 13.7 us  [plane_subspace(): pl.pallas_call(kernel, in_specs=[SMEM, VMEM, VMEM, VMEM, HBM], out_specs=...]
where the time goes in v7:
time: 173 us; the launch traced here: 172 us
  blocking collectives  56.7 us (33%)
  Pallas kernels  42.6 us (25%)
  starting transfers between devices  41 us (24%)
  waiting for transfers between devices  30.9 us (18%)
    all_to_all x1, blocking collectives, on_device(): lax.all_to_all(core_time, ('blk', 'pen'), split_axis=0, concat_axis=0, ti...  56.7 us
    ppermute x25, starting transfers between devices, swap(): return lax.ppermute(value, ('blk', 'pen'), self.partners(stage, step))  41 us
    ppermute x25, waiting for transfers between devices, swap(): return lax.ppermute(value, ('blk', 'pen'), self.partners(stage, step))  30.9 us
    pallas_call x1, Pallas kernels, time_subspace(): pl.pallas_call(kernel, in_specs=[SMEM, VMEM, VMEM, VMEM], out_specs=[VMEM...  15.9 us
    pallas_call x1, Pallas kernels, plane_subspace(): pl.pallas_call(kernel, in_specs=[SMEM, VMEM, VMEM, VMEM, HBM], out_specs=...  13.7 us
    pallas_call x1, Pallas kernels, time_gram(): pl.pallas_call(kernel, in_specs=[SMEM, HBM], out_specs=[VMEM, VMEM, VMEM]...  6.55 us
    pallas_call x1, Pallas kernels, plane_gram(): pl.pallas_call(kernel, in_specs=[SMEM, VMEM], out_specs=[VMEM, VMEM, HBM]...  4.12 us
  transfers between devices with their start and end apart: 25, of which 19 were waited for; matrix products, arithmetic and copies ran while one was open for 0% of the time, Pallas kernels for 0%

profile of v7, /device:TPU:1, one launch (start us, length us, event | category | flops | bytes accessed | tf_op | source)
XLA Modules:
  0.0 172.4 jit_solution(15883628129902148974)
XLA Ops:
  0.7 6.5 %shard_map.58 = (f32[64,128]{1,0:T(8,128)S(1)}, f32[64,128]{1,0:T(8,128)S(1)}, bf16[32768,128]{1,0:T(8,128)(2,1)S(1)}) custom-call(s32[1]{0:T(128)} %bitcast.core_ref, bf16[32768,128]{1,0:T(8,128)(2,1)} %bitcast.32), custom_call_target="tpu_custom_call" | custom-call | tf_op jit(solution)/shard_map/pallas_call | solution.py:176
  10.9 2.6 %collective-permute-start.2 = (f32[64,128]{1,0:T(8,128)S(1)}, f32[64,128]{1,0:T(8,128)S(1)}, u32[]{:S(2)}, u32[]{:S(2)}) collective-permute-start(f32[64,128]{1,0:T(8,128)S(1)} %add.87), channel_id=1, source_target_pairs={{0,2},{1,3},{2,0},{3,1},{4,20},{5,21},{6,22},{7,23},{8,10},{9,11},... | collective-permute-start | bytes 98312 | tf_op jit(solution)/shard_map/ppermute | solution.py:41
  15.2 2.3 %collective-permute-done.3 = f32[64,128]{1,0:T(8,128)S(1)} collective-permute-done((f32[64,128]{1,0:T(8,128)S(1)}, f32[64,128]{1,0:T(8,128)S(1)}, u32[]{:S(2)}, u32[]{:S(2)}) %collective-permute-start.3) | collective-permute-done | bytes 32800 | tf_op jit(solution)/shard_map/ppermute | solution.py:41
  17.6 1.7 collective-permute-start.4
  19.3 3.3 %collective-permute-start.5 = (f32[64,128]{1,0:T(8,128)S(1)}, f32[64,128]{1,0:T(8,128)S(1)}, u32[]{:S(2)}, u32[]{:S(2)}) collective-permute-start(f32[64,128]{1,0:T(8,128)S(1)} %add_add_fusion.4), channel_id=1, source_target_pairs={{0,16},{1,17},{2,18},{3,19},{4,68},{5,69},{6,70},{7,71},{8,24},{9,... | collective-permute-start | bytes 98312 | tf_op jit(solution)/shard_map/ppermute | solution.py:41
  24.2 2.3 %collective-permute-done.6 = f32[64,128]{1,0:T(8,128)S(1)} collective-permute-done((f32[64,128]{1,0:T(8,128)S(1)}, f32[64,128]{1,0:T(8,128)S(1)}, u32[]{:S(2)}, u32[]{:S(2)}) %collective-permute-start.6) | collective-permute-done | bytes 32800 | tf_op jit(solution)/shard_map/ppermute | solution.py:41
  27.9 2.5 %collective-permute-start.8 = (f32[64,128]{1,0:T(8,128)S(1)}, f32[64,128]{1,0:T(8,128)S(1)}, u32[]{:S(2)}, u32[]{:S(2)}) collective-permute-start(f32[64,128]{1,0:T(8,128)S(1)} %add_add_fusion.3), channel_id=1, source_target_pairs={{0,64},{1,65},{2,66},{3,67},{4,6},{5,7},{6,4},{7,5},{8,72},{9,73},... | collective-permute-start | bytes 98312 | tf_op jit(solution)/shard_map/ppermute | solution.py:41
  32.1 2.2 %collective-permute-done.9 = f32[64,128]{1,0:T(8,128)S(1)} collective-permute-done((f32[64,128]{1,0:T(8,128)S(1)}, f32[64,128]{1,0:T(8,128)S(1)}, u32[]{:S(2)}, u32[]{:S(2)}) %collective-permute-start.9) | collective-permute-done | bytes 32800 | tf_op jit(solution)/shard_map/ppermute | solution.py:41
  34.3 5.6 %collective-permute-start.10 = (f32[64,128]{1,0:T(8,128)S(1)}, f32[64,128]{1,0:T(8,128)S(1)}, u32[]{:S(2)}, u32[]{:S(2)}) collective-permute-start(f32[64,128]{1,0:T(8,128)S(1)} %add_add_fusion.2.mine_ref), channel_id=1, source_target_pairs={{0,4},{1,5},{2,6},{3,7},{4,0},{5,1},{6,2},{7,3},{8,12},{9,13},{10,... | collective-permute-start | bytes 98312 | tf_op jit(solution)/shard_map/ppermute | solution.py:41
  40.7 15.9 %shard_map.59 = (f32[64,128]{1,0:T(8,128)}, bf16[256,128]{1,0:T(8,128)(2,1)S(1)}) custom-call(s32[1]{0:T(128)} %bitcast.core_ref, f32[64,128]{1,0:T(8,128)S(1)} %add_add_fusion.2.mine_ref, f32[64,128]{1,0:T(8,128)S(1)} %collective-permute-done.10.other_ref, f32[64,128]{1,0:T(8,128)S(1)} %bitcast.31), custom_call_target="tpu_custom_call" | custom-call | tf_op jit(solution)/shard_map/pallas_call | solution.py:210
  56.6 2.3 %shard_map.60 = bf16[128,4,2,16,128]{4,3,2,1,0:T(8,128)(2,1)S(1)} custom-call(bf16[32768,128]{1,0:T(8,128)(2,1)S(1)} %get-tuple-element.16.near_ref, bf16[256,128]{1,0:T(8,128)(2,1)S(1)} %get-tuple-element.17.basis_ref), custom_call_target="tpu_custom_call" | custom-call | tf_op jit(solution)/shard_map/pallas_call | solution.py:240
  58.9 56.7 %all_to_all.5 = bf16[128,4,2,16,128]{4,3,2,1,0:T(8,128)(2,1)S(1)} all-to-all(bf16[128,4,2,16,128]{4,3,2,1,0:T(8,128)(2,1)S(1)} %shard_map.60), channel_id=1, replica_groups=mesh['blk'=32,'pen'=4] {'blk','pen'}, dimensions={0} | all-to-all | bytes 8388608 | tf_op jit(solution)/shard_map/all_to_all | solution.py:341
  115.6 4.1 %shard_map.61 = (f32[256,512]{1,0:T(8,128)S(1)}, f32[256,512]{1,0:T(8,128)S(1)}, bf16[32,512,128]{2,1,0:T(8,128)(2,1)}) custom-call(s32[1]{0:T(128)} %bitcast.core_ref, bf16[512,32,128]{2,1,0:T(8,128)(2,1)S(1)} %bitcast.27), custom_call_target="tpu_custom_call" | custom-call | tf_op jit(solution)/shard_map/pallas_call | solution.py:269
  122.1 1.7 collective-permute-start.13
  123.8 2.1 %collective-permute-start.14 = (f32[64,512]{1,0:T(8,128)S(1)}, f32[64,512]{1,0:T(8,128)S(1)}, u32[]{:S(2)}, u32[]{:S(2)}) collective-permute-start(f32[64,512]{1,0:T(8,128)S(1)} %get-tuple-element.25), channel_id=1, source_target_pairs={{0,3},{1,2},{2,1},{3,0},{4,28},{5,29},{6,30},{7,31},{8,11},{9,10},... | collective-permute-start | bytes 393224 | tf_op jit(solution)/shard_map/ppermute | solution.py:41
  126.1 1.7 %collective-permute-done.13 = f32[64,512]{1,0:T(8,128)S(1)} collective-permute-done((f32[64,512]{1,0:T(8,128)S(1)}, f32[64,512]{1,0:T(8,128)S(1)}, u32[]{:S(2)}, u32[]{:S(2)}) %collective-permute-start.13) | collective-permute-done | bytes 131104 | tf_op jit(solution)/shard_map/ppermute | solution.py:41
  131.1 2.2 %collective-permute-start.17 = (f32[64,512]{1,0:T(8,128)S(1)}, f32[64,512]{1,0:T(8,128)S(1)}, u32[]{:S(2)}, u32[]{:S(2)}) collective-permute-start(f32[64,512]{1,0:T(8,128)S(1)} %fusion), channel_id=1, source_target_pairs={{0,24},{1,25},{2,26},{3,27},{4,100},{5,101},{6,102},{7,103},{8,16}... | collective-permute-start | bytes 393224 | tf_op jit(solution)/shard_map/ppermute | solution.py:41
  133.2 1.9 %collective-permute-done.16 = f32[64,512]{1,0:T(8,128)S(1)} collective-permute-done((f32[64,512]{1,0:T(8,128)S(1)}, f32[64,512]{1,0:T(8,128)S(1)}, u32[]{:S(2)}, u32[]{:S(2)}) %collective-permute-start.16) | collective-permute-done | bytes 131104 | tf_op jit(solution)/shard_map/ppermute | solution.py:41
  137.1 1.9 %collective-permute-start.19 = (f32[64,512]{1,0:T(8,128)S(1)}, f32[64,512]{1,0:T(8,128)S(1)}, u32[]{:S(2)}, u32[]{:S(2)}) collective-permute-start(f32[64,512]{1,0:T(8,128)S(1)} %add_add_fusion.1), channel_id=1, source_target_pairs={{0,64},{1,65},{2,66},{3,67},{4,6},{5,7},{6,4},{7,5},{8,72},{9,73},... | collective-permute-start | bytes 393224 | tf_op jit(solution)/shard_map/ppermute | solution.py:41
  139.0 1.8 %collective-permute-start.20 = (f32[64,512]{1,0:T(8,128)S(1)}, f32[64,512]{1,0:T(8,128)S(1)}, u32[]{:S(2)}, u32[]{:S(2)}) collective-permute-start(f32[64,512]{1,0:T(8,128)S(1)} %add_add_fusion.1), channel_id=1, source_target_pairs={{0,96},{1,97},{2,98},{3,99},{4,7},{5,6},{6,5},{7,4},{8,104},{9,105... | collective-permute-start | bytes 393224 | tf_op jit(solution)/shard_map/ppermute | solution.py:41
  140.8 2.0 %collective-permute-done.19 = f32[64,512]{1,0:T(8,128)S(1)} collective-permute-done((f32[64,512]{1,0:T(8,128)S(1)}, f32[64,512]{1,0:T(8,128)S(1)}, u32[]{:S(2)}, u32[]{:S(2)}) %collective-permute-start.19) | collective-permute-done | bytes 131104 | tf_op jit(solution)/shard_map/ppermute | solution.py:41
  147.0 2.7 %collective-permute-done.21 = f32[64,512]{1,0:T(8,128)S(1)} collective-permute-done((f32[64,512]{1,0:T(8,128)S(1)}, f32[64,512]{1,0:T(8,128)S(1)}, u32[]{:S(2)}, u32[]{:S(2)}) %collective-permute-start.21) | collective-permute-done | bytes 131104 | tf_op jit(solution)/shard_map/ppermute | solution.py:41
  151.1 5.8 %collective-permute-start.24 = (f32[256,512]{1,0:T(8,128)S(1)}, f32[256,512]{1,0:T(8,128)S(1)}, u32[]{:S(2)}, u32[]{:S(2)}) collective-permute-start(f32[256,512]{1,0:T(8,128)S(1)} %bitcast.28), channel_id=1, source_target_pairs={{0,4},{1,5},{2,6},{3,7},{4,0},{5,1},{6,2},{7,3},{8,12},{9,13},{10,... | collective-permute-start | bytes 1572872 | tf_op jit(solution)/shard_map/ppermute | solution.py:41
  158.5 13.7 %shard_map.62 = (f32[32,512]{1,0:T(8,128)}, bf16[4,32,1024]{2,1,0:T(8,128)(2,1)}) custom-call(s32[1]{0:T(128)} %bitcast.core_ref, f32[256,512]{1,0:T(8,128)S(1)} %bitcast.29, f32[256,512]{1,0:T(8,128)S(1)} %collective-permute-done.24.other_ref, f32[32,512]{1,0:T(8,128)S(1)} %bitcast.30, bf16[32,512,128]{2,1,0:T(8,128)(2,1)} %get-tuple-element.20.far_ref), custom_call_target="tpu_custom_call" | custom-call | tf_op jit(solution)/shard_map/pallas_call | solution.py:306
  (49 shorter events, 25.9 us)
Async XLA Ops:
  7.2 2.3 %collective-permute-start = (f32[64,128]{1,0:T(8,128)S(1)}, f32[64,128]{1,0:T(8,128)S(1)}, u32[]{:S(2)}, u32[]{:S(2)}) collective-permute-start(f32[64,128]{1,0:T(8,128)S(1)} %get-tuple-element.14), channel_id=1, source_target_pairs={{0,4},{1,5},{2,6},{3,7},{4,0},{5,1},{6,2},{7,3},{8,12},{9,13},{10,... | collective-permute-start | bytes 98312 | tf_op jit(solution)/shard_map/ppermute | solution.py:41
  9.5 4.0 %collective-permute-start.1 = (f32[64,128]{1,0:T(8,128)S(1)}, f32[64,128]{1,0:T(8,128)S(1)}, u32[]{:S(2)}, u32[]{:S(2)}) collective-permute-start(f32[64,128]{1,0:T(8,128)S(1)} %add.87), channel_id=1, source_target_pairs={{0,1},{1,0},{2,3},{3,2},{4,12},{5,13},{6,14},{7,15},{8,9},{9,8},{1... | collective-permute-start | bytes 98312 | tf_op jit(solution)/shard_map/ppermute | solution.py:41
  10.9 4.3 %collective-permute-start.2 = (f32[64,128]{1,0:T(8,128)S(1)}, f32[64,128]{1,0:T(8,128)S(1)}, u32[]{:S(2)}, u32[]{:S(2)}) collective-permute-start(f32[64,128]{1,0:T(8,128)S(1)} %add.87), channel_id=1, source_target_pairs={{0,2},{1,3},{2,0},{3,1},{4,20},{5,21},{6,22},{7,23},{8,10},{9,11},... | collective-permute-start | bytes 98312 | tf_op jit(solution)/shard_map/ppermute | solution.py:41
  13.6 4.0 %collective-permute-start.3 = (f32[64,128]{1,0:T(8,128)S(1)}, f32[64,128]{1,0:T(8,128)S(1)}, u32[]{:S(2)}, u32[]{:S(2)}) collective-permute-start(f32[64,128]{1,0:T(8,128)S(1)} %add.87), channel_id=1, source_target_pairs={{0,3},{1,2},{2,1},{3,0},{4,28},{5,29},{6,30},{7,31},{8,11},{9,10},... | collective-permute-start | bytes 98312 | tf_op jit(solution)/shard_map/ppermute | solution.py:41
  17.6 5.0 %collective-permute-start.4 = (f32[64,128]{1,0:T(8,128)S(1)}, f32[64,128]{1,0:T(8,128)S(1)}, u32[]{:S(2)}, u32[]{:S(2)}) collective-permute-start(f32[64,128]{1,0:T(8,128)S(1)} %add_add_fusion.4), channel_id=1, source_target_pairs={{0,8},{1,9},{2,10},{3,11},{4,36},{5,37},{6,38},{7,39},{8,0},{9,1},... | collective-permute-start | bytes 98312 | tf_op jit(solution)/shard_map/ppermute | solution.py:41
  19.3 5.0 %collective-permute-start.5 = (f32[64,128]{1,0:T(8,128)S(1)}, f32[64,128]{1,0:T(8,128)S(1)}, u32[]{:S(2)}, u32[]{:S(2)}) collective-permute-start(f32[64,128]{1,0:T(8,128)S(1)} %add_add_fusion.4), channel_id=1, source_target_pairs={{0,16},{1,17},{2,18},{3,19},{4,68},{5,69},{6,70},{7,71},{8,24},{9,... | collective-permute-start | bytes 98312 | tf_op jit(solution)/shard_map/ppermute | solution.py:41
  22.6 4.0 %collective-permute-start.6 = (f32[64,128]{1,0:T(8,128)S(1)}, f32[64,128]{1,0:T(8,128)S(1)}, u32[]{:S(2)}, u32[]{:S(2)}) collective-permute-start(f32[64,128]{1,0:T(8,128)S(1)} %add_add_fusion.4), channel_id=1, source_target_pairs={{0,24},{1,25},{2,26},{3,27},{4,100},{5,101},{6,102},{7,103},{8,16}... | collective-permute-start | bytes 98312 | tf_op jit(solution)/shard_map/ppermute | solution.py:41
  26.6 3.9 %collective-permute-start.7 = (f32[64,128]{1,0:T(8,128)S(1)}, f32[64,128]{1,0:T(8,128)S(1)}, u32[]{:S(2)}, u32[]{:S(2)}) collective-permute-start(f32[64,128]{1,0:T(8,128)S(1)} %add_add_fusion.3), channel_id=1, source_target_pairs={{0,32},{1,33},{2,34},{3,35},{4,5},{5,4},{6,7},{7,6},{8,40},{9,41},... | collective-permute-start | bytes 98312 | tf_op jit(solution)/shard_map/ppermute | solution.py:41
  27.9 4.3 %collective-permute-start.8 = (f32[64,128]{1,0:T(8,128)S(1)}, f32[64,128]{1,0:T(8,128)S(1)}, u32[]{:S(2)}, u32[]{:S(2)}) collective-permute-start(f32[64,128]{1,0:T(8,128)S(1)} %add_add_fusion.3), channel_id=1, source_target_pairs={{0,64},{1,65},{2,66},{3,67},{4,6},{5,7},{6,4},{7,5},{8,72},{9,73},... | collective-permute-start | bytes 98312 | tf_op jit(solution)/shard_map/ppermute | solution.py:41
  30.3 4.0 %collective-permute-start.9 = (f32[64,128]{1,0:T(8,128)S(1)}, f32[64,128]{1,0:T(8,128)S(1)}, u32[]{:S(2)}, u32[]{:S(2)}) collective-permute-start(f32[64,128]{1,0:T(8,128)S(1)} %add_add_fusion.3), channel_id=1, source_target_pairs={{0,96},{1,97},{2,98},{3,99},{4,7},{5,6},{6,5},{7,4},{8,104},{9,105... | collective-permute-start | bytes 98312 | tf_op jit(solution)/shard_map/ppermute | solution.py:41
  34.3 6.4 %collective-permute-start.10 = (f32[64,128]{1,0:T(8,128)S(1)}, f32[64,128]{1,0:T(8,128)S(1)}, u32[]{:S(2)}, u32[]{:S(2)}) collective-permute-start(f32[64,128]{1,0:T(8,128)S(1)} %add_add_fusion.2.mine_ref), channel_id=1, source_target_pairs={{0,4},{1,5},{2,6},{3,7},{4,0},{5,1},{6,2},{7,3},{8,12},{9,13},{10,... | collective-permute-start | bytes 98312 | tf_op jit(solution)/shard_map/ppermute | solution.py:41
  121.9 4.2 %collective-permute-start.12 = (f32[64,512]{1,0:T(8,128)S(1)}, f32[64,512]{1,0:T(8,128)S(1)}, u32[]{:S(2)}, u32[]{:S(2)}) collective-permute-start(f32[64,512]{1,0:T(8,128)S(1)} %get-tuple-element.27), channel_id=1, source_target_pairs={{0,1},{1,0},{2,3},{3,2},{4,12},{5,13},{6,14},{7,15},{8,9},{9,8},{1... | collective-permute-start | bytes 393224 | tf_op jit(solution)/shard_map/ppermute | solution.py:41
  122.1 5.8 %collective-permute-start.13 = (f32[64,512]{1,0:T(8,128)S(1)}, f32[64,512]{1,0:T(8,128)S(1)}, u32[]{:S(2)}, u32[]{:S(2)}) collective-permute-start(f32[64,512]{1,0:T(8,128)S(1)} %get-tuple-element.26), channel_id=1, source_target_pairs={{0,2},{1,3},{2,0},{3,1},{4,20},{5,21},{6,22},{7,23},{8,10},{9,11},... | collective-permute-start | bytes 393224 | tf_op jit(solution)/shard_map/ppermute | solution.py:41
  123.8 5.5 %collective-permute-start.14 = (f32[64,512]{1,0:T(8,128)S(1)}, f32[64,512]{1,0:T(8,128)S(1)}, u32[]{:S(2)}, u32[]{:S(2)}) collective-permute-start(f32[64,512]{1,0:T(8,128)S(1)} %get-tuple-element.25), channel_id=1, source_target_pairs={{0,3},{1,2},{2,1},{3,0},{4,28},{5,29},{6,30},{7,31},{8,11},{9,10},... | collective-permute-start | bytes 393224 | tf_op jit(solution)/shard_map/ppermute | solution.py:41
  129.3 3.9 %collective-permute-start.15 = (f32[64,512]{1,0:T(8,128)S(1)}, f32[64,512]{1,0:T(8,128)S(1)}, u32[]{:S(2)}, u32[]{:S(2)}) collective-permute-start(f32[64,512]{1,0:T(8,128)S(1)} %fusion), channel_id=1, source_target_pairs={{0,8},{1,9},{2,10},{3,11},{4,36},{5,37},{6,38},{7,39},{8,0},{9,1},... | collective-permute-start | bytes 393224 | tf_op jit(solution)/shard_map/ppermute | solution.py:41
  129.8 5.4 %collective-permute-start.16 = (f32[64,512]{1,0:T(8,128)S(1)}, f32[64,512]{1,0:T(8,128)S(1)}, u32[]{:S(2)}, u32[]{:S(2)}) collective-permute-start(f32[64,512]{1,0:T(8,128)S(1)} %fusion), channel_id=1, source_target_pairs={{0,16},{1,17},{2,18},{3,19},{4,68},{5,69},{6,70},{7,71},{8,24},{9,... | collective-permute-start | bytes 393224 | tf_op jit(solution)/shard_map/ppermute | solution.py:41
  131.1 5.8 %collective-permute-start.17 = (f32[64,512]{1,0:T(8,128)S(1)}, f32[64,512]{1,0:T(8,128)S(1)}, u32[]{:S(2)}, u32[]{:S(2)}) collective-permute-start(f32[64,512]{1,0:T(8,128)S(1)} %fusion), channel_id=1, source_target_pairs={{0,24},{1,25},{2,26},{3,27},{4,100},{5,101},{6,102},{7,103},{8,16}... | collective-permute-start | bytes 393224 | tf_op jit(solution)/shard_map/ppermute | solution.py:41
  136.9 3.9 %collective-permute-start.18 = (f32[64,512]{1,0:T(8,128)S(1)}, f32[64,512]{1,0:T(8,128)S(1)}, u32[]{:S(2)}, u32[]{:S(2)}) collective-permute-start(f32[64,512]{1,0:T(8,128)S(1)} %add_add_fusion.1), channel_id=1, source_target_pairs={{0,32},{1,33},{2,34},{3,35},{4,5},{5,4},{6,7},{7,6},{8,40},{9,41},... | collective-permute-start | bytes 393224 | tf_op jit(solution)/shard_map/ppermute | solution.py:41
  137.1 5.7 %collective-permute-start.19 = (f32[64,512]{1,0:T(8,128)S(1)}, f32[64,512]{1,0:T(8,128)S(1)}, u32[]{:S(2)}, u32[]{:S(2)}) collective-permute-start(f32[64,512]{1,0:T(8,128)S(1)} %add_add_fusion.1), channel_id=1, source_target_pairs={{0,64},{1,65},{2,66},{3,67},{4,6},{5,7},{6,4},{7,5},{8,72},{9,73},... | collective-permute-start | bytes 393224 | tf_op jit(solution)/shard_map/ppermute | solution.py:41
  139.0 5.2 %collective-permute-start.20 = (f32[64,512]{1,0:T(8,128)S(1)}, f32[64,512]{1,0:T(8,128)S(1)}, u32[]{:S(2)}, u32[]{:S(2)}) collective-permute-start(f32[64,512]{1,0:T(8,128)S(1)} %add_add_fusion.1), channel_id=1, source_target_pairs={{0,96},{1,97},{2,98},{3,99},{4,7},{5,6},{6,5},{7,4},{8,104},{9,105... | collective-permute-start | bytes 393224 | tf_op jit(solution)/shard_map/ppermute | solution.py:41
  144.3 5.4 %collective-permute-start.21 = (f32[64,512]{1,0:T(8,128)S(1)}, f32[64,512]{1,0:T(8,128)S(1)}, u32[]{:S(2)}, u32[]{:S(2)}) collective-permute-start(f32[64,512]{1,0:T(8,128)S(1)} %get-tuple-element.24), channel_id=1, source_target_pairs={{0,2},{1,3},{2,0},{3,1},{4,20},{5,21},{6,22},{7,23},{8,10},{9,11},... | collective-permute-start | bytes 393224 | tf_op jit(solution)/shard_map/ppermute | solution.py:41
  145.7 5.4 %collective-permute-start.22 = (f32[64,512]{1,0:T(8,128)S(1)}, f32[64,512]{1,0:T(8,128)S(1)}, u32[]{:S(2)}, u32[]{:S(2)}) collective-permute-start(f32[64,512]{1,0:T(8,128)S(1)} %get-tuple-element.24), channel_id=1, source_target_pairs={{0,3},{1,2},{2,1},{3,0},{4,28},{5,29},{6,30},{7,31},{8,11},{9,10},... | collective-permute-start | bytes 393224 | tf_op jit(solution)/shard_map/ppermute | solution.py:41
  146.7 4.4 %collective-permute-start.23 = (f32[64,512]{1,0:T(8,128)S(1)}, f32[64,512]{1,0:T(8,128)S(1)}, u32[]{:S(2)}, u32[]{:S(2)}) collective-permute-start(f32[64,512]{1,0:T(8,128)S(1)} %get-tuple-element.24), channel_id=1, source_target_pairs={{0,1},{1,0},{2,3},{3,2},{4,12},{5,13},{6,14},{7,15},{8,9},{9,8},{1... | collective-permute-start | bytes 393224 | tf_op jit(solution)/shard_map/ppermute | solution.py:41
  151.1 7.4 %collective-permute-start.24 = (f32[256,512]{1,0:T(8,128)S(1)}, f32[256,512]{1,0:T(8,128)S(1)}, u32[]{:S(2)}, u32[]{:S(2)}) collective-permute-start(f32[256,512]{1,0:T(8,128)S(1)} %bitcast.28), channel_id=1, source_target_pairs={{0,4},{1,5},{2,6},{3,7},{4,0},{5,1},{6,2},{7,3},{8,12},{9,13},{10,... | collective-permute-start | bytes 1572872 | tf_op jit(solution)/shard_map/ppermute | solution.py:41
  (3 other events, 85.1 us)

commit v8 on v7

--- a/solution.py
+++ b/solution.py
@@ -17,7 +17,7 @@
 
 
 class Torus:
-    orders = ("xyz", "yzx")
+    orders = ("xyz", "zxy")
     steps = (2, 3, 1)
 
     def __init__(self):

time: 173 us -> 173 us (level)
  no operation moved by 1% of the time
where the time goes in v8:
time: 173 us
  blocking collectives  56.7 us (33%)
  Pallas kernels  42.6 us (25%)
  starting transfers between devices  40.9 us (24%)
  waiting for transfers between devices  31.2 us (18%)
    all_to_all x1, blocking collectives, on_device(): lax.all_to_all(core_time, ('blk', 'pen'), split_axis=0, concat_axis=0, ti...  56.7 us
    ppermute x25, starting transfers between devices, swap(): return lax.ppermute(value, ('blk', 'pen'), self.partners(stage, step))  40.9 us
    ppermute x25, waiting for transfers between devices, swap(): return lax.ppermute(value, ('blk', 'pen'), self.partners(stage, step))  31.2 us
    pallas_call x1, Pallas kernels, time_subspace(): pl.pallas_call(kernel, in_specs=[SMEM, VMEM, VMEM, VMEM], out_specs=[VMEM...  15.9 us
    pallas_call x1, Pallas kernels, plane_subspace(): pl.pallas_call(kernel, in_specs=[SMEM, VMEM, VMEM, VMEM, HBM], out_specs=...  13.7 us
    pallas_call x1, Pallas kernels, time_gram(): pl.pallas_call(kernel, in_specs=[SMEM, HBM], out_specs=[VMEM, VMEM, VMEM]...  6.55 us
    pallas_call x1, Pallas kernels, plane_gram(): pl.pallas_call(kernel, in_specs=[SMEM, VMEM], out_specs=[VMEM, VMEM, HBM]...  4.12 us
  transfers between devices with their start and end apart: 25, of which 19 were waited for; matrix products, arithmetic and copies ran while one was open for 0% of the time, Pallas kernels for 0%

profile of v8, /device:TPU:1, one launch (start us, length us, event | category | flops | bytes accessed | tf_op | source)
XLA Modules:
  0.0 172.6 jit_solution(2366700633401053337)
XLA Ops:
  0.7 6.5 %shard_map.58 = (f32[64,128]{1,0:T(8,128)S(1)}, f32[64,128]{1,0:T(8,128)S(1)}, bf16[32768,128]{1,0:T(8,128)(2,1)S(1)}) custom-call(s32[1]{0:T(128)} %bitcast.core_ref, bf16[32768,128]{1,0:T(8,128)(2,1)} %bitcast.32), custom_call_target="tpu_custom_call" | custom-call | tf_op jit(solution)/shard_map/pallas_call | solution.py:176
  9.5 1.7 %collective-permute-start.1 = (f32[64,128]{1,0:T(8,128)S(1)}, f32[64,128]{1,0:T(8,128)S(1)}, u32[]{:S(2)}, u32[]{:S(2)}) collective-permute-start(f32[64,128]{1,0:T(8,128)S(1)} %add.84), channel_id=1, source_target_pairs={{0,1},{1,0},{2,3},{3,2},{4,36},{5,37},{6,38},{7,39},{8,9},{9,8},{1... | collective-permute-start | bytes 98312 | tf_op jit(solution)/shard_map/ppermute | solution.py:41
  11.3 3.3 %collective-permute-start.2 = (f32[64,128]{1,0:T(8,128)S(1)}, f32[64,128]{1,0:T(8,128)S(1)}, u32[]{:S(2)}, u32[]{:S(2)}) collective-permute-start(f32[64,128]{1,0:T(8,128)S(1)} %add.84), channel_id=1, source_target_pairs={{0,2},{1,3},{2,0},{3,1},{4,68},{5,69},{6,70},{7,71},{8,10},{9,11},... | collective-permute-start | bytes 98312 | tf_op jit(solution)/shard_map/ppermute | solution.py:41
  14.6 1.9 %collective-permute-done.2 = f32[64,128]{1,0:T(8,128)S(1)} collective-permute-done((f32[64,128]{1,0:T(8,128)S(1)}, f32[64,128]{1,0:T(8,128)S(1)}, u32[]{:S(2)}, u32[]{:S(2)}) %collective-permute-start.2) | collective-permute-done | bytes 32800 | tf_op jit(solution)/shard_map/ppermute | solution.py:41
  16.5 2.3 %collective-permute-done.3 = f32[64,128]{1,0:T(8,128)S(1)} collective-permute-done((f32[64,128]{1,0:T(8,128)S(1)}, f32[64,128]{1,0:T(8,128)S(1)}, u32[]{:S(2)}, u32[]{:S(2)}) %collective-permute-start.3) | collective-permute-done | bytes 32800 | tf_op jit(solution)/shard_map/ppermute | solution.py:41
  19.9 2.5 %collective-permute-start.5 = (f32[64,128]{1,0:T(8,128)S(1)}, f32[64,128]{1,0:T(8,128)S(1)}, u32[]{:S(2)}, u32[]{:S(2)}) collective-permute-start(f32[64,128]{1,0:T(8,128)S(1)} %add_add_fusion.4), channel_id=1, source_target_pairs={{0,16},{1,17},{2,18},{3,19},{4,6},{5,7},{6,4},{7,5},{8,24},{9,25},... | collective-permute-start | bytes 98312 | tf_op jit(solution)/shard_map/ppermute | solution.py:41
  24.1 2.2 %collective-permute-done.6 = f32[64,128]{1,0:T(8,128)S(1)} collective-permute-done((f32[64,128]{1,0:T(8,128)S(1)}, f32[64,128]{1,0:T(8,128)S(1)}, u32[]{:S(2)}, u32[]{:S(2)}) %collective-permute-start.6) | collective-permute-done | bytes 32800 | tf_op jit(solution)/shard_map/ppermute | solution.py:41
  27.7 2.6 %collective-permute-start.8 = (f32[64,128]{1,0:T(8,128)S(1)}, f32[64,128]{1,0:T(8,128)S(1)}, u32[]{:S(2)}, u32[]{:S(2)}) collective-permute-start(f32[64,128]{1,0:T(8,128)S(1)} %add_add_fusion.3), channel_id=1, source_target_pairs={{0,64},{1,65},{2,66},{3,67},{4,20},{5,21},{6,22},{7,23},{8,72},{9,... | collective-permute-start | bytes 98312 | tf_op jit(solution)/shard_map/ppermute | solution.py:41
  30.3 1.6 collective-permute-done.8
  32.0 2.3 %collective-permute-done.9 = f32[64,128]{1,0:T(8,128)S(1)} collective-permute-done((f32[64,128]{1,0:T(8,128)S(1)}, f32[64,128]{1,0:T(8,128)S(1)}, u32[]{:S(2)}, u32[]{:S(2)}) %collective-permute-start.9) | collective-permute-done | bytes 32800 | tf_op jit(solution)/shard_map/ppermute | solution.py:41
  34.3 5.8 %collective-permute-start.10 = (f32[64,128]{1,0:T(8,128)S(1)}, f32[64,128]{1,0:T(8,128)S(1)}, u32[]{:S(2)}, u32[]{:S(2)}) collective-permute-start(f32[64,128]{1,0:T(8,128)S(1)} %add_add_fusion.2.mine_ref), channel_id=1, source_target_pairs={{0,4},{1,5},{2,6},{3,7},{4,0},{5,1},{6,2},{7,3},{8,12},{9,13},{10,... | collective-permute-start | bytes 98312 | tf_op jit(solution)/shard_map/ppermute | solution.py:41
  40.9 15.9 %shard_map.59 = (f32[64,128]{1,0:T(8,128)}, bf16[256,128]{1,0:T(8,128)(2,1)S(1)}) custom-call(s32[1]{0:T(128)} %bitcast.core_ref, f32[64,128]{1,0:T(8,128)S(1)} %add_add_fusion.2.mine_ref, f32[64,128]{1,0:T(8,128)S(1)} %collective-permute-done.10.other_ref, f32[64,128]{1,0:T(8,128)S(1)} %bitcast.31), custom_call_target="tpu_custom_call" | custom-call | tf_op jit(solution)/shard_map/pallas_call | solution.py:210
  56.8 2.3 %shard_map.60 = bf16[128,4,2,16,128]{4,3,2,1,0:T(8,128)(2,1)S(1)} custom-call(bf16[32768,128]{1,0:T(8,128)(2,1)S(1)} %get-tuple-element.16.near_ref, bf16[256,128]{1,0:T(8,128)(2,1)S(1)} %get-tuple-element.17.basis_ref), custom_call_target="tpu_custom_call" | custom-call | tf_op jit(solution)/shard_map/pallas_call | solution.py:240
  59.1 56.7 %all_to_all.5 = bf16[128,4,2,16,128]{4,3,2,1,0:T(8,128)(2,1)S(1)} all-to-all(bf16[128,4,2,16,128]{4,3,2,1,0:T(8,128)(2,1)S(1)} %shard_map.60), channel_id=1, replica_groups=mesh['blk'=32,'pen'=4] {'blk','pen'}, dimensions={0} | all-to-all | bytes 8388608 | tf_op jit(solution)/shard_map/all_to_all | solution.py:341
  115.8 4.1 %shard_map.61 = (f32[256,512]{1,0:T(8,128)S(1)}, f32[256,512]{1,0:T(8,128)S(1)}, bf16[32,512,128]{2,1,0:T(8,128)(2,1)}) custom-call(s32[1]{0:T(128)} %bitcast.core_ref, bf16[512,32,128]{2,1,0:T(8,128)(2,1)S(1)} %bitcast.27), custom_call_target="tpu_custom_call" | custom-call | tf_op jit(solution)/shard_map/pallas_call | solution.py:269
  124.0 2.0 %collective-permute-start.14 = (f32[64,512]{1,0:T(8,128)S(1)}, f32[64,512]{1,0:T(8,128)S(1)}, u32[]{:S(2)}, u32[]{:S(2)}) collective-permute-start(f32[64,512]{1,0:T(8,128)S(1)} %get-tuple-element.25), channel_id=1, source_target_pairs={{0,3},{1,2},{2,1},{3,0},{4,100},{5,101},{6,102},{7,103},{8,11},{9,... | collective-permute-start | bytes 393224 | tf_op jit(solution)/shard_map/ppermute | solution.py:41
  126.3 2.1 %collective-permute-done.13 = f32[64,512]{1,0:T(8,128)S(1)} collective-permute-done((f32[64,512]{1,0:T(8,128)S(1)}, f32[64,512]{1,0:T(8,128)S(1)}, u32[]{:S(2)}, u32[]{:S(2)}) %collective-permute-start.13) | collective-permute-done | bytes 131104 | tf_op jit(solution)/shard_map/ppermute | solution.py:41
  129.8 2.4 %collective-permute-start.16 = (f32[64,512]{1,0:T(8,128)S(1)}, f32[64,512]{1,0:T(8,128)S(1)}, u32[]{:S(2)}, u32[]{:S(2)}) collective-permute-start(f32[64,512]{1,0:T(8,128)S(1)} %fusion), channel_id=1, source_target_pairs={{0,16},{1,17},{2,18},{3,19},{4,6},{5,7},{6,4},{7,5},{8,24},{9,25},... | collective-permute-start | bytes 393224 | tf_op jit(solution)/shard_map/ppermute | solution.py:41
  133.5 2.5 %collective-permute-done.16 = f32[64,512]{1,0:T(8,128)S(1)} collective-permute-done((f32[64,512]{1,0:T(8,128)S(1)}, f32[64,512]{1,0:T(8,128)S(1)}, u32[]{:S(2)}, u32[]{:S(2)}) %collective-permute-start.16) | collective-permute-done | bytes 131104 | tf_op jit(solution)/shard_map/ppermute | solution.py:41
  136.0 1.7 collective-permute-done.17
  138.5 3.2 %collective-permute-start.20 = (f32[64,512]{1,0:T(8,128)S(1)}, f32[64,512]{1,0:T(8,128)S(1)}, u32[]{:S(2)}, u32[]{:S(2)}) collective-permute-start(f32[64,512]{1,0:T(8,128)S(1)} %add_add_fusion.1), channel_id=1, source_target_pairs={{0,96},{1,97},{2,98},{3,99},{4,28},{5,29},{6,30},{7,31},{8,104},{9... | collective-permute-start | bytes 393224 | tf_op jit(solution)/shard_map/ppermute | solution.py:41
  147.5 2.7 %collective-permute-done.21 = f32[64,512]{1,0:T(8,128)S(1)} collective-permute-done((f32[64,512]{1,0:T(8,128)S(1)}, f32[64,512]{1,0:T(8,128)S(1)}, u32[]{:S(2)}, u32[]{:S(2)}) %collective-permute-start.21) | collective-permute-done | bytes 131104 | tf_op jit(solution)/shard_map/ppermute | solution.py:41
  151.6 5.6 %collective-permute-start.24 = (f32[256,512]{1,0:T(8,128)S(1)}, f32[256,512]{1,0:T(8,128)S(1)}, u32[]{:S(2)}, u32[]{:S(2)}) collective-permute-start(f32[256,512]{1,0:T(8,128)S(1)} %bitcast.28), channel_id=1, source_target_pairs={{0,4},{1,5},{2,6},{3,7},{4,0},{5,1},{6,2},{7,3},{8,12},{9,13},{10,... | collective-permute-start | bytes 1572872 | tf_op jit(solution)/shard_map/ppermute | solution.py:41
  158.7 13.7 %shard_map.62 = (f32[32,512]{1,0:T(8,128)}, bf16[4,32,1024]{2,1,0:T(8,128)(2,1)}) custom-call(s32[1]{0:T(128)} %bitcast.core_ref, f32[256,512]{1,0:T(8,128)S(1)} %bitcast.29, f32[256,512]{1,0:T(8,128)S(1)} %collective-permute-done.24.other_ref, f32[32,512]{1,0:T(8,128)S(1)} %bitcast.30, bf16[32,512,128]{2,1,0:T(8,128)(2,1)} %get-tuple-element.20.far_ref), custom_call_target="tpu_custom_call" | custom-call | tf_op jit(solution)/shard_map/pallas_call | solution.py:306
  (49 shorter events, 24.0 us)
Async XLA Ops:
  7.2 2.3 %collective-permute-start = (f32[64,128]{1,0:T(8,128)S(1)}, f32[64,128]{1,0:T(8,128)S(1)}, u32[]{:S(2)}, u32[]{:S(2)}) collective-permute-start(f32[64,128]{1,0:T(8,128)S(1)} %get-tuple-element.14), channel_id=1, source_target_pairs={{0,4},{1,5},{2,6},{3,7},{4,0},{5,1},{6,2},{7,3},{8,12},{9,13},{10,... | collective-permute-start | bytes 98312 | tf_op jit(solution)/shard_map/ppermute | solution.py:41
  9.5 5.1 %collective-permute-start.1 = (f32[64,128]{1,0:T(8,128)S(1)}, f32[64,128]{1,0:T(8,128)S(1)}, u32[]{:S(2)}, u32[]{:S(2)}) collective-permute-start(f32[64,128]{1,0:T(8,128)S(1)} %add.84), channel_id=1, source_target_pairs={{0,1},{1,0},{2,3},{3,2},{4,36},{5,37},{6,38},{7,39},{8,9},{9,8},{1... | collective-permute-start | bytes 98312 | tf_op jit(solution)/shard_map/ppermute | solution.py:41
  11.3 5.2 %collective-permute-start.2 = (f32[64,128]{1,0:T(8,128)S(1)}, f32[64,128]{1,0:T(8,128)S(1)}, u32[]{:S(2)}, u32[]{:S(2)}) collective-permute-start(f32[64,128]{1,0:T(8,128)S(1)} %add.84), channel_id=1, source_target_pairs={{0,2},{1,3},{2,0},{3,1},{4,68},{5,69},{6,70},{7,71},{8,10},{9,11},... | collective-permute-start | bytes 98312 | tf_op jit(solution)/shard_map/ppermute | solution.py:41
  14.6 4.3 %collective-permute-start.3 = (f32[64,128]{1,0:T(8,128)S(1)}, f32[64,128]{1,0:T(8,128)S(1)}, u32[]{:S(2)}, u32[]{:S(2)}) collective-permute-start(f32[64,128]{1,0:T(8,128)S(1)} %add.84), channel_id=1, source_target_pairs={{0,3},{1,2},{2,1},{3,0},{4,100},{5,101},{6,102},{7,103},{8,11},{9,... | collective-permute-start | bytes 98312 | tf_op jit(solution)/shard_map/ppermute | solution.py:41
  18.9 3.9 %collective-permute-start.4 = (f32[64,128]{1,0:T(8,128)S(1)}, f32[64,128]{1,0:T(8,128)S(1)}, u32[]{:S(2)}, u32[]{:S(2)}) collective-permute-start(f32[64,128]{1,0:T(8,128)S(1)} %add_add_fusion.4), channel_id=1, source_target_pairs={{0,8},{1,9},{2,10},{3,11},{4,5},{5,4},{6,7},{7,6},{8,0},{9,1},{10,... | collective-permute-start | bytes 98312 | tf_op jit(solution)/shard_map/ppermute | solution.py:41
  19.9 4.3 %collective-permute-start.5 = (f32[64,128]{1,0:T(8,128)S(1)}, f32[64,128]{1,0:T(8,128)S(1)}, u32[]{:S(2)}, u32[]{:S(2)}) collective-permute-start(f32[64,128]{1,0:T(8,128)S(1)} %add_add_fusion.4), channel_id=1, source_target_pairs={{0,16},{1,17},{2,18},{3,19},{4,6},{5,7},{6,4},{7,5},{8,24},{9,25},... | collective-permute-start | bytes 98312 | tf_op jit(solution)/shard_map/ppermute | solution.py:41
  22.3 4.0 %collective-permute-start.6 = (f32[64,128]{1,0:T(8,128)S(1)}, f32[64,128]{1,0:T(8,128)S(1)}, u32[]{:S(2)}, u32[]{:S(2)}) collective-permute-start(f32[64,128]{1,0:T(8,128)S(1)} %add_add_fusion.4), channel_id=1, source_target_pairs={{0,24},{1,25},{2,26},{3,27},{4,7},{5,6},{6,5},{7,4},{8,16},{9,17},... | collective-permute-start | bytes 98312 | tf_op jit(solution)/shard_map/ppermute | solution.py:41
  26.3 4.0 %collective-permute-start.7 = (f32[64,128]{1,0:T(8,128)S(1)}, f32[64,128]{1,0:T(8,128)S(1)}, u32[]{:S(2)}, u32[]{:S(2)}) collective-permute-start(f32[64,128]{1,0:T(8,128)S(1)} %add_add_fusion.3), channel_id=1, source_target_pairs={{0,32},{1,33},{2,34},{3,35},{4,12},{5,13},{6,14},{7,15},{8,40},{9,... | collective-permute-start | bytes 98312 | tf_op jit(solution)/shard_map/ppermute | solution.py:41
  27.7 4.3 %collective-permute-start.8 = (f32[64,128]{1,0:T(8,128)S(1)}, f32[64,128]{1,0:T(8,128)S(1)}, u32[]{:S(2)}, u32[]{:S(2)}) collective-permute-start(f32[64,128]{1,0:T(8,128)S(1)} %add_add_fusion.3), channel_id=1, source_target_pairs={{0,64},{1,65},{2,66},{3,67},{4,20},{5,21},{6,22},{7,23},{8,72},{9,... | collective-permute-start | bytes 98312 | tf_op jit(solution)/shard_map/ppermute | solution.py:41
  30.3 4.0 %collective-permute-start.9 = (f32[64,128]{1,0:T(8,128)S(1)}, f32[64,128]{1,0:T(8,128)S(1)}, u32[]{:S(2)}, u32[]{:S(2)}) collective-permute-start(f32[64,128]{1,0:T(8,128)S(1)} %add_add_fusion.3), channel_id=1, source_target_pairs={{0,96},{1,97},{2,98},{3,99},{4,28},{5,29},{6,30},{7,31},{8,104},{9... | collective-permute-start | bytes 98312 | tf_op jit(solution)/shard_map/ppermute | solution.py:41
  34.3 6.6 %collective-permute-start.10 = (f32[64,128]{1,0:T(8,128)S(1)}, f32[64,128]{1,0:T(8,128)S(1)}, u32[]{:S(2)}, u32[]{:S(2)}) collective-permute-start(f32[64,128]{1,0:T(8,128)S(1)} %add_add_fusion.2.mine_ref), channel_id=1, source_target_pairs={{0,4},{1,5},{2,6},{3,7},{4,0},{5,1},{6,2},{7,3},{8,12},{9,13},{10,... | collective-permute-start | bytes 98312 | tf_op jit(solution)/shard_map/ppermute | solution.py:41
  122.1 4.2 %collective-permute-start.12 = (f32[64,512]{1,0:T(8,128)S(1)}, f32[64,512]{1,0:T(8,128)S(1)}, u32[]{:S(2)}, u32[]{:S(2)}) collective-permute-start(f32[64,512]{1,0:T(8,128)S(1)} %get-tuple-element.27), channel_id=1, source_target_pairs={{0,1},{1,0},{2,3},{3,2},{4,36},{5,37},{6,38},{7,39},{8,9},{9,8},{1... | collective-permute-start | bytes 393224 | tf_op jit(solution)/shard_map/ppermute | solution.py:41
  122.8 5.6 %collective-permute-start.13 = (f32[64,512]{1,0:T(8,128)S(1)}, f32[64,512]{1,0:T(8,128)S(1)}, u32[]{:S(2)}, u32[]{:S(2)}) collective-permute-start(f32[64,512]{1,0:T(8,128)S(1)} %get-tuple-element.26), channel_id=1, source_target_pairs={{0,2},{1,3},{2,0},{3,1},{4,68},{5,69},{6,70},{7,71},{8,10},{9,11},... | collective-permute-start | bytes 393224 | tf_op jit(solution)/shard_map/ppermute | solution.py:41
  124.0 5.5 %collective-permute-start.14 = (f32[64,512]{1,0:T(8,128)S(1)}, f32[64,512]{1,0:T(8,128)S(1)}, u32[]{:S(2)}, u32[]{:S(2)}) collective-permute-start(f32[64,512]{1,0:T(8,128)S(1)} %get-tuple-element.25), channel_id=1, source_target_pairs={{0,3},{1,2},{2,1},{3,0},{4,100},{5,101},{6,102},{7,103},{8,11},{9,... | collective-permute-start | bytes 393224 | tf_op jit(solution)/shard_map/ppermute | solution.py:41
  129.6 3.9 %collective-permute-start.15 = (f32[64,512]{1,0:T(8,128)S(1)}, f32[64,512]{1,0:T(8,128)S(1)}, u32[]{:S(2)}, u32[]{:S(2)}) collective-permute-start(f32[64,512]{1,0:T(8,128)S(1)} %fusion), channel_id=1, source_target_pairs={{0,8},{1,9},{2,10},{3,11},{4,5},{5,4},{6,7},{7,6},{8,0},{9,1},{10,... | collective-permute-start | bytes 393224 | tf_op jit(solution)/shard_map/ppermute | solution.py:41
  129.8 6.2 %collective-permute-start.16 = (f32[64,512]{1,0:T(8,128)S(1)}, f32[64,512]{1,0:T(8,128)S(1)}, u32[]{:S(2)}, u32[]{:S(2)}) collective-permute-start(f32[64,512]{1,0:T(8,128)S(1)} %fusion), channel_id=1, source_target_pairs={{0,16},{1,17},{2,18},{3,19},{4,6},{5,7},{6,4},{7,5},{8,24},{9,25},... | collective-permute-start | bytes 393224 | tf_op jit(solution)/shard_map/ppermute | solution.py:41
  132.3 5.5 %collective-permute-start.17 = (f32[64,512]{1,0:T(8,128)S(1)}, f32[64,512]{1,0:T(8,128)S(1)}, u32[]{:S(2)}, u32[]{:S(2)}) collective-permute-start(f32[64,512]{1,0:T(8,128)S(1)} %fusion), channel_id=1, source_target_pairs={{0,24},{1,25},{2,26},{3,27},{4,7},{5,6},{6,5},{7,4},{8,16},{9,17},... | collective-permute-start | bytes 393224 | tf_op jit(solution)/shard_map/ppermute | solution.py:41
  137.8 3.9 %collective-permute-start.18 = (f32[64,512]{1,0:T(8,128)S(1)}, f32[64,512]{1,0:T(8,128)S(1)}, u32[]{:S(2)}, u32[]{:S(2)}) collective-permute-start(f32[64,512]{1,0:T(8,128)S(1)} %add_add_fusion.1), channel_id=1, source_target_pairs={{0,32},{1,33},{2,34},{3,35},{4,12},{5,13},{6,14},{7,15},{8,40},{9,... | collective-permute-start | bytes 393224 | tf_op jit(solution)/shard_map/ppermute | solution.py:41
  137.9 5.5 %collective-permute-start.19 = (f32[64,512]{1,0:T(8,128)S(1)}, f32[64,512]{1,0:T(8,128)S(1)}, u32[]{:S(2)}, u32[]{:S(2)}) collective-permute-start(f32[64,512]{1,0:T(8,128)S(1)} %add_add_fusion.1), channel_id=1, source_target_pairs={{0,64},{1,65},{2,66},{3,67},{4,20},{5,21},{6,22},{7,23},{8,72},{9,... | collective-permute-start | bytes 393224 | tf_op jit(solution)/shard_map/ppermute | solution.py:41
  138.5 6.1 %collective-permute-start.20 = (f32[64,512]{1,0:T(8,128)S(1)}, f32[64,512]{1,0:T(8,128)S(1)}, u32[]{:S(2)}, u32[]{:S(2)}) collective-permute-start(f32[64,512]{1,0:T(8,128)S(1)} %add_add_fusion.1), channel_id=1, source_target_pairs={{0,96},{1,97},{2,98},{3,99},{4,28},{5,29},{6,30},{7,31},{8,104},{9... | collective-permute-start | bytes 393224 | tf_op jit(solution)/shard_map/ppermute | solution.py:41
  144.8 5.4 %collective-permute-start.21 = (f32[64,512]{1,0:T(8,128)S(1)}, f32[64,512]{1,0:T(8,128)S(1)}, u32[]{:S(2)}, u32[]{:S(2)}) collective-permute-start(f32[64,512]{1,0:T(8,128)S(1)} %get-tuple-element.24), channel_id=1, source_target_pairs={{0,2},{1,3},{2,0},{3,1},{4,68},{5,69},{6,70},{7,71},{8,10},{9,11},... | collective-permute-start | bytes 393224 | tf_op jit(solution)/shard_map/ppermute | solution.py:41
  146.3 5.3 %collective-permute-start.22 = (f32[64,512]{1,0:T(8,128)S(1)}, f32[64,512]{1,0:T(8,128)S(1)}, u32[]{:S(2)}, u32[]{:S(2)}) collective-permute-start(f32[64,512]{1,0:T(8,128)S(1)} %get-tuple-element.24), channel_id=1, source_target_pairs={{0,3},{1,2},{2,1},{3,0},{4,100},{5,101},{6,102},{7,103},{8,11},{9,... | collective-permute-start | bytes 393224 | tf_op jit(solution)/shard_map/ppermute | solution.py:41
  146.9 4.7 %collective-permute-start.23 = (f32[64,512]{1,0:T(8,128)S(1)}, f32[64,512]{1,0:T(8,128)S(1)}, u32[]{:S(2)}, u32[]{:S(2)}) collective-permute-start(f32[64,512]{1,0:T(8,128)S(1)} %get-tuple-element.24), channel_id=1, source_target_pairs={{0,1},{1,0},{2,3},{3,2},{4,36},{5,37},{6,38},{7,39},{8,9},{9,8},{1... | collective-permute-start | bytes 393224 | tf_op jit(solution)/shard_map/ppermute | solution.py:41
  151.6 7.1 %collective-permute-start.24 = (f32[256,512]{1,0:T(8,128)S(1)}, f32[256,512]{1,0:T(8,128)S(1)}, u32[]{:S(2)}, u32[]{:S(2)}) collective-permute-start(f32[256,512]{1,0:T(8,128)S(1)} %bitcast.28), channel_id=1, source_target_pairs={{0,4},{1,5},{2,6},{3,7},{4,0},{5,1},{6,2},{7,3},{8,12},{9,13},{10,... | collective-permute-start | bytes 1572872 | tf_op jit(solution)/shard_map/ppermute | solution.py:41
  (3 other events, 85.3 us)
